TPU v7x, 32 devices: a whole 2x2x4 slice. The times are simulated.
32 devices in a mesh: dp: 16 (over z, y, x), tensor: 2 (over core).
Axes of the slice: x: 2, y: 2, z: 4, core: 2. Of those that a mesh axis runs over, the one named last changes fastest.
Arguments:
- video_input: bfloat16 [16, 8, 197, 768], P('dp', 'tensor'), may hold values from -6 to 6
- text_input: bfloat16 [16384, 512], P(('dp', 'tensor')), may hold values from -6 to 6
- caption_lengths: int32 [16, 64], P('dp'), may hold values from 1 to 77, 1024 in all within a row
- video_first_gain: bfloat16 [768], replicated, may hold values from 0.5 to 1.5
- video_first_shift: bfloat16 [768], replicated, may hold values from -1.25 to 1.25
- video_message_weight: bfloat16 [768, 768], replicated, may hold values from -0.21875 to 0.21875
- video_message_bias: bfloat16 [768], replicated, may hold values from -1.25 to 1.25
- video_message_gain: bfloat16 [768], replicated, may hold values from 0.5 to 1.5
- video_message_shift: bfloat16 [768], replicated, may hold values from -1.25 to 1.25
- video_message_attend_weight: bfloat16 [768, 3, 768], replicated, may hold values from -0.21875 to 0.21875
- video_message_attend_bias: bfloat16 [2, 768], replicated, may hold values from -1.25 to 1.25
- video_message_out_weight: bfloat16 [768, 768], replicated, may hold values from -0.625 to 0.625
- video_message_out_bias: bfloat16 [768], replicated, may hold values from -1.25 to 1.25
- video_attend_weight: bfloat16 [768, 3, 768], P(None, None, 'tensor'), may hold values from -0.21875 to 0.21875
- video_attend_bias: bfloat16 [2, 768], P(None, 'tensor'), may hold values from -1.25 to 1.25
- video_output_weight: bfloat16 [768, 768], P('tensor'), may hold values from -0.875 to 0.875
- video_output_bias: bfloat16 [768], replicated, may hold values from -1.25 to 1.25
- video_final_gain: bfloat16 [768], replicated, may hold values from 0.5 to 1.5
- video_final_shift: bfloat16 [768], replicated, may hold values from -1.25 to 1.25
- video_expand_weight: bfloat16 [768, 3072], P(None, 'tensor'), may hold values from -0.21875 to 0.21875
- video_expand_bias: bfloat16 [3072], P('tensor'), may hold values from -1.25 to 1.25
- video_reduce_weight: bfloat16 [3072, 768], P('tensor'), may hold values from -0.109375 to 0.109375
- video_reduce_bias: bfloat16 [768], replicated, may hold values from -1.25 to 1.25
- text_first_gain: bfloat16 [512], replicated, may hold values from 0.5 to 1.5
- text_first_shift: bfloat16 [512], replicated, may hold values from -1.25 to 1.25
- text_attend_weight: bfloat16 [512, 3, 512], P(None, None, 'tensor'), may hold values from -0.25 to 0.25
- text_attend_bias: bfloat16 [2, 512], P(None, 'tensor'), may hold values from -1.25 to 1.25
- text_output_weight: bfloat16 [512, 512], P('tensor'), may hold values from -0.5 to 0.5
- text_output_bias: bfloat16 [512], replicated, may hold values from -1.25 to 1.25
- text_final_gain: bfloat16 [512], replicated, may hold values from 0.5 to 1.5
- text_final_shift: bfloat16 [512], replicated, may hold values from -1.25 to 1.25
- text_expand_weight: bfloat16 [512, 2048], P(None, 'tensor'), may hold values from -0.25 to 0.25
- text_expand_bias: bfloat16 [2048], P('tensor'), may hold values from -1.25 to 1.25
- text_reduce_weight: bfloat16 [2048, 512], P('tensor'), may hold values from -0.125 to 0.125
- text_reduce_bias: bfloat16 [512], replicated, may hold values from -1.25 to 1.25
- video_out_grad: bfloat16 [16, 8, 197, 768], P('dp', 'tensor'), may hold values from -6 to 6
- message_out_grad: bfloat16 [16, 8, 768], P('dp', 'tensor'), may hold values from -6 to 6
- text_out_grad: bfloat16 [16384, 512], P(('dp', 'tensor')), may hold values from -6 to 6
Outputs:
- video_output: bfloat16 [16, 8, 197, 768], P('dp', 'tensor')
- message_output: bfloat16 [16, 8, 768], P('dp', 'tensor')
- text_output: bfloat16 [16384, 512], P(('dp', 'tensor'))
- video_input_grad: bfloat16 [16, 8, 197, 768], P('dp', 'tensor')
- text_input_grad: bfloat16 [16384, 512], P(('dp', 'tensor'))
- grad_video_first_gain: float32 [768], replicated
- grad_video_first_shift: float32 [768], replicated
- grad_video_message_weight: float32 [768, 768], replicated
- grad_video_message_bias: float32 [768], replicated
- grad_video_message_gain: float32 [768], replicated
- grad_video_message_shift: float32 [768], replicated
- grad_video_message_attend_weight: float32 [768, 3, 768], replicated
- grad_video_message_attend_bias: float32 [2, 768], replicated
- grad_video_message_out_weight: float32 [768, 768], replicated
- grad_video_message_out_bias: float32 [768], replicated
- grad_video_attend_weight: float32 [768, 3, 768], P(None, None, 'tensor')
- grad_video_attend_bias: float32 [2, 768], P(None, 'tensor')
- grad_video_output_weight: float32 [768, 768], P('tensor')
- grad_video_output_bias: float32 [768], replicated
- grad_video_final_gain: float32 [768], replicated
- grad_video_final_shift: float32 [768], replicated
- grad_video_expand_weight: float32 [768, 3072], P(None, 'tensor')
- grad_video_expand_bias: float32 [3072], P('tensor')
- grad_video_reduce_weight: float32 [3072, 768], P('tensor')
- grad_video_reduce_bias: float32 [768], replicated
- grad_text_first_gain: float32 [512], replicated
- grad_text_first_shift: float32 [512], replicated
- grad_text_attend_weight: float32 [512, 3, 512], P(None, None, 'tensor')
- grad_text_attend_bias: float32 [2, 512], P(None, 'tensor')
- grad_text_output_weight: float32 [512, 512], P('tensor')
- grad_text_output_bias: float32 [512], replicated
- grad_text_final_gain: float32 [512], replicated
- grad_text_final_shift: float32 [512], replicated
- grad_text_expand_weight: float32 [512, 2048], P(None, 'tensor')
- grad_text_expand_bias: float32 [2048], P('tensor')
- grad_text_reduce_weight: float32 [2048, 512], P('tensor')
- grad_text_reduce_bias: float32 [512], replicated
Inputs may be any that keep to these rules, and one draw needn't show every extreme that they name: Each row of caption_lengths holds the lengths of the 64 captions packed in order into one pack; each row sums to 1024 and its longest caption has exactly 77 tokens.
All inputs are finite; a program needn't handle non-finite values.
Results may differ from a plain program's by a relative error of at most 0.02.
Values may be sent and summed in bfloat16 or wider, within the bound.
No kernel may reach another device: no remote copies, remote signals or barrier semaphores. Data moves between devices by JAX's collectives and lax.ppermute only.
A program may use at most 256 MiB of HBM per device.

v0:
```python
import jax
import jax.numpy as jnp
from jax import lax
from jax.sharding import PartitionSpec as P

HD = 64
MAXLEN = 77


def norm_forward(inputs, gain_row, shift_row):
    centre = inputs - jnp.mean(inputs, axis=-1, keepdims=True)
    inverse = lax.rsqrt(jnp.mean(centre * centre, axis=-1, keepdims=True) + 1e-05)
    unit_rows = centre * inverse
    return (unit_rows * gain_row + shift_row, unit_rows, inverse)


def norm_backward(grad_out, unit_rows, inverse, gain_row):
    scaled = grad_out * gain_row
    grad_in = inverse * (
        scaled
        - jnp.mean(scaled, axis=-1, keepdims=True)
        - unit_rows * jnp.mean(scaled * unit_rows, axis=-1, keepdims=True)
    )
    columns = grad_out.shape[-1]
    gain_grad = jnp.sum((grad_out * unit_rows).reshape(-1, columns), axis=0)
    shift_grad = jnp.sum(grad_out.reshape(-1, columns), axis=0)
    return (grad_in, gain_grad, shift_grad)


def gelu_parts(hidden):
    logistic = jax.nn.sigmoid(1.702 * hidden)
    return (hidden * logistic, logistic + 1.702 * hidden * logistic * (1.0 - logistic))


def full_bias(attend_bias):
    bias_rows = attend_bias.astype(jnp.float32)
    return jnp.stack([bias_rows[0], jnp.zeros_like(bias_rows[0]), bias_rows[1]])


def row_sums(values):
    return jnp.sum(values.reshape(-1, values.shape[-1]), axis=0)


def video_scores(queries, key_rows):
    return (
        jnp.einsum("vfrhe,vfkhe->vfhrk", queries, key_rows, preferred_element_type=jnp.float32)
        * 0.125
    )


def text_scores(query_block, key_block, segment_ids, block_start, key_start):
    block_rows = query_block.shape[0]
    window = key_block.shape[0]
    positions = block_start + jnp.arange(block_rows, dtype=jnp.int32)
    query_segments = lax.dynamic_slice_in_dim(segment_ids, block_start, block_rows)
    key_positions = key_start + jnp.arange(window, dtype=jnp.int32)
    key_segments = lax.dynamic_slice_in_dim(segment_ids, key_start, window)
    allowed = (query_segments[:, None] == key_segments[None, :]) & (
        key_positions[None, :] <= positions[:, None]
    )
    scores = (
        jnp.einsum("qhe,khe->hqk", query_block, key_block, preferred_element_type=jnp.float32)
        * 0.125
    )
    return jnp.where(allowed[None], scores, -1000000000.0)


def on_device(
    video_input,
    text_input,
    caption_lengths,
    video_first_gain,
    video_first_shift,
    video_message_weight,
    video_message_bias,
    video_message_gain,
    video_message_shift,
    video_message_attend_weight,
    video_message_attend_bias,
    video_message_out_weight,
    video_message_out_bias,
    video_attend_weight,
    video_attend_bias,
    video_output_weight,
    video_output_bias,
    video_final_gain,
    video_final_shift,
    video_expand_weight,
    video_expand_bias,
    video_reduce_weight,
    video_reduce_bias,
    text_first_gain,
    text_first_shift,
    text_attend_weight,
    text_attend_bias,
    text_output_weight,
    text_output_bias,
    text_final_gain,
    text_final_shift,
    text_expand_weight,
    text_expand_bias,
    text_reduce_weight,
    text_reduce_bias,
    video_out_grad,
    message_out_grad,
    text_out_grad,
):
    token_count = video_input.shape[2]
    frames_here = video_input.shape[1]
    class_rows = video_input[:, :, 0, :]
    message_here = jnp.einsum(
        "vfd,de->vfe", class_rows, video_message_weight, preferred_element_type=jnp.float32
    ) + video_message_bias.astype(jnp.float32)
    message_all = lax.all_gather(message_here, "tensor", axis=1, tiled=True)
    message_gain_row = video_message_gain.astype(jnp.float32)
    message_normed, message_unit, message_inverse = norm_forward(
        message_all, message_gain_row, video_message_shift.astype(jnp.float32)
    )
    message_normed_low = message_normed.astype(jnp.bfloat16)
    message_mixed = (
        jnp.einsum(
            "vfd,dcm->vfcm",
            message_normed_low,
            video_message_attend_weight,
            preferred_element_type=jnp.float32,
        )
        + full_bias(video_message_attend_bias)
    ).astype(jnp.bfloat16)
    message_heads = message_mixed.reshape(message_mixed.shape[:3] + (-1, HD))
    message_queries = message_heads[:, :, 0]
    message_keys = message_heads[:, :, 1]
    message_values = message_heads[:, :, 2]
    message_scores = (
        jnp.einsum(
            "vfhe,vghe->vhfg", message_queries, message_keys, preferred_element_type=jnp.float32
        )
        * 0.125
    )
    message_probs = jax.nn.softmax(message_scores, axis=-1)
    message_probs_low = message_probs.astype(jnp.bfloat16)
    message_attended = jnp.einsum(
        "vhfg,vghe->vfhe", message_probs_low, message_values, preferred_element_type=jnp.float32
    ).astype(jnp.bfloat16)
    message_attended = message_attended.reshape(message_attended.shape[:2] + (-1,))
    message_tokens = (
        message_all
        + jnp.einsum(
            "vfm,md->vfd",
            message_attended,
            video_message_out_weight,
            preferred_element_type=jnp.float32,
        )
        + video_message_out_bias.astype(jnp.float32)
    )
    frame_start = lax.axis_index("tensor") * frames_here
    tokens_here = lax.dynamic_slice_in_dim(message_tokens, frame_start, frames_here, 1)
    video_rows = jnp.concatenate([video_input.astype(jnp.float32), tokens_here[:, :, None]], axis=2)
    video_normed, video_unit_one, video_inverse_one = norm_forward(
        video_rows, video_first_gain.astype(jnp.float32), video_first_shift.astype(jnp.float32)
    )
    text_rows = text_input.astype(jnp.float32)
    text_normed, text_unit_one, text_inverse_one = norm_forward(
        text_rows, text_first_gain.astype(jnp.float32), text_first_shift.astype(jnp.float32)
    )
    video_first_full, text_first_full = (
        lax.all_gather(video_normed.astype(jnp.bfloat16), "tensor", axis=1, tiled=True),
        lax.all_gather(text_normed.astype(jnp.bfloat16), "tensor", axis=0, tiled=True),
    )
    video_mixed = (
        jnp.einsum(
            "vfrd,dcm->vfrcm",
            video_first_full,
            video_attend_weight,
            preferred_element_type=jnp.float32,
        )
        + full_bias(video_attend_bias)
    ).astype(jnp.bfloat16)
    video_heads = video_mixed.reshape(video_mixed.shape[:4] + (-1, HD))
    video_queries = video_heads[:, :, :, 0]
    video_key_rows = video_heads[:, :, :, 1]
    video_value_rows = video_heads[:, :, :, 2]
    scores_now = video_scores(video_queries, video_key_rows)
    row_max = jnp.max(scores_now, axis=-1, keepdims=True)
    video_logsum = row_max + jnp.log(jnp.sum(jnp.exp(scores_now - row_max), axis=-1, keepdims=True))
    video_probs = jnp.exp(scores_now - video_logsum).astype(jnp.bfloat16)
    video_attended = jnp.einsum(
        "vfhrk,vfkhe->vfrhe", video_probs, video_value_rows, preferred_element_type=jnp.float32
    ).astype(jnp.bfloat16)
    video_attended = video_attended.reshape(video_attended.shape[:3] + (-1,))
    text_length = text_first_full.shape[0]
    block_rows = min(512, text_length)
    block_count = text_length // block_rows
    key_extra = -(-(MAXLEN - 1) // 128) * 128
    window = min(block_rows + key_extra, text_length)
    starts = jnp.arange(block_count, dtype=jnp.int32) * block_rows
    caption_ends = jnp.cumsum(caption_lengths[0])
    positions = jnp.arange(text_length, dtype=jnp.int32)
    text_segments = jnp.sum((positions[:, None] >= caption_ends[None, :]).astype(jnp.int32), axis=1)
    text_mixed = (
        jnp.einsum(
            "sd,dcm->scm", text_first_full, text_attend_weight, preferred_element_type=jnp.float32
        )
        + full_bias(text_attend_bias)
    ).astype(jnp.bfloat16)
    text_heads = text_mixed.reshape(text_length, 3, -1, HD)
    text_key_rows = text_heads[:, 1]
    text_value_rows = text_heads[:, 2]
    query_blocks = text_heads[:, 0].reshape((block_count, block_rows) + text_heads.shape[2:])

    def window_start(block_start):
        return jnp.clip(block_start - key_extra, 0, text_length - window)

    def text_forward_block(operands):
        query_block, block_start = operands
        key_start = window_start(block_start)
        key_block = lax.dynamic_slice_in_dim(text_key_rows, key_start, window)
        value_block = lax.dynamic_slice_in_dim(text_value_rows, key_start, window)
        scores = text_scores(query_block, key_block, text_segments, block_start, key_start)
        block_max = jnp.max(scores, axis=-1, keepdims=True)
        logsum = block_max + jnp.log(jnp.sum(jnp.exp(scores - block_max), axis=-1, keepdims=True))
        probs = jnp.exp(scores - logsum).astype(jnp.bfloat16)
        output = jnp.einsum(
            "hqk,khe->qhe", probs, value_block, preferred_element_type=jnp.float32
        ).astype(jnp.bfloat16)
        return (output, logsum)

    text_outputs, text_logsums = lax.map(text_forward_block, (query_blocks, starts))
    text_attended = text_outputs.reshape(text_length, -1)
    video_partial = jnp.einsum(
        "vfrm,md->vfrd", video_attended, video_output_weight, preferred_element_type=jnp.float32
    )
    text_partial = jnp.dot(text_attended, text_output_weight, preferred_element_type=jnp.float32)
    video_attend_sum, text_attend_sum = (
        lax.psum_scatter(
            video_partial.astype(jnp.bfloat16), "tensor", scatter_dimension=1, tiled=True
        ).astype(jnp.float32),
        lax.psum_scatter(
            text_partial.astype(jnp.bfloat16), "tensor", scatter_dimension=0, tiled=True
        ).astype(jnp.float32),
    )
    video_resid = video_rows + video_attend_sum + video_output_bias.astype(jnp.float32)
    text_resid = text_rows + text_attend_sum + text_output_bias.astype(jnp.float32)
    video_trunk = video_resid[:, :, :token_count]
    message_output = video_resid[:, :, token_count].astype(jnp.bfloat16)
    video_second, video_unit_two, video_inverse_two = norm_forward(
        video_trunk, video_final_gain.astype(jnp.float32), video_final_shift.astype(jnp.float32)
    )
    text_second, text_unit_two, text_inverse_two = norm_forward(
        text_resid, text_final_gain.astype(jnp.float32), text_final_shift.astype(jnp.float32)
    )
    video_second_full, text_second_full = (
        lax.all_gather(video_second.astype(jnp.bfloat16), "tensor", axis=1, tiled=True),
        lax.all_gather(text_second.astype(jnp.bfloat16), "tensor", axis=0, tiled=True),
    )
    video_hidden = jnp.einsum(
        "vfrd,dn->vfrn", video_second_full, video_expand_weight, preferred_element_type=jnp.float32
    ) + video_expand_bias.astype(jnp.float32)
    video_active_full, video_slope = gelu_parts(video_hidden)
    video_active = video_active_full.astype(jnp.bfloat16)
    text_hidden = jnp.dot(
        text_second_full, text_expand_weight, preferred_element_type=jnp.float32
    ) + text_expand_bias.astype(jnp.float32)
    text_active_full, text_slope = gelu_parts(text_hidden)
    text_active = text_active_full.astype(jnp.bfloat16)
    video_mlp_partial = jnp.einsum(
        "vfrn,nd->vfrd", video_active, video_reduce_weight, preferred_element_type=jnp.float32
    )
    text_mlp_partial = jnp.dot(text_active, text_reduce_weight, preferred_element_type=jnp.float32)
    video_mlp_sum, text_mlp_sum = (
        lax.psum_scatter(
            video_mlp_partial.astype(jnp.bfloat16), "tensor", scatter_dimension=1, tiled=True
        ).astype(jnp.float32),
        lax.psum_scatter(
            text_mlp_partial.astype(jnp.bfloat16), "tensor", scatter_dimension=0, tiled=True
        ).astype(jnp.float32),
    )
    video_final = video_trunk + video_mlp_sum + video_reduce_bias.astype(jnp.float32)
    text_final = text_resid + text_mlp_sum + text_reduce_bias.astype(jnp.float32)
    video_output = video_final.astype(jnp.bfloat16)
    text_output = text_final.astype(jnp.bfloat16)
    video_cot_full, text_cot_full = (
        lax.all_gather(video_out_grad, "tensor", axis=1, tiled=True),
        lax.all_gather(text_out_grad, "tensor", axis=0, tiled=True),
    )
    grad_video_reduce_bias = row_sums(video_out_grad.astype(jnp.float32))
    grad_text_reduce_bias = row_sums(text_out_grad.astype(jnp.float32))
    grad_video_reduce_weight = jnp.einsum(
        "vfrn,vfrd->nd", video_active, video_cot_full, preferred_element_type=jnp.float32
    )
    grad_text_reduce_weight = jnp.einsum(
        "sn,sd->nd", text_active, text_cot_full, preferred_element_type=jnp.float32
    )
    video_grad_hidden = (
        jnp.einsum(
            "vfrd,nd->vfrn", video_cot_full, video_reduce_weight, preferred_element_type=jnp.float32
        )
        * video_slope
    ).astype(jnp.bfloat16)
    text_grad_hidden = (
        jnp.einsum(
            "sd,nd->sn", text_cot_full, text_reduce_weight, preferred_element_type=jnp.float32
        )
        * text_slope
    ).astype(jnp.bfloat16)
    grad_video_expand_bias = row_sums(video_grad_hidden.astype(jnp.float32))
    grad_text_expand_bias = row_sums(text_grad_hidden.astype(jnp.float32))
    grad_video_expand_weight = jnp.einsum(
        "vfrd,vfrn->dn", video_second_full, video_grad_hidden, preferred_element_type=jnp.float32
    )
    grad_text_expand_weight = jnp.einsum(
        "sd,sn->dn", text_second_full, text_grad_hidden, preferred_element_type=jnp.float32
    )
    video_grad_second = jnp.einsum(
        "vfrn,dn->vfrd", video_grad_hidden, video_expand_weight, preferred_element_type=jnp.float32
    )
    text_grad_second = jnp.einsum(
        "sn,dn->sd", text_grad_hidden, text_expand_weight, preferred_element_type=jnp.float32
    )
    video_back_second, text_back_second = (
        lax.psum_scatter(
            video_grad_second.astype(jnp.bfloat16), "tensor", scatter_dimension=1, tiled=True
        ).astype(jnp.float32),
        lax.psum_scatter(
            text_grad_second.astype(jnp.bfloat16), "tensor", scatter_dimension=0, tiled=True
        ).astype(jnp.float32),
    )
    video_norm_grad, grad_video_final_gain, grad_video_final_shift = norm_backward(
        video_back_second, video_unit_two, video_inverse_two, video_final_gain.astype(jnp.float32)
    )
    text_norm_grad, grad_text_final_gain, grad_text_final_shift = norm_backward(
        text_back_second, text_unit_two, text_inverse_two, text_final_gain.astype(jnp.float32)
    )
    video_grad_trunk = video_out_grad.astype(jnp.float32) + video_norm_grad
    video_grad_resid = jnp.concatenate(
        [video_grad_trunk, message_out_grad.astype(jnp.float32)[:, :, None]], axis=2
    )
    text_grad_resid = text_out_grad.astype(jnp.float32) + text_norm_grad
    grad_video_output_bias = row_sums(video_grad_resid)
    grad_text_output_bias = row_sums(text_grad_resid)
    video_resid_full, text_resid_full = (
        lax.all_gather(video_grad_resid.astype(jnp.bfloat16), "tensor", axis=1, tiled=True),
        lax.all_gather(text_grad_resid.astype(jnp.bfloat16), "tensor", axis=0, tiled=True),
    )
    grad_video_output_weight = jnp.einsum(
        "vfrm,vfrd->md", video_attended, video_resid_full, preferred_element_type=jnp.float32
    )
    grad_text_output_weight = jnp.einsum(
        "sm,sd->md", text_attended, text_resid_full, preferred_element_type=jnp.float32
    )
    video_grad_attended = jnp.einsum(
        "vfrd,md->vfrm", video_resid_full, video_output_weight, preferred_element_type=jnp.float32
    ).astype(jnp.bfloat16)
    video_grad_attended = video_grad_attended.reshape(video_grad_attended.shape[:3] + (-1, HD))
    text_grad_attended = jnp.einsum(
        "sd,md->sm", text_resid_full, text_output_weight, preferred_element_type=jnp.float32
    ).astype(jnp.bfloat16)
    video_weights = jnp.exp(video_scores(video_queries, video_key_rows) - video_logsum)
    video_weights_low = video_weights.astype(jnp.bfloat16)
    video_grad_values = jnp.einsum(
        "vfhrk,vfrhe->vfkhe",
        video_weights_low,
        video_grad_attended,
        preferred_element_type=jnp.float32,
    )
    video_grad_probs = jnp.einsum(
        "vfrhe,vfkhe->vfhrk",
        video_grad_attended,
        video_value_rows,
        preferred_element_type=jnp.float32,
    )
    video_row_dot = jnp.sum(video_weights * video_grad_probs, axis=-1, keepdims=True)
    video_grad_scores = (video_weights * (video_grad_probs - video_row_dot)).astype(jnp.bfloat16)
    video_grad_queries = (
        jnp.einsum(
            "vfhrk,vfkhe->vfrhe",
            video_grad_scores,
            video_key_rows,
            preferred_element_type=jnp.float32,
        )
        * 0.125
    )
    video_grad_keys = (
        jnp.einsum(
            "vfhrk,vfrhe->vfkhe",
            video_grad_scores,
            video_queries,
            preferred_element_type=jnp.float32,
        )
        * 0.125
    )
    video_grad_mixed = jnp.stack([video_grad_queries, video_grad_keys, video_grad_values], axis=3)
    video_grad_mixed = video_grad_mixed.reshape(video_grad_mixed.shape[:4] + (-1,)).astype(
        jnp.bfloat16
    )
    grad_blocks = text_grad_attended.reshape((block_count, block_rows, -1, HD))

    def text_backward_block(carried, operands):
        grad_key_rows, grad_value_rows = carried
        query_block, grad_block, logsum, block_start = operands
        key_start = window_start(block_start)
        key_block = lax.dynamic_slice_in_dim(text_key_rows, key_start, window)
        value_block = lax.dynamic_slice_in_dim(text_value_rows, key_start, window)
        weights = jnp.exp(
            text_scores(query_block, key_block, text_segments, block_start, key_start) - logsum
        )
        value_term = jnp.einsum(
            "hqk,qhe->khe",
            weights.astype(jnp.bfloat16),
            grad_block,
            preferred_element_type=jnp.float32,
        )
        grad_value_rows = lax.dynamic_update_slice_in_dim(
            grad_value_rows,
            lax.dynamic_slice_in_dim(grad_value_rows, key_start, window) + value_term,
            key_start,
            0,
        )
        grad_probs = jnp.einsum(
            "qhe,khe->hqk", grad_block, value_block, preferred_element_type=jnp.float32
        )
        row_dot = jnp.sum(weights * grad_probs, axis=-1, keepdims=True)
        grad_scores = (weights * (grad_probs - row_dot)).astype(jnp.bfloat16)
        grad_query = (
            jnp.einsum("hqk,khe->qhe", grad_scores, key_block, preferred_element_type=jnp.float32)
            * 0.125
        )
        key_term = (
            jnp.einsum("hqk,qhe->khe", grad_scores, query_block, preferred_element_type=jnp.float32)
            * 0.125
        )
        grad_key_rows = lax.dynamic_update_slice_in_dim(
            grad_key_rows,
            lax.dynamic_slice_in_dim(grad_key_rows, key_start, window) + key_term,
            key_start,
            0,
        )
        return ((grad_key_rows, grad_value_rows), grad_query)

    zero_rows = jnp.zeros(text_key_rows.shape, jnp.float32)
    (text_grad_keys, text_grad_values), text_grad_query_blocks = lax.scan(
        text_backward_block,
        (zero_rows, zero_rows),
        (query_blocks, grad_blocks, text_logsums, starts),
    )
    text_grad_queries = text_grad_query_blocks.reshape(text_grad_keys.shape)
    text_grad_mixed = jnp.stack([text_grad_queries, text_grad_keys, text_grad_values], axis=1)
    text_grad_mixed = text_grad_mixed.reshape(text_length, 3, -1).astype(jnp.bfloat16)
    video_mixed_sums = jnp.sum(
        video_grad_mixed.astype(jnp.float32).reshape((-1,) + video_grad_mixed.shape[3:]), axis=0
    )
    grad_video_attend_bias = jnp.stack([video_mixed_sums[0], video_mixed_sums[2]])
    text_mixed_sums = jnp.sum(text_grad_mixed.astype(jnp.float32), axis=0)
    grad_text_attend_bias = jnp.stack([text_mixed_sums[0], text_mixed_sums[2]])
    grad_video_attend_weight = jnp.einsum(
        "vfrd,vfrcm->dcm", video_first_full, video_grad_mixed, preferred_element_type=jnp.float32
    )
    grad_text_attend_weight = jnp.einsum(
        "sd,scm->dcm", text_first_full, text_grad_mixed, preferred_element_type=jnp.float32
    )
    video_grad_first = jnp.einsum(
        "vfrcm,dcm->vfrd", video_grad_mixed, video_attend_weight, preferred_element_type=jnp.float32
    )
    text_grad_first = jnp.einsum(
        "scm,dcm->sd", text_grad_mixed, text_attend_weight, preferred_element_type=jnp.float32
    )
    video_back_first, text_back_first = (
        lax.psum_scatter(
            video_grad_first.astype(jnp.bfloat16), "tensor", scatter_dimension=1, tiled=True
        ).astype(jnp.float32),
        lax.psum_scatter(
            text_grad_first.astype(jnp.bfloat16), "tensor", scatter_dimension=0, tiled=True
        ).astype(jnp.float32),
    )
    video_norm_first, grad_video_first_gain, grad_video_first_shift = norm_backward(
        video_back_first, video_unit_one, video_inverse_one, video_first_gain.astype(jnp.float32)
    )
    text_norm_first, grad_text_first_gain, grad_text_first_shift = norm_backward(
        text_back_first, text_unit_one, text_inverse_one, text_first_gain.astype(jnp.float32)
    )
    video_grad_rows = video_grad_resid + video_norm_first
    text_grad_rows = text_grad_resid + text_norm_first
    token_grad_here = video_grad_rows[:, :, token_count]
    token_grad_all = lax.dynamic_update_slice_in_dim(
        jnp.zeros(message_tokens.shape, jnp.float32), token_grad_here, frame_start, 1
    )
    grad_video_message_out_bias = row_sums(token_grad_all)
    token_low = token_grad_all.astype(jnp.bfloat16)
    grad_video_message_out_weight = jnp.einsum(
        "vfm,vfd->md", message_attended, token_low, preferred_element_type=jnp.float32
    )
    message_grad_attended = jnp.einsum(
        "vfd,md->vfm", token_low, video_message_out_weight, preferred_element_type=jnp.float32
    ).astype(jnp.bfloat16)
    message_grad_attended = message_grad_attended.reshape(
        message_grad_attended.shape[:2] + (-1, HD)
    )
    message_grad_values = jnp.einsum(
        "vhfg,vfhe->vghe",
        message_probs_low,
        message_grad_attended,
        preferred_element_type=jnp.float32,
    )
    message_grad_probs = jnp.einsum(
        "vfhe,vghe->vhfg", message_grad_attended, message_values, preferred_element_type=jnp.float32
    )
    message_row_dot = jnp.sum(message_probs * message_grad_probs, axis=-1, keepdims=True)
    message_grad_scores = (message_probs * (message_grad_probs - message_row_dot)).astype(
        jnp.bfloat16
    )
    message_grad_queries = (
        jnp.einsum(
            "vhfg,vghe->vfhe", message_grad_scores, message_keys, preferred_element_type=jnp.float32
        )
        * 0.125
    )
    message_grad_keys = (
        jnp.einsum(
            "vhfg,vfhe->vghe",
            message_grad_scores,
            message_queries,
            preferred_element_type=jnp.float32,
        )
        * 0.125
    )
    message_grad_mixed = jnp.stack(
        [message_grad_queries, message_grad_keys, message_grad_values], axis=2
    )
    message_grad_mixed = message_grad_mixed.reshape(message_grad_mixed.shape[:3] + (-1,)).astype(
        jnp.bfloat16
    )
    message_mixed_sums = jnp.sum(
        message_grad_mixed.astype(jnp.float32).reshape((-1,) + message_grad_mixed.shape[2:]), axis=0
    )
    grad_video_message_attend_bias = jnp.stack([message_mixed_sums[0], message_mixed_sums[2]])
    grad_video_message_attend_weight = jnp.einsum(
        "vfd,vfcm->dcm", message_normed_low, message_grad_mixed, preferred_element_type=jnp.float32
    )
    message_grad_normed = jnp.einsum(
        "vfcm,dcm->vfd",
        message_grad_mixed,
        video_message_attend_weight,
        preferred_element_type=jnp.float32,
    )
    message_norm_grad, grad_video_message_gain, grad_video_message_shift = norm_backward(
        message_grad_normed, message_unit, message_inverse, message_gain_row
    )
    grad_message_here = lax.psum_scatter(
        token_grad_all + message_norm_grad, "tensor", scatter_dimension=1, tiled=True
    )
    grad_video_message_bias = row_sums(grad_message_here)
    message_low = grad_message_here.astype(jnp.bfloat16)
    grad_video_message_weight = jnp.einsum(
        "vfd,vfe->de", class_rows, message_low, preferred_element_type=jnp.float32
    )
    class_grad = jnp.einsum(
        "vfe,de->vfd", message_low, video_message_weight, preferred_element_type=jnp.float32
    )
    video_input_grad = (
        video_grad_rows[:, :, :token_count].at[:, :, 0].add(class_grad).astype(jnp.bfloat16)
    )
    text_input_grad = text_grad_rows.astype(jnp.bfloat16)
    (
        grad_video_attend_weight,
        grad_video_attend_bias,
        grad_video_output_weight,
        grad_video_expand_weight,
        grad_video_expand_bias,
        grad_video_reduce_weight,
        grad_text_attend_weight,
        grad_text_attend_bias,
        grad_text_output_weight,
        grad_text_expand_weight,
        grad_text_expand_bias,
        grad_text_reduce_weight,
    ) = lax.psum(
        (
            grad_video_attend_weight,
            grad_video_attend_bias,
            grad_video_output_weight,
            grad_video_expand_weight,
            grad_video_expand_bias,
            grad_video_reduce_weight,
            grad_text_attend_weight,
            grad_text_attend_bias,
            grad_text_output_weight,
            grad_text_expand_weight,
            grad_text_expand_bias,
            grad_text_reduce_weight,
        ),
        "dp",
    )
    (
        grad_video_first_gain,
        grad_video_first_shift,
        grad_video_message_weight,
        grad_video_message_bias,
        grad_video_message_gain,
        grad_video_message_shift,
        grad_video_message_attend_weight,
        grad_video_message_attend_bias,
        grad_video_message_out_weight,
        grad_video_message_out_bias,
        grad_video_output_bias,
        grad_video_final_gain,
        grad_video_final_shift,
        grad_video_reduce_bias,
        grad_text_first_gain,
        grad_text_first_shift,
        grad_text_output_bias,
        grad_text_final_gain,
        grad_text_final_shift,
        grad_text_reduce_bias,
    ) = lax.psum(
        (
            grad_video_first_gain,
            grad_video_first_shift,
            grad_video_message_weight,
            grad_video_message_bias,
            grad_video_message_gain,
            grad_video_message_shift,
            grad_video_message_attend_weight,
            grad_video_message_attend_bias,
            grad_video_message_out_weight,
            grad_video_message_out_bias,
            grad_video_output_bias,
            grad_video_final_gain,
            grad_video_final_shift,
            grad_video_reduce_bias,
            grad_text_first_gain,
            grad_text_first_shift,
            grad_text_output_bias,
            grad_text_final_gain,
            grad_text_final_shift,
            grad_text_reduce_bias,
        ),
        ("dp", "tensor"),
    )
    return (
        video_output,
        message_output,
        text_output,
        video_input_grad,
        text_input_grad,
        grad_video_first_gain,
        grad_video_first_shift,
        grad_video_message_weight,
        grad_video_message_bias,
        grad_video_message_gain,
        grad_video_message_shift,
        grad_video_message_attend_weight,
        grad_video_message_attend_bias,
        grad_video_message_out_weight,
        grad_video_message_out_bias,
        grad_video_attend_weight,
        grad_video_attend_bias,
        grad_video_output_weight,
        grad_video_output_bias,
        grad_video_final_gain,
        grad_video_final_shift,
        grad_video_expand_weight,
        grad_video_expand_bias,
        grad_video_reduce_weight,
        grad_video_reduce_bias,
        grad_text_first_gain,
        grad_text_first_shift,
        grad_text_attend_weight,
        grad_text_attend_bias,
        grad_text_output_weight,
        grad_text_output_bias,
        grad_text_final_gain,
        grad_text_final_shift,
        grad_text_expand_weight,
        grad_text_expand_bias,
        grad_text_reduce_weight,
        grad_text_reduce_bias,
    )


def solution(mesh):
    in_specs = (
        P("dp", "tensor", None, None),
        P(("dp", "tensor"), None),
        P("dp", None),
        P(),
        P(),
        P(),
        P(),
        P(),
        P(),
        P(),
        P(),
        P(),
        P(),
        P(None, None, "tensor"),
        P(None, "tensor"),
        P("tensor", None),
        P(),
        P(),
        P(),
        P(None, "tensor"),
        P("tensor"),
        P("tensor", None),
        P(),
        P(),
        P(),
        P(None, None, "tensor"),
        P(None, "tensor"),
        P("tensor", None),
        P(),
        P(),
        P(),
        P(None, "tensor"),
        P("tensor"),
        P("tensor", None),
        P(),
        P("dp", "tensor", None, None),
        P("dp", "tensor", None),
        P(("dp", "tensor"), None),
    )
    out_specs = (
        P("dp", "tensor", None, None),
        P("dp", "tensor", None),
        P(("dp", "tensor"), None),
        P("dp", "tensor", None, None),
        P(("dp", "tensor"), None),
        P(),
        P(),
        P(),
        P(),
        P(),
        P(),
        P(),
        P(),
        P(),
        P(),
        P(None, None, "tensor"),
        P(None, "tensor"),
        P("tensor", None),
        P(),
        P(),
        P(),
        P(None, "tensor"),
        P("tensor"),
        P("tensor", None),
        P(),
        P(),
        P(),
        P(None, None, "tensor"),
        P(None, "tensor"),
        P("tensor", None),
        P(),
        P(),
        P(),
        P(None, "tensor"),
        P("tensor"),
        P("tensor", None),
        P(),
    )
    return jax.shard_map(
        on_device, mesh=mesh, in_specs=in_specs, out_specs=out_specs, check_vma=False
    )
```

profile of v0, /device:TPU:0, one launch (start us, length us, event | category | flops | bytes accessed | tf_op | source)
XLA Modules:
  0.0 1278.4 jit_solution(14980192443766706816)
XLA Ops:
  68.6 23.3 %while.31 = (s32[]{:T(128)}, bf16[2,512,4,64]{1,3,2,0:T(8,128)(2,1)}, f32[2,4,512,1]{2,1,3,0:T(4,128)}, s32[2]{0:T(128)}, bf16[1024,4,64]{0,2,1:T(8,128)(2,1)}, ...) while((s32[]{:T(128)}, ...), condition=%wide.region_19.20_spmd, body=%wide.region_16.19_spmd.sunk | while | flops 351075456 | bytes 24730504 | solution.py:227
  97.1 7.4 add_convert_fusion
  104.6 6.5 copy.228
  141.7 9.0 all-reduce.16.cloned.1.call-done
  162.9 5.8 multiply_convert_fusion.5
  168.7 5.8 all-gather.23.cloned.1.call-done
  174.5 5.9 convert_reduce_fusion.2
  189.0 13.7 %multiply_convert_fusion.3 = (bf16[8,197,1536]{2,1,0:T(8,128)(2,1)}, f32[8,197,1536]{2,1,0:T(8,128)}) fusion(f32[1536]{0:T(1024)S(1)} %convert_element_type.377, bf16[768,1536]{1,0:T(8,128)(2,1)} %param.63, bf16[1,8,197,768]{3,2,0,1:T(8,128)(2,1)} %all-gather.13.cloned.1.call-done), kind=kOutput, calls=%fused_computation.66 | convolution fusion | flops 3735195648 | bytes 19310592 | tf_op jit(solution)/shard_map/vfrd,dn->vfrn/dot_general | solution.py:255
  203.4 11.3 convert_reduce_fusion
  234.0 20.1 %all-reduce.18.cloned.1.call-done = bf16[1,8,197,768]{3,1,2,0:T(8,128)(2,1)} async-done(((bf16[1,8,197,768]{3,1,2,0:T(8,128)(2,1)}), bf16[1,8,197,768]{3,1,2,0:T(8,128)(2,1)}) %all-reduce.18.cloned.1.call-update) | async-done | bytes 2420752
  254.1 8.2 fusion.78
  262.4 5.0 fusion.184
  270.8 7.2 convert_bitcast_fusion.1
  294.5 7.4 convolution_convert_fusion
  301.9 9.2 multiply_reduce_fusion.1
  311.1 11.5 multiply_convert_fusion.1
  322.6 5.8 multiply_convert_fusion.6
  340.0 6.1 fusion.57
  350.3 57.8 %while.32 = (s32[]{:T(128)}, f32[1024,4,64]{0,2,1:T(8,128)}, f32[1024,4,64]{0,2,1:T(8,128)}, bf16[2,512,4,64]{1,3,2,0:T(8,128)(2,1)}, s32[2]{0:T(128)S(1)}, /*in...) while((s32[]{:T(128)}, f32[1024,4,64]{0,2,1:T(8,128)}, ...), condition=%wide.region_40.41_spmd, body=%wide.region_38.40_spmd.sunk | while | flops 860126336 | bytes 111950944 | solution.py:440
  366.6 5.1 multiply_reduce_fusion.9
  395.3 4.9 multiply_reduce_fusion.9
  425.2 6.7 fusion.74
  432.0 5.2 fusion.72
  459.9 4.7 all-reduce.4
  481.6 9.2 convolution_bitcast_fusion.1
  490.8 6.2 convolution_bitcast_fusion
  503.3 7.3 fusion.89
  547.7 77.5 %all-reduce.7 = (f32[2,384]{1,0:T(2,128)}, f32[1536]{0:T(1024)}, f32[2,256]{1,0:T(2,128)}, f32[1024]{0:T(1024)}) all-reduce(f32[2,384]{1,0:T(2,128)S(1)} %pad_maximum_fusion.10, f32[1536]{0:T(1024)} %get-tuple-element.647, f32[2,256]{1,0:T(2,128)S(1)} %copy-done.107, ...), channel_id=1, replica_groups=mesh['dp'=16,'tensor'=2] {'dp'}, use_global_device_ids=true, to_apply=%region_63.64 | all-reduce | flops 3840 | bytes 30720 | tf_op jit(solution)/shard_map/psum | solution.py:575
  631.8 40.7 %all-reduce.5 = (f32[768]{0:T(1024)}, f32[768]{0:T(1024)}, f32[768]{0:T(1024)}, f32[768]{0:T(1024)}, f32[768]{0:T(1024)}, /*index=5*/f32[2,768]{1,0:T(2,128)}, f...) all-reduce(f32[768]{0:T(1024)} %get-tuple-element.511, ...), channel_id=1, replica_groups=mesh['dp'=16,'tensor'=2] {'dp','tensor'}, use_global_device_ids=true, to_apply=%region_45.46 | all-reduce | flops 12288 | bytes 98304 | tf_op jit(solution)/shard_map/psum | solution.py:613
  679.5 21.8 %all-reduce.20.cloned.1.call-done = (f32[768,768]{0,1:T(8,128)}, f32[768,3,768]{2,0,1:T(8,128)}, f32[768,768]{1,0:T(8,128)}) async-done(((f32[768,768]{0,1:T(8,128)}, f32[768,3,768]{2,0,1:T(8,128)}, f32[768,768]{1,0:T(8,128)}), (f32[768,768]{0,1:T(8,128)}, f32[768,3,768]{2,0,1:T(8,128)}, f32[768,768]{1,0:T(8,128)})) %all-reduce.20.cloned.1.call-update) | async-done | bytes 11796496 | tf_op jit(solution)/shard_map/psum | solution.py:613
  704.3 544.0 %all-reduce.22.cloned.1.call-done = (f32[768,3,384]{2,0,1:T(8,128)}, f32[384,768]{1,0:T(8,128)}, f32[768,1536]{1,0:T(8,128)}, f32[1536,768]{1,0:T(8,128)}, f32[5...) async-done(((f32[768,3,384]{2,0,1:T(8,128)}, f32[384,768]{1,0:T(8,128)}, f32[768,1536]{1,0:T(8,128)}, f32[1536,768]{1,0:T(8,128)}, ...) | async-done | bytes 20447248 | tf_op jit(solution)/shard_map/psum | solution.py:575
  1248.2 6.6 copy.385
  (587 shorter events, 365.6 us)
Async XLA Ops:
  7.2 24.2 %copy-start = (bf16[768,3,768]{2,0,1:T(8,128)(2,1)S(1)}, bf16[768,3,768]{2,0,1:T(8,128)(2,1)}, u32[]{:S(2)}) copy-start(bf16[768,3,768]{2,0,1:T(8,128)(2,1)} %param.53) | copy-start | bytes 10616836
  7.3 11.6 copy-start.102
  7.3 53.4 %all-gather.15.cloned.1.call-start = ((), (), s32[]{:S(2)}) async-start(), calls=%async_computation.6 | async-start | bytes 1572864 | tf_op jit(solution)/shard_map/all_gather | solution.py:167
  14.2 82.9 %all-gather.11.cloned.1.call-start = ((), (), s32[]{:S(2)}) async-start(), calls=%async_computation.4 | async-start | bytes 3686400 | tf_op jit(solution)/shard_map/all_gather | solution.py:166
  14.3 17.1 %copy-start.69 = (f32[768]{0:T(1024)}, f32[768]{0:T(1024)S(1)}, u32[]{:S(2)}) copy-start(f32[768]{0:T(1024)S(1)} %convert_element_type.351) | copy-start | bytes 9220
  15.6 15.8 %copy-start.87 = (f32[768]{0:T(1024)}, f32[768]{0:T(1024)S(1)}, u32[]{:S(2)}) copy-start(f32[768]{0:T(1024)S(1)} %convert_element_type.352) | copy-start | bytes 9220
  29.1 9.8 copy-start.99
  43.5 107.1 %copy-start.59 = (f32[1,4,1,768]{3,1,2,0:T(4,128)}, f32[1,4,1,768]{3,1,2,0:T(4,128)S(1)}, u32[]{:S(2)}) copy-start(f32[1,4,1,768]{3,1,2,0:T(4,128)S(1)} %fusion.156) | copy-start | bytes 36868
  50.0 79.6 %reduce-scatter.10.cloned.1.call-start = ((), (), s32[]{:S(2)}) async-start(), calls=%async_computation.7 | async-start | bytes 1572864 | tf_op jit(solution)/shard_map/reduce_scatter | solution.py:237
  96.9 53.8 %all-reduce.16.cloned.1.call-start = ((), (), s32[]{:S(2)}) async-start(), calls=%async_computation.16 | async-start | bytes 4866048
  126.3 36.5 %all-gather.17.cloned.1.call-start = ((), (), s32[]{:S(2)}) async-start(), calls=%async_computation.8 | async-start | bytes 1572864 | tf_op jit(solution)/shard_map/all_gather | solution.py:253
  127.1 27.0 %copy-start.77 = (f32[512]{0:T(512)}, f32[512]{0:T(512)S(1)}, u32[]{:S(2)}) copy-start(f32[512]{0:T(512)S(1)} %convert_element_type.394) | copy-start | bytes 6148
  135.1 39.4 %all-gather.23.cloned.1.call-start = ((), (), s32[]{:S(2)}) async-start(), calls=%async_computation.12 | async-start | bytes 1572864 | tf_op jit(solution)/shard_map/all_gather | solution.py:283
  135.7 53.3 %all-gather.13.cloned.1.call-start = ((), (), s32[]{:S(2)}) async-start(), calls=%async_computation.5 | async-start | bytes 3686400 | tf_op jit(solution)/shard_map/all_gather | solution.py:252
  157.8 45.6 %all-gather.19.cloned.1.call-start = ((), (), s32[]{:S(2)}) async-start(), calls=%async_computation.10 | async-start | bytes 3686400 | tf_op jit(solution)/shard_map/all_gather | solution.py:282
  160.3 62.0 %reduce-scatter.14.cloned.1.call-start = ((), (), s32[]{:S(2)}) async-start(), calls=%async_computation.13 | async-start | bytes 1572864 | tf_op jit(solution)/shard_map/reduce_scatter | solution.py:323
  184.0 44.1 %reduce-scatter.12.cloned.1.call-start = ((), (), s32[]{:S(2)}) async-start(), calls=%async_computation.9 | async-start | bytes 1572864 | tf_op jit(solution)/shard_map/reduce_scatter | solution.py:273
  188.5 65.6 %all-reduce.18.cloned.1.call-start = ((), (), s32[]{:S(2)}) async-start(), calls=%async_computation.17 | async-start | bytes 4841472
  203.4 11.3 copy-start.119
  220.9 58.9 %all-gather.25.cloned.1.call-start = ((), (), s32[]{:S(2)}) async-start(), calls=%async_computation.14 | async-start | bytes 1572864 | tf_op jit(solution)/shard_map/all_gather | solution.py:342
  222.3 45.2 %copy-start.73 = (f32[1,4,1,768]{3,1,2,0:T(4,128)}, f32[1,4,1,768]{3,1,2,0:T(4,128)S(1)}, u32[]{:S(2)}) copy-start(f32[1,4,1,768]{3,1,2,0:T(4,128)S(1)} %convert_bitcast_fusion.3) | copy-start | bytes 36868
  233.7 28.6 %copy-start.80 = (f32[768]{0:T(1024)S(1)}, f32[768]{0:T(1024)}, u32[]{:S(2)}) copy-start(f32[768]{0:T(1024)} %convert_element_type.374) | copy-start | bytes 9220
  233.8 53.9 %all-gather.21.cloned.1.call-start = ((), (), s32[]{:S(2)}) async-start(), calls=%async_computation.11 | async-start | bytes 3686400 | tf_op jit(solution)/shard_map/all_gather | solution.py:341
  270.7 154.4 %all-reduce.24.cloned.1.call-start = ((), (), s32[]{:S(2)}) async-start(), calls=%async_computation.20 | async-start | bytes 9707520
  348.0 168.8 %reduce-scatter.16.cloned.1.call-start = ((), (), s32[]{:S(2)}) async-start(), calls=%async_computation.15 | async-start | bytes 1572864 | tf_op jit(solution)/shard_map/reduce_scatter | solution.py:470
  425.1 276.1 %all-reduce.20.cloned.1.call-start = ((), (), s32[]{:S(2)}) async-start(), calls=%async_computation.18 | async-start | bytes 23592960 | tf_op jit(solution)/shard_map/psum | solution.py:613
  432.0 22.8 %copy-start.70 = (f32[768]{0:T(1024)S(1)}, f32[768]{0:T(1024)}, u32[]{:S(2)}) copy-start(f32[768]{0:T(1024)} %copy-done.69) | copy-start | bytes 9220
  454.8 12.6 copy-start.72
  474.2 774.0 %all-reduce.22.cloned.1.call-start = ((), (), s32[]{:S(2)}) async-start(), calls=%async_computation.19 | async-start | bytes 40894464 | tf_op jit(solution)/shard_map/psum | solution.py:575
  478.9 11.8 slice-start.4
  544.9 86.9 %copy-start.97 = (f32[768]{0:T(1024)S(1)}, f32[768]{0:T(1024)}, u32[]{:S(2)}) copy-start(f32[768]{0:T(1024)} %get-tuple-element.513) | copy-start | bytes 9220
  544.9 86.9 %copy-start.98 = (f32[768]{0:T(1024)S(1)}, f32[768]{0:T(1024)}, u32[]{:S(2)}) copy-start(f32[768]{0:T(1024)} %get-tuple-element.518) | copy-start | bytes 9220
  (134 other events, 507.7 us)
Sparse Core Ops, SparseCore 0:
  14.4 11.7 all-gather.14
  50.1 13.6 all-gather.10
  97.0 10.8 reduce-scatter.9
  126.4 24.1 all-reduce.15
  152.6 10.2 all-gather.16
  164.3 10.1 all-gather.22
  176.6 12.2 all-gather.12
  191.0 12.2 all-gather.18
  206.2 9.5 reduce-scatter.13
  218.4 9.5 reduce-scatter.11
  231.0 23.0 all-reduce.17
  256.1 10.2 all-gather.24
  270.8 12.2 all-gather.20
  348.2 30.3 all-reduce.23
  425.2 9.5 reduce-scatter.15
  474.4 226.8 all-reduce.19
  709.8 538.3 all-reduce.21
where the time goes:
time: 1290 us; the launch traced here: 1280 us
  waiting for transfers between devices  607 us (47%)
  matrix products  214 us (17%)
  local copies, waits for them, and re-layouts  168 us (13%)
  other arithmetic  135 us (10%)
  blocking collectives  125 us (10%)
  between operations  16.1 us (1%)
    psum x1, waiting for transfers between devices, on_device(): lax.psum((grad_video_attend_weight, grad_video_attend_bias, grad_video_ou...  544 us
    psum x1, blocking collectives, on_device(): lax.psum((grad_video_attend_weight, grad_video_attend_bias, grad_video_ou...  77.5 us
    unnamed x250, local copies, waits for them, and re-layouts  44.2 us
    psum x1, blocking collectives, on_device(): lax.psum((grad_video_first_gain, grad_video_first_shift, grad_video_messa...  40.7 us
    unnamed x20, waiting for transfers between devices  29.9 us
  transfers between devices with their start and end apart: 17, of which 8 were waited for; matrix products, arithmetic and copies ran while one was open for 32% of the time, Pallas kernels for 0%

commit v1 on v0

--- a/solution.py
+++ b/solution.py
@@ -63,6 +63,21 @@
         * 0.125
     )
     return jnp.where(allowed[None], scores, -1000000000.0)
+
+
+def reduce_low(values, axes):
+    sums = lax.psum(tuple(value.astype(jnp.bfloat16) for value in values), axes)
+    return tuple(value.astype(jnp.float32) for value in sums)
+
+
+def reduce_packed(values, axes):
+    packed = lax.psum(jnp.concatenate([value.reshape(-1) for value in values]), axes)
+    results = []
+    start = 0
+    for value in values:
+        results.append(packed[start : start + value.size].reshape(value.shape))
+        start += value.size
+    return tuple(results)
 
 
 def on_device(
@@ -561,44 +576,59 @@
     text_input_grad = text_grad_rows.astype(jnp.bfloat16)
     (
         grad_video_attend_weight,
-        grad_video_attend_bias,
         grad_video_output_weight,
         grad_video_expand_weight,
-        grad_video_expand_bias,
         grad_video_reduce_weight,
         grad_text_attend_weight,
-        grad_text_attend_bias,
         grad_text_output_weight,
         grad_text_expand_weight,
-        grad_text_expand_bias,
         grad_text_reduce_weight,
-    ) = lax.psum(
+    ) = reduce_low(
         (
             grad_video_attend_weight,
-            grad_video_attend_bias,
             grad_video_output_weight,
             grad_video_expand_weight,
-            grad_video_expand_bias,
             grad_video_reduce_weight,
             grad_text_attend_weight,
-            grad_text_attend_bias,
             grad_text_output_weight,
             grad_text_expand_weight,
-            grad_text_expand_bias,
             grad_text_reduce_weight,
         ),
         "dp",
     )
     (
+        grad_video_message_weight,
+        grad_video_message_attend_weight,
+        grad_video_message_out_weight,
+    ) = reduce_low(
+        (
+            grad_video_message_weight,
+            grad_video_message_attend_weight,
+            grad_video_message_out_weight,
+        ),
+        ("dp", "tensor"),
+    )
+    (
+        grad_video_attend_bias,
+        grad_video_expand_bias,
+        grad_text_attend_bias,
+        grad_text_expand_bias,
+    ) = reduce_packed(
+        (
+            grad_video_attend_bias,
+            grad_video_expand_bias,
+            grad_text_attend_bias,
+            grad_text_expand_bias,
+        ),
+        "dp",
+    )
+    (
         grad_video_first_gain,
         grad_video_first_shift,
-        grad_video_message_weight,
         grad_video_message_bias,
         grad_video_message_gain,
         grad_video_message_shift,
-        grad_video_message_attend_weight,
         grad_video_message_attend_bias,
-        grad_video_message_out_weight,
         grad_video_message_out_bias,
         grad_video_output_bias,
         grad_video_final_gain,
@@ -610,17 +640,14 @@
         grad_text_final_gain,
         grad_text_final_shift,
         grad_text_reduce_bias,
-    ) = lax.psum(
+    ) = reduce_packed(
         (
             grad_video_first_gain,
             grad_video_first_shift,
-            grad_video_message_weight,
             grad_video_message_bias,
             grad_video_message_gain,
             grad_video_message_shift,
-            grad_video_message_attend_weight,
             grad_video_message_attend_bias,
-            grad_video_message_out_weight,
             grad_video_message_out_bias,
             grad_video_output_bias,
             grad_video_final_gain,

time: 1290 us -> 978 us (0.76)
  waiting for transfers between devices: 607 us -> 267 us
  other arithmetic: 135 us -> 158 us
    psum x2, waiting for transfers between devices: 566 us -> 230 us  [reduce_low(): lax.psum(tuple((value.astype(jnp.bfloat16) for value in values)), axes)]
    convert_element_type x0 -> x10, other arithmetic: none -> 22.5 us  [reduce_low(): return tuple((value.astype(jnp.float32) for value in sums))]
    unnamed x250 -> x230, local copies, waits for them, and re-layouts: 44.2 us -> 41 us
  transfers between devices with their start and end apart: 17 -> 17, of which waited for: 8 -> 7; matrix products, arithmetic and copies ran while one was open for 32% -> 45% of each run, Pallas kernels for 0% -> 0%
where the time goes in v1:
time: 978 us; the launch traced here: 967 us
  waiting for transfers between devices  267 us (27%)
  matrix products  212 us (22%)
  local copies, waits for them, and re-layouts  175 us (18%)
  other arithmetic  158 us (16%)
  blocking collectives  127 us (13%)
  between operations  16 us (2%)
  loops' own time  11.1 us (1%)
    psum x2, waiting for transfers between devices, reduce_low(): lax.psum(tuple((value.astype(jnp.bfloat16) for value in values)), axes)  230 us
    psum x2, blocking collectives, reduce_packed(): lax.psum(jnp.concatenate([value.reshape(-1) for value in values]), axes)  120 us
    unnamed x230, local copies, waits for them, and re-layouts  41 us
    unnamed x20, waiting for transfers between devices  28.1 us
    convert_element_type x10, other arithmetic, reduce_low(): return tuple((value.astype(jnp.float32) for value in sums))  22.5 us
    reduce_sum x4, other arithmetic, norm_backward(): gain_grad = jnp.sum((grad_out * unit_rows).reshape(-1, columns), axis=0)  20.3 us
    another operation x6, local copies, waits for them, and re-layouts, on_device(): jnp.stack([video_grad_queries, video_grad_keys, video_grad_values], axis=3)  19.6 us
  transfers between devices with their start and end apart: 17, of which 7 were waited for; matrix products, arithmetic and copies ran while one was open for 45% of the time, Pallas kernels for 0%

profile of v1, /device:TPU:0, one launch (start us, length us, event | category | flops | bytes accessed | tf_op | source)
XLA Modules:
  0.0 967.0 jit_solution(4868081070879499720)
XLA Ops:
  68.2 23.3 %while.31 = (s32[]{:T(128)}, bf16[2,512,4,64]{1,3,2,0:T(8,128)(2,1)}, f32[2,4,512,1]{2,1,3,0:T(4,128)}, s32[2]{0:T(128)}, bf16[1024,4,64]{0,2,1:T(8,128)(2,1)}, ...) while((s32[]{:T(128)}, ...), condition=%wide.region_19.20_spmd, body=%wide.region_16.19_spmd.sunk | while | flops 351075456 | bytes 24730504 | solution.py:242
  96.7 7.4 add_convert_fusion
  104.2 6.5 copy.228
  141.4 8.8 all-reduce.14.cloned.1.call-done
  162.4 5.8 multiply_convert_fusion.5
  168.3 5.8 all-gather.23.cloned.1.call-done
  174.1 5.8 convert_reduce_fusion.2
  183.6 4.5 convolution_convert_fusion.8
  188.5 13.7 %multiply_convert_fusion.3 = (bf16[8,197,1536]{2,1,0:T(8,128)(2,1)}, f32[8,197,1536]{2,1,0:T(8,128)}) fusion(f32[1536]{0:T(1024)S(1)} %convert_element_type.446, bf16[768,1536]{1,0:T(8,128)(2,1)} %param.63, bf16[1,8,197,768]{3,2,0,1:T(8,128)(2,1)} %all-gather.13.cloned.1.call-done), kind=kOutput, calls=%fused_computation.66 | convolution fusion | flops 3735195648 | bytes 19310592 | tf_op jit(solution)/shard_map/vfrd,dn->vfrn/dot_general | solution.py:270
  202.9 11.3 %convert_reduce_fusion = (f32[1536]{0:T(1024)}, bf16[8,197,1536]{2,1,0:T(8,128)(2,1)S(1)}) fusion(f32[8,197,1536]{2,1,0:T(8,128)} %get-tuple-element.636, f32[1536]{0:T(1024)S(1)} %convert_element_type.446, bf16[1536,768]{1,0:T(8,128)(2,1)} %param.65, bf16[1,8,197,768]{3,2,0,1:T(8,128)(2,1)} %all-gather.19.cloned.1.call-done), kind=kOutput, calls=%fused_computation.62 | convolution fusion | flops 3749718528 | bytes 19316736 | tf_op jit(solution)/shard_map/vfrd,nd->vfrn/dot_general | solution.py:309
  235.3 18.4 %all-reduce.16.cloned.1.call-done = bf16[1,8,197,768]{3,1,2,0:T(8,128)(2,1)} async-done(((bf16[1,8,197,768]{3,1,2,0:T(8,128)(2,1)}), bf16[1,8,197,768]{3,1,2,0:T(8,128)(2,1)}) %all-reduce.16.cloned.1.call-update) | async-done | bytes 2420752
  253.7 8.2 fusion.78
  262.0 5.0 fusion.184
  274.6 6.5 convert_bitcast_fusion.1
  283.5 6.3 bitcast_convert_fusion.1
  304.1 7.4 convolution_convert_fusion.1
  311.5 9.4 multiply_reduce_fusion.1
  320.8 11.5 %multiply_convert_fusion.1 = bf16[8,6,198,198]{2,3,1,0:T(8,128)(2,1)} fusion(f32[8,6,198,198]{2,3,1,0:T(8,128)} %get-tuple-element.634, f32[8,6,198,198]{2,3,1,0:T(8,128)} %copy-done.3, f32[8,6,198]{2,1,0:T(8,128)} %get-tuple-element.633, f32[8,6,198]{2,1,0:T(8,128)} %copy-done.45), kind=kLoop, calls=%fused_computation.63 | loop fusion | flops 9408960 | bytes 18893952 | tf_op jit(solution)/shard_map/convert_element_type | solution.py:387
  332.3 5.8 multiply_convert_fusion.6
  349.4 6.1 fusion.57
  359.7 58.0 %while.32 = (s32[]{:T(128)}, f32[1024,4,64]{0,2,1:T(8,128)}, f32[1024,4,64]{0,2,1:T(8,128)}, bf16[2,512,4,64]{1,3,2,0:T(8,128)(2,1)}, s32[2]{0:T(128)S(1)}, /*in...) while((s32[]{:T(128)}, f32[1024,4,64]{0,2,1:T(8,128)}, ...), condition=%wide.region_40.41_spmd, body=%wide.region_38.40_spmd.sunk | while | flops 860126336 | bytes 111950944 | solution.py:455
  376.1 5.2 multiply_reduce_fusion.9
  404.8 4.9 multiply_reduce_fusion.9
  434.8 6.9 fusion.74
  441.8 5.1 fusion.72
  469.6 4.7 all-reduce.4
  482.9 9.2 bitcast_convert_fusion.2
  497.9 6.7 bitcast_convert_fusion.3
  541.3 77.9 %psum.96 = f32[3840]{0:T(1024)S(1)} all-reduce(f32[3840]{0:T(1024)} %pad_maximum_fusion.6), channel_id=1, replica_groups=mesh['dp'=16,'tensor'=2] {'dp'}, use_global_device_ids=true, to_apply=%region_71.72 | all-reduce | flops 3840 | bytes 30720 | tf_op jit(solution)/shard_map/psum | solution.py:74
  652.3 42.1 %psum.91 = f32[12288]{0:T(1024)} all-reduce(f32[12288]{0:T(1024)} %constant_dynamic-update-slice_fusion.4), channel_id=1, replica_groups=mesh['dp'=16,'tensor'=2] {'dp','tensor'}, use_global_device_ids=true, to_apply=%region_62.63 | all-reduce | flops 12288 | bytes 98304 | tf_op jit(solution)/shard_map/psum | solution.py:74
  700.9 4.4 add_convert_fusion.3
  714.7 229.6 %all-reduce.20.cloned.1.call-done = (bf16[768,3,384]{2,0,1:T(8,128)(2,1)}, bf16[384,768]{1,0:T(8,128)(2,1)}, bf16[768,1536]{1,0:T(8,128)(2,1)}, bf16[1536,768]{1...) async-done(((bf16[768,3,384]{2,0,1:T(8,128)(2,1)}, ...) | async-done | bytes 10223632 | tf_op jit(solution)/shard_map/psum | solution.py:69
  (590 shorter events, 388.9 us)
Async XLA Ops:
  7.2 24.1 %copy-start = (bf16[768,3,768]{2,0,1:T(8,128)(2,1)S(1)}, bf16[768,3,768]{2,0,1:T(8,128)(2,1)}, u32[]{:S(2)}) copy-start(bf16[768,3,768]{2,0,1:T(8,128)(2,1)} %param.53) | copy-start | bytes 10616836
  7.3 11.6 %copy-start.96 = (bf16[2,768]{1,0:T(2,128)(2,1)S(1)}, bf16[2,768]{1,0:T(2,128)(2,1)}, u32[]{:S(2)}) copy-start(bf16[2,768]{1,0:T(2,128)(2,1)} %param.54) | copy-start | bytes 9220
  7.3 52.9 %all-gather.15.cloned.1.call-start = ((), (), s32[]{:S(2)}) async-start(), calls=%async_computation.6 | async-start | bytes 1572864 | tf_op jit(solution)/shard_map/all_gather | solution.py:182
  14.3 82.5 %all-gather.11.cloned.1.call-start = ((), (), s32[]{:S(2)}) async-start(), calls=%async_computation.4 | async-start | bytes 3686400 | tf_op jit(solution)/shard_map/all_gather | solution.py:181
  14.3 17.0 %copy-start.68 = (f32[768]{0:T(1024)}, f32[768]{0:T(1024)S(1)}, u32[]{:S(2)}) copy-start(f32[768]{0:T(1024)S(1)} %convert_element_type.420) | copy-start | bytes 9220
  15.6 15.7 %copy-start.86 = (f32[768]{0:T(1024)}, f32[768]{0:T(1024)S(1)}, u32[]{:S(2)}) copy-start(f32[768]{0:T(1024)S(1)} %convert_element_type.421) | copy-start | bytes 9220
  43.4 106.8 %copy-start.59 = (f32[1,4,1,768]{3,1,2,0:T(4,128)}, f32[1,4,1,768]{3,1,2,0:T(4,128)S(1)}, u32[]{:S(2)}) copy-start(f32[1,4,1,768]{3,1,2,0:T(4,128)S(1)} %fusion.158) | copy-start | bytes 36868
  49.9 79.3 %reduce-scatter.10.cloned.1.call-start = ((), (), s32[]{:S(2)}) async-start(), calls=%async_computation.7 | async-start | bytes 1572864 | tf_op jit(solution)/shard_map/reduce_scatter | solution.py:252
  96.4 53.8 %all-reduce.14.cloned.1.call-start = ((), (), s32[]{:S(2)}) async-start(), calls=%async_computation.16 | async-start | bytes 4866048
  125.9 36.6 %all-gather.17.cloned.1.call-start = ((), (), s32[]{:S(2)}) async-start(), calls=%async_computation.8 | async-start | bytes 1572864 | tf_op jit(solution)/shard_map/all_gather | solution.py:268
  126.6 27.0 %copy-start.76 = (f32[512]{0:T(512)}, f32[512]{0:T(512)S(1)}, u32[]{:S(2)}) copy-start(f32[512]{0:T(512)S(1)} %convert_element_type.463) | copy-start | bytes 6148
  134.6 39.4 %all-gather.23.cloned.1.call-start = ((), (), s32[]{:S(2)}) async-start(), calls=%async_computation.12 | async-start | bytes 1572864 | tf_op jit(solution)/shard_map/all_gather | solution.py:298
  135.2 53.3 %all-gather.13.cloned.1.call-start = ((), (), s32[]{:S(2)}) async-start(), calls=%async_computation.5 | async-start | bytes 3686400 | tf_op jit(solution)/shard_map/all_gather | solution.py:267
  157.3 45.6 %all-gather.19.cloned.1.call-start = ((), (), s32[]{:S(2)}) async-start(), calls=%async_computation.10 | async-start | bytes 3686400 | tf_op jit(solution)/shard_map/all_gather | solution.py:297
  159.9 66.4 %reduce-scatter.14.cloned.1.call-start = ((), (), s32[]{:S(2)}) async-start(), calls=%async_computation.13 | async-start | bytes 1572864 | tf_op jit(solution)/shard_map/reduce_scatter | solution.py:338
  183.5 46.0 %reduce-scatter.12.cloned.1.call-start = ((), (), s32[]{:S(2)}) async-start(), calls=%async_computation.9 | async-start | bytes 1572864 | tf_op jit(solution)/shard_map/reduce_scatter | solution.py:288
  188.1 65.6 %all-reduce.16.cloned.1.call-start = ((), (), s32[]{:S(2)}) async-start(), calls=%async_computation.17 | async-start | bytes 4841472
  202.9 11.3 %copy-start.111 = (bf16[768,1536]{1,0:T(8,128)(2,1)S(1)}, bf16[768,1536]{1,0:T(8,128)(2,1)}, u32[]{:S(2)}) copy-start(bf16[768,1536]{1,0:T(8,128)(2,1)} %param.63) | copy-start | bytes 7077892
  220.5 69.2 %all-gather.25.cloned.1.call-start = ((), (), s32[]{:S(2)}) async-start(), calls=%async_computation.14 | async-start | bytes 1572864 | tf_op jit(solution)/shard_map/all_gather | solution.py:357
  222.1 44.9 %copy-start.72 = (f32[1,4,1,768]{3,1,2,0:T(4,128)}, f32[1,4,1,768]{3,1,2,0:T(4,128)S(1)}, u32[]{:S(2)}) copy-start(f32[1,4,1,768]{3,1,2,0:T(4,128)S(1)} %convert_bitcast_fusion.3) | copy-start | bytes 36868
  235.2 26.8 %copy-start.79 = (f32[768]{0:T(1024)S(1)}, f32[768]{0:T(1024)}, u32[]{:S(2)}) copy-start(f32[768]{0:T(1024)} %convert_element_type.443) | copy-start | bytes 9220
  235.2 62.1 %all-gather.21.cloned.1.call-start = ((), (), s32[]{:S(2)}) async-start(), calls=%async_computation.11 | async-start | bytes 3686400 | tf_op jit(solution)/shard_map/all_gather | solution.py:356
  270.3 164.4 %all-reduce.22.cloned.1.call-start = ((), (), s32[]{:S(2)}) async-start(), calls=%async_computation.20 | async-start | bytes 9707520
  270.4 12.6 %slice-start = ((s8[4915200]{0:T(1024)(128)(4,1)}), s8[4194304]{0:T(1024)(128)(4,1)S(1)}, s32[]{:S(2)}) async-start(s8[4915200]{0:T(1024)(128)(4,1)} %bitcast.439), calls=%async_computation.21 | async-start | bytes 8388608
  357.4 153.3 %reduce-scatter.16.cloned.1.call-start = ((), (), s32[]{:S(2)}) async-start(), calls=%async_computation.15 | async-start | bytes 1572864 | tf_op jit(solution)/shard_map/reduce_scatter | solution.py:485
  434.7 270.7 %all-reduce.18.cloned.1.call-start = ((), (), s32[]{:S(2)}) async-start(), calls=%async_computation.18 | async-start | bytes 11796480 | tf_op jit(solution)/shard_map/psum | solution.py:69
  441.8 22.7 %copy-start.69 = (f32[768]{0:T(1024)S(1)}, f32[768]{0:T(1024)}, u32[]{:S(2)}) copy-start(f32[768]{0:T(1024)} %copy-done.68) | copy-start | bytes 9220
  464.5 12.1 %copy-start.71 = (bf16[8,768]{1,0:T(8,128)(2,1)S(1)}, bf16[8,768]{1,0:T(8,128)(2,1)}, u32[]{:S(2)}) copy-start(bf16[8,768]{1,0:T(8,128)(2,1)} %copy-done.70) | copy-start | bytes 36868
  482.6 461.6 %all-reduce.20.cloned.1.call-start = ((), (), s32[]{:S(2)}) async-start(), calls=%async_computation.19 | async-start | bytes 20447232 | tf_op jit(solution)/shard_map/psum | solution.py:69
  482.9 10.4 %copy-start.40 = (bf16[1024,1,256]{2,0,1:T(8,128)(2,1)S(1)}, bf16[1024,1,256]{2,0,1:T(8,128)(2,1)}, u32[]{:S(2)}) copy-start(bf16[1024,1,256]{2,0,1:T(8,128)(2,1)} %reshape.1134) | copy-start | bytes 1572868
  482.9 10.4 %copy-start.41 = (bf16[1024,1,256]{2,0,1:T(8,128)(2,1)S(1)}, bf16[1024,1,256]{2,0,1:T(8,128)(2,1)}, u32[]{:S(2)}) copy-start(bf16[1024,1,256]{2,0,1:T(8,128)(2,1)} %copy.263) | copy-start | bytes 1572868
  482.9 10.3 %copy-start.42 = (bf16[1024,1,256]{2,0,1:T(8,128)(2,1)S(1)}, bf16[1024,1,256]{2,0,1:T(8,128)(2,1)}, u32[]{:S(2)}) copy-start(bf16[1024,1,256]{2,0,1:T(8,128)(2,1)} %copy.264) | copy-start | bytes 1572868
  (121 other events, 438.7 us)
Sparse Core Ops, SparseCore 0:
  14.4 11.7 all-gather.14
  50.0 13.6 all-gather.10
  96.5 10.8 reduce-scatter.9
  126.0 24.1 all-reduce.13
  152.2 10.2 all-gather.16
  163.8 10.1 all-gather.22
  176.2 12.2 all-gather.12
  190.6 12.2 all-gather.18
  205.8 9.5 reduce-scatter.13
  218.0 9.5 reduce-scatter.11
  230.6 23.0 all-reduce.15
  255.7 10.2 all-gather.24
  270.4 12.2 all-gather.20
  357.6 30.4 all-reduce.21
  434.8 9.5 reduce-scatter.15
  482.8 155.1 all-reduce.17
  646.0 298.2 all-reduce.19

commit v2 on v0

v2 whole, which is shorter than its diff:
```python
import functools
import jax
import jax.numpy as jnp
from jax import lax
from jax.experimental import pallas as pl
from jax.experimental.pallas import tpu as pltpu
from jax.sharding import PartitionSpec as P

HD = 64
MAXLEN = 77
LANES = 128
NEGATIVE = -1000000000.0
F32 = jnp.float32
BF16 = jnp.bfloat16
PARAMS = pltpu.CompilerParams(vmem_limit_bytes=60 << 20)


def nt(left, right):
    return lax.dot_general(left, right, (((1,), (1,)), ((), ())), preferred_element_type=F32)


def tn(left, right):
    return lax.dot_general(left, right, (((0,), (0,)), ((), ())), preferred_element_type=F32)


def mm(left, right):
    return jnp.dot(left, right, preferred_element_type=F32)


def unit_of(rows):
    centre = rows - jnp.mean(rows, axis=-1, keepdims=True)
    inverse = lax.rsqrt(jnp.mean(centre * centre, axis=-1, keepdims=True) + 1e-05)
    return centre * inverse, inverse


def norm_back(grad_out, unit_rows, inverse, gain_row):
    scaled = grad_out * gain_row
    return inverse * (
        scaled
        - jnp.mean(scaled, axis=-1, keepdims=True)
        - unit_rows * jnp.mean(scaled * unit_rows, axis=-1, keepdims=True)
    )


def column_sum(values):
    return jnp.sum(values, axis=0, keepdims=True)


def row_is(shape, row):
    return lax.broadcasted_iota(jnp.int32, shape, 0) == row


def low_half():
    return lax.broadcasted_iota(jnp.int32, (1, LANES), 1) < HD


def head_masks():
    first = low_half().astype(F32)
    return first.astype(BF16), (1.0 - first).astype(BF16)


def whole(array):
    return pl.BlockSpec(array.shape, lambda *_: (0,) * array.ndim)


def rows_block(rows, columns, offset=0):
    return pl.BlockSpec((rows, columns), lambda i: (i + offset, 0))


def cost(flops, arrays, outs):
    moved = sum(a.size * a.dtype.itemsize for a in arrays) + sum(
        a.size * jnp.dtype(a.dtype).itemsize for a in outs
    )
    return pl.CostEstimate(flops=int(flops), transcendentals=0, bytes_accessed=int(moved))


def call(body, grid, ins, in_specs, outs, out_specs, scratch=(), flops=0, name=None):
    return pl.pallas_call(
        body,
        grid=grid,
        in_specs=in_specs,
        out_specs=out_specs,
        out_shape=outs,
        scratch_shapes=list(scratch),
        compiler_params=PARAMS,
        cost_estimate=cost(flops, ins, outs),
        name=name,
    )(*ins)


def shape_of(shape, dtype):
    return jax.ShapeDtypeStruct(shape, dtype)


def video_first(frames_rows, tokens, gain, shift, token_row):
    frames, rows, width = frames_rows.shape

    def body(x_ref, token_ref, gain_ref, shift_ref, rows_ref, first_ref):
        x = x_ref[0].astype(F32)
        x = jnp.where(row_is(x.shape, token_row), token_ref[0], x)
        rows_ref[...] = x
        unit, _ = unit_of(x)
        first_ref[...] = (unit * gain_ref[...] + shift_ref[...]).astype(BF16)

    ins = (frames_rows, tokens, gain, shift)
    return call(
        body,
        (frames,),
        ins,
        [
            pl.BlockSpec((1, rows, width), lambda i: (i, 0, 0)),
            pl.BlockSpec((1, 1, width), lambda i: (i, 0, 0)),
            whole(gain),
            whole(shift),
        ],
        [shape_of((frames * rows, width), F32), shape_of((frames * rows, width), BF16)],
        [rows_block(rows, width), rows_block(rows, width)],
        name="video_first",
    )


def text_first(rows_in, gain, shift, block):
    rows, width = rows_in.shape

    def body(x_ref, gain_ref, shift_ref, first_ref):
        unit, _ = unit_of(x_ref[...].astype(F32))
        first_ref[...] = (unit * gain_ref[...] + shift_ref[...]).astype(BF16)

    ins = (rows_in, gain, shift)
    return call(
        body,
        (rows // block,),
        ins,
        [rows_block(block, width), whole(gain), whole(shift)],
        [shape_of((rows, width), BF16)],
        [rows_block(block, width)],
        name="text_first",
    )[0]


def masked(scores, plan, group, segments):
    if plan["keys"] is not None:
        columns = lax.broadcasted_iota(jnp.int32, scores.shape, 1)
        return jnp.where(columns < plan["keys"], scores, NEGATIVE)
    query_start, queries, key_start, keys, _ = group
    column_ref, row_ref = segments
    same = (
        column_ref[query_start : query_start + queries, :]
        == row_ref[:, key_start : key_start + keys]
    )
    columns = lax.broadcasted_iota(jnp.int32, scores.shape, 1) + key_start
    positions = lax.broadcasted_iota(jnp.int32, scores.shape, 0) + query_start
    return jnp.where(same & (columns <= positions), scores, NEGATIVE)


def attention_forward(first, weight, bias, plan, segments, name):
    rows, width = first.shape
    heads_width = weight.shape[2]
    steps = heads_width // LANES
    out_rows = plan["out_rows"]

    def body(x_ref, w_ref, b_ref, *rest):
        segment_refs, (mixed_ref, out_ref, lse_ref, wide_ref) = rest[:-4], rest[-4:]
        for part in range(3):
            wide_ref[:, part * LANES : (part + 1) * LANES] = w_ref[part]
        mixed = mm(x_ref[...], wide_ref[...])
        for part in range(3):
            mixed_ref[part] = (
                mixed[:, part * LANES : (part + 1) * LANES] + b_ref[part : part + 1, :]
            ).astype(BF16)
        masks = head_masks()
        lower = low_half()
        for group in plan["groups"]:
            query_start, queries, key_start, keys, out_start = group
            q = mixed_ref[0, query_start : query_start + queries, :] * jnp.asarray(0.125, BF16)
            k = mixed_ref[1, key_start : key_start + keys, :]
            v = mixed_ref[2, key_start : key_start + keys, :]
            outs, sums = [], []
            for mask in masks:
                scores = masked(nt(q * mask, k), plan, group, segment_refs)
                top = jnp.max(scores, axis=-1, keepdims=True)
                powers = jnp.exp(scores - top)
                total = jnp.sum(powers, axis=-1, keepdims=True)
                probs = (powers * (1.0 / total)).astype(BF16)
                outs.append(mm(probs, v))
                sums.append(top + jnp.log(total))
            out_ref[out_start : out_start + queries, :] = jnp.where(lower, outs[0], outs[1]).astype(
                BF16
            )
            lse_ref[out_start : out_start + queries, :] = jnp.where(lower, sums[0], sums[1])

    ins = (first, weight, bias) + segments
    return call(
        body,
        (steps,),
        ins,
        [
            whole(first),
            pl.BlockSpec((3, width, LANES), lambda i: (0, 0, i)),
            pl.BlockSpec((3, LANES), lambda i: (0, i)),
        ]
        + [whole(s) for s in segments],
        [
            shape_of((3, rows, heads_width), BF16),
            shape_of((out_rows, heads_width), BF16),
            shape_of((out_rows, heads_width), F32),
        ],
        [
            pl.BlockSpec((3, rows, LANES), lambda i: (0, 0, i)),
            pl.BlockSpec((out_rows, LANES), lambda i: (0, i)),
            pl.BlockSpec((out_rows, LANES), lambda i: (0, i)),
        ],
        scratch=[pltpu.VMEM((width, 3 * LANES), BF16)],
        flops=2 * rows * width * 3 * heads_width * 2,
        name=name,
    )


def attention_backward(
    low, out_weight, attended, first, weight, mixed, lse, plan, segments, name
):
    rows, width = first.shape
    out_rows = plan["out_rows"]
    heads_width = weight.shape[2]
    steps = heads_width // LANES
    shared = plan["keys"] is None

    def body(low_ref, ow_ref, att_ref, x_ref, w_ref, mixed_ref, lse_ref, *rest):
        segment_refs = rest[: len(segments)]
        (
            out_grad_ref,
            weight_grad_ref,
            bias_ref,
            first_grad_ref,
            wide_ref,
            turned_ref,
            grad_ref,
            key_ref,
            value_ref,
        ) = rest[len(segments) :]
        step = pl.program_id(0)

        @pl.when(step == 0)
        def _():
            turned_ref[...] = x_ref[...].T
            first_grad_ref[...] = jnp.zeros_like(first_grad_ref)

        for part in range(3):
            wide_ref[:, part * LANES : (part + 1) * LANES] = w_ref[part]
        low_rows = low_ref[...]
        grad_out = nt(low_rows, ow_ref[...]).astype(BF16)
        out_grad_ref[...] = tn(att_ref[...], low_rows).astype(BF16)
        if shared:
            grad_ref[...] = jnp.zeros_like(grad_ref)
            key_ref[...] = jnp.zeros_like(key_ref)
            value_ref[...] = jnp.zeros_like(value_ref)
        masks = head_masks()
        lower = low_half()
        for group in plan["groups"]:
            query_start, queries, key_start, keys, out_start = group
            q = mixed_ref[0, query_start : query_start + queries, :] * jnp.asarray(0.125, BF16)
            k = mixed_ref[1, key_start : key_start + keys, :]
            v = mixed_ref[2, key_start : key_start + keys, :]
            g = grad_out[out_start : out_start + queries, :]
            query_grads, key_grad, value_grad = [], None, None
            for head, mask in enumerate(masks):
                query_head, grad_head = q * mask, g * mask
                scores = masked(nt(query_head, k), plan, group, segment_refs)
                column = lse_ref[out_start : out_start + queries, head * HD : head * HD + 1]
                probs = jnp.exp(scores - column)
                grad_probs = nt(grad_head, v)
                dots = jnp.sum(probs * grad_probs, axis=-1, keepdims=True)
                grad_scores = (probs * (grad_probs - dots)).astype(BF16)
                query_grads.append(mm(grad_scores, k))
                key_term = tn(grad_scores, query_head)
                value_term = tn(probs.astype(BF16), grad_head)
                key_grad = key_term if key_grad is None else key_grad + key_term
                value_grad = value_term if value_grad is None else value_grad + value_term
            query_grad = jnp.where(lower, query_grads[0], query_grads[1]) * 0.125
            grad_ref[query_start : query_start + queries, :LANES] = query_grad.astype(BF16)
            span = slice(key_start, key_start + keys)
            if shared:
                key_ref[span, :] += key_grad
                value_ref[span, :] += value_grad
            else:
                grad_ref[span, LANES : 2 * LANES] = key_grad.astype(BF16)
                grad_ref[span, 2 * LANES :] = value_grad.astype(BF16)
        if shared:
            grad_ref[:, LANES : 2 * LANES] = key_ref[...].astype(BF16)
            grad_ref[:, 2 * LANES :] = value_ref[...].astype(BF16)
        grads = grad_ref[...]
        weight_grads = mm(turned_ref[...], grads)
        sums = column_sum(grads.astype(F32))
        for part in range(3):
            weight_grad_ref[part] = weight_grads[:, part * LANES : (part + 1) * LANES].astype(BF16)
        bias_ref[0:1, :] = sums[:, :LANES]
        bias_ref[1:2, :] = sums[:, 2 * LANES :]
        first_grad_ref[...] += nt(grads, wide_ref[...])

    ins = (low, out_weight, attended, first, weight, mixed, lse) + segments
    return call(
        body,
        (steps,),
        ins,
        [
            whole(low),
            pl.BlockSpec((LANES, width), lambda i: (i, 0)),
            pl.BlockSpec((out_rows, LANES), lambda i: (0, i)),
            whole(first),
            pl.BlockSpec((3, width, LANES), lambda i: (0, 0, i)),
            pl.BlockSpec((3, rows, LANES), lambda i: (0, 0, i)),
            pl.BlockSpec((out_rows, LANES), lambda i: (0, i)),
        ]
        + [whole(s) for s in segments],
        [
            shape_of((heads_width, width), BF16),
            shape_of((3, width, heads_width), BF16),
            shape_of((2, heads_width), F32),
            shape_of((rows, width), F32),
        ],
        [
            pl.BlockSpec((LANES, width), lambda i: (i, 0)),
            pl.BlockSpec((3, width, LANES), lambda i: (0, 0, i)),
            pl.BlockSpec((2, LANES), lambda i: (0, i)),
            pl.BlockSpec((rows, width), lambda i: (0, 0)),
        ],
        scratch=[
            pltpu.VMEM((width, 3 * LANES), BF16),
            pltpu.VMEM((width, rows), BF16),
            pltpu.VMEM((rows, 3 * LANES), BF16),
            pltpu.VMEM((rows, LANES), F32),
            pltpu.VMEM((rows, LANES), F32),
        ],
        flops=2 * rows * width * 8 * heads_width * 2,
        name=name,
    )


def project_norm(parts, weights, rows_in, bias, gain, shift, block, offset, name):
    out_rows, half = parts[0].shape
    width = bias.shape[1]

    def body(a_ref, b_ref, wa_ref, wb_ref, rows_ref, bias_ref, gain_ref, shift_ref, res_ref, out_ref):
        resid = (
            rows_ref[...].astype(F32)
            + mm(a_ref[...], wa_ref[...])
            + mm(b_ref[...], wb_ref[...])
            + bias_ref[...]
        )
        res_ref[...] = resid
        unit, _ = unit_of(resid)
        out_ref[...] = (unit * gain_ref[...] + shift_ref[...]).astype(BF16)

    ins = (*parts, *weights, rows_in, bias, gain, shift)
    return call(
        body,
        (out_rows // block,),
        ins,
        [
            rows_block(block, half),
            rows_block(block, half),
            whole(weights[0]),
            whole(weights[1]),
            rows_block(block, width, offset),
            whole(bias),
            whole(gain),
            whole(shift),
        ],
        [shape_of((out_rows, width), F32), shape_of((out_rows, width), BF16)],
        [rows_block(block, width), rows_block(block, width)],
        flops=4 * out_rows * half * width,
        name=name,
    )


def feed_forward(second, cot, expand, expand_bias, reduce, chunk, name):
    rows, width = second.shape
    units = expand.shape[1]

    def body(x_ref, cot_ref, e_ref, b_ref, r_ref, *rest):
        ge_ref, gr_ref, gb_ref, out_ref, back_ref, turned_ref = rest

        @pl.when(pl.program_id(0) == 0)
        def _():
            turned_ref[...] = x_ref[...].T
            out_ref[...] = jnp.zeros_like(out_ref)
            back_ref[...] = jnp.zeros_like(back_ref)

        cot_rows = cot_ref[...]
        hidden = mm(x_ref[...], e_ref[...]) + b_ref[...]
        grad_active = nt(cot_rows, r_ref[...])
        logistic = 1.0 / (1.0 + jnp.exp(-1.702 * hidden))
        active = (hidden * logistic).astype(BF16)
        slope = logistic + 1.702 * hidden * logistic * (1.0 - logistic)
        grad_hidden = grad_active * slope
        grad_low = grad_hidden.astype(BF16)
        gb_ref[...] = column_sum(grad_low.astype(F32))
        out_ref[...] += mm(active, r_ref[...])
        back_ref[...] += nt(grad_low, e_ref[...])
        gr_ref[...] = tn(active, cot_rows).astype(BF16)
        ge_ref[...] = mm(turned_ref[...], grad_low).astype(BF16)

    ins = (second, cot, expand, expand_bias, reduce)
    return call(
        body,
        (units // chunk,),
        ins,
        [
            whole(second),
            whole(cot),
            pl.BlockSpec((width, chunk), lambda i: (0, i)),
            pl.BlockSpec((1, chunk), lambda i: (0, i)),
            pl.BlockSpec((chunk, width), lambda i: (i, 0)),
        ],
        [
            shape_of((width, units), BF16),
            shape_of((units, width), BF16),
            shape_of((1, units), F32),
            shape_of((rows, width), F32),
            shape_of((rows, width), F32),
        ],
        [
            pl.BlockSpec((width, chunk), lambda i: (0, i)),
            pl.BlockSpec((chunk, width), lambda i: (i, 0)),
            pl.BlockSpec((1, chunk), lambda i: (0, i)),
            pl.BlockSpec((rows, width), lambda i: (0, 0)),
            pl.BlockSpec((rows, width), lambda i: (0, 0)),
        ],
        scratch=[pltpu.VMEM((width, rows), BF16)],
        flops=12 * rows * width * units,
        name=name,
    )


def resid_back(resid, outs, backs, cot, token_grads, gain, reduce_bias, block, token_row, name):
    rows, width = resid.shape

    def body(res_ref, oa_ref, ob_ref, ba_ref, bb_ref, cot_ref, *rest):
        if token_row is None:
            gain_ref, rb_ref, final_ref, grad_ref, low_ref, sums_ref = rest
        else:
            token_ref, gain_ref, rb_ref, final_ref, grad_ref, low_ref, sums_ref = rest

        @pl.when(pl.program_id(0) == 0)
        def _():
            sums_ref[...] = jnp.zeros_like(sums_ref)

        resid_rows = res_ref[...]
        final_ref[...] = (resid_rows + oa_ref[...] + ob_ref[...] + rb_ref[...]).astype(BF16)
        back = ba_ref[...] + bb_ref[...]
        unit, inverse = unit_of(resid_rows)
        cot_rows = cot_ref[...].astype(F32)
        sums_ref[0:1, :] += column_sum(cot_rows)
        sums_ref[1:2, :] += column_sum(back * unit)
        sums_ref[2:3, :] += column_sum(back)
        if token_row is not None:
            cot_rows = jnp.where(row_is(cot_rows.shape, token_row), token_ref[0], cot_rows)
        grad = cot_rows + norm_back(back, unit, inverse, gain_ref[...])
        sums_ref[3:4, :] += column_sum(grad)
        grad_ref[...] = grad
        low_ref[...] = grad.astype(BF16)

    ins = (resid, *outs, *backs, cot)
    specs = [rows_block(block, width)] * 6
    if token_row is not None:
        ins += (token_grads,)
        specs.append(pl.BlockSpec((1, 1, width), lambda i: (i, 0, 0)))
    ins += (gain, reduce_bias)
    specs += [whole(gain), whole(reduce_bias)]
    return call(
        body,
        (rows // block,),
        ins,
        specs,
        [
            shape_of((rows, width), BF16),
            shape_of((rows, width), F32),
            shape_of((rows, width), BF16),
            shape_of((4, width), F32),
        ],
        [rows_block(block, width)] * 3 + [pl.BlockSpec((4, width), lambda i: (0, 0))],
        name=name,
    )


def video_rows_back(rows_in, firsts, grad_resid, gain, block, token_row):
    rows, width = rows_in.shape
    frames = rows // block

    def body(rows_ref, fa_ref, fb_ref, grad_ref, gain_ref, out_ref, edge_ref, sums_ref):
        @pl.when(pl.program_id(0) == 0)
        def _():
            sums_ref[...] = jnp.zeros_like(sums_ref)

        unit, inverse = unit_of(rows_ref[...])
        back = fa_ref[...] + fb_ref[...]
        sums_ref[0:1, :] += column_sum(back * unit)
        sums_ref[1:2, :] += column_sum(back)
        grad = grad_ref[...] + norm_back(back, unit, inverse, gain_ref[...])
        out_ref[...] = grad.astype(BF16)
        edge_ref[0, 0:1, :] = grad[0:1, :]
        edge_ref[0, 1:2, :] = grad[token_row : token_row + 1, :]

    ins = (rows_in, *firsts, grad_resid, gain)
    return call(
        body,
        (frames,),
        ins,
        [rows_block(block, width)] * 4 + [whole(gain)],
        [
            shape_of((rows, width), BF16),
            shape_of((frames, 2, width), F32),
            shape_of((2, width), F32),
        ],
        [
            rows_block(block, width),
            pl.BlockSpec((1, 2, width), lambda i: (i, 0, 0)),
            pl.BlockSpec((2, width), lambda i: (0, 0)),
        ],
        name="video_rows_back",
    )


def text_rows_back(rows_in, firsts, grad_resid, gain, block):
    rows, width = rows_in.shape
    ahead = (rows - grad_resid.shape[0]) // block

    def body(rows_ref, fa_ref, fb_ref, grad_ref, gain_ref, out_ref, sums_ref):
        step = pl.program_id(0)

        @pl.when(step == 0)
        def _():
            sums_ref[...] = jnp.zeros_like(sums_ref)

        unit, inverse = unit_of(rows_ref[...].astype(F32))
        back = fa_ref[...] + fb_ref[...]
        sums_ref[0:1, :] += column_sum(back * unit)
        sums_ref[1:2, :] += column_sum(back)
        own = jnp.where(step >= ahead, 1.0, 0.0)
        out_ref[...] = grad_ref[...] * own + norm_back(back, unit, inverse, gain_ref[...])

    ins = (rows_in, *firsts, grad_resid, gain)
    return call(
        body,
        (rows // block,),
        ins,
        [rows_block(block, width)] * 3
        + [
            pl.BlockSpec((block, width), lambda i: (jnp.maximum(i - ahead, 0), 0)),
            whole(gain),
        ],
        [shape_of((rows, width), F32), shape_of((2, width), F32)],
        [rows_block(block, width), pl.BlockSpec((2, width), lambda i: (0, 0))],
        name="text_rows_back",
    )


def head_rows(values, heads):
    lanes = lax.broadcasted_iota(jnp.int32, values.shape, 1) // HD
    return jnp.concatenate(
        [jnp.where(lanes == head, values, 0.0) for head in range(heads)], axis=0
    ).astype(BF16)


def fold_heads(values, heads, rows):
    lanes = lax.broadcasted_iota(jnp.int32, (rows, values.shape[1]), 1) // HD
    total = jnp.zeros((rows, values.shape[1]), F32)
    for head in range(heads):
        total = total + jnp.where(lanes == head, values[head * rows : (head + 1) * rows], 0.0)
    return total


def message_probs(mixed_ref, heads):
    query_rows = head_rows(mixed_ref[0].astype(F32) * 0.125, heads)
    scores = nt(query_rows, mixed_ref[1])
    top = jnp.max(scores, axis=-1, keepdims=True)
    powers = jnp.exp(scores - top)
    return query_rows, powers * (1.0 / jnp.sum(powers, axis=-1, keepdims=True))


def messages_forward(messages, gain, shift, weight, bias, out_weight, out_bias):
    rows, width = messages.shape
    heads = width // HD

    def body(m_ref, gain_ref, shift_ref, w_ref, b_ref, ow_ref, ob_ref, n_ref, mixed_ref, a_ref, t_ref):
        messages_now = m_ref[...]
        unit, _ = unit_of(messages_now)
        normed = (unit * gain_ref[...] + shift_ref[...]).astype(BF16)
        n_ref[...] = normed
        for part in range(3):
            mixed_ref[part] = (mm(normed, w_ref[part]) + b_ref[part : part + 1, :]).astype(BF16)
        _, probs = message_probs(mixed_ref, heads)
        attended = fold_heads(mm(probs.astype(BF16), mixed_ref[2]), heads, rows).astype(BF16)
        a_ref[...] = attended
        t_ref[...] = messages_now + mm(attended, ow_ref[...]) + ob_ref[...]

    ins = (messages, gain, shift, weight, bias, out_weight, out_bias)
    outs = [
        shape_of((rows, width), BF16),
        shape_of((3, rows, width), BF16),
        shape_of((rows, width), BF16),
        shape_of((rows, width), F32),
    ]
    return call(
        body, (1,), ins, [whole(a) for a in ins], outs, [whole(o) for o in outs], name="messages"
    )


def messages_backward(messages, mixed, token_grads, gain, weight, out_weight, in_weight):
    rows, width = messages.shape
    heads = width // HD

    def body(m_ref, mixed_ref, t_ref, gain_ref, w_ref, ow_ref, iw_ref, g_ref, low_ref, c_ref, s_ref):
        token = t_ref[...]
        grad_attended = nt(token.astype(BF16), ow_ref[...]).astype(BF16)
        query_rows, probs = message_probs(mixed_ref, heads)
        grad_rows = head_rows(grad_attended.astype(F32), heads)
        grad_probs = nt(grad_rows, mixed_ref[2])
        dots = jnp.sum(probs * grad_probs, axis=-1, keepdims=True)
        grad_scores = (probs * (grad_probs - dots)).astype(BF16)
        grads = (
            fold_heads(mm(grad_scores, mixed_ref[1]), heads, rows) * 0.125,
            tn(grad_scores, query_rows),
            tn(probs.astype(BF16), grad_rows),
        )
        normed_grad = jnp.zeros((rows, width), F32)
        for part in range(3):
            low = grads[part].astype(BF16)
            g_ref[part] = low
            normed_grad = normed_grad + nt(low, w_ref[part])
        s_ref[0:1, :] = column_sum(g_ref[0].astype(F32))
        s_ref[1:2, :] = column_sum(g_ref[2].astype(F32))
        unit, inverse = unit_of(m_ref[...])
        s_ref[2:3, :] = column_sum(normed_grad * unit)
        s_ref[3:4, :] = column_sum(normed_grad)
        grad = token + norm_back(normed_grad, unit, inverse, gain_ref[...])
        s_ref[4:5, :] = column_sum(grad)
        s_ref[5:6, :] = column_sum(token)
        low = grad.astype(BF16)
        low_ref[...] = low
        c_ref[...] = nt(low, iw_ref[...])

    ins = (messages, mixed, token_grads, gain, weight, out_weight, in_weight)
    outs = [
        shape_of((3, rows, width), BF16),
        shape_of((rows, width), BF16),
        shape_of((rows, width), F32),
        shape_of((6, width), F32),
    ]
    return call(
        body,
        (1,),
        ins,
        [whole(a) for a in ins],
        outs,
        [whole(o) for o in outs],
        name="messages_back",
    )


def swap(value):
    return lax.ppermute(value, "tensor", [(0, 1), (1, 0)])


def in_order(own, other, axis=0):
    first = lax.axis_index("tensor") == 0
    return jnp.where(
        first, jnp.concatenate([own, other], axis), jnp.concatenate([other, own], axis)
    )


def own_part(values, size, axis=0):
    return lax.dynamic_slice_in_dim(values, lax.axis_index("tensor") * size, size, axis)


def row_of(vector):
    return vector.astype(F32).reshape(1, -1)


def qkv_bias(flat):
    rows = flat.astype(F32).reshape(2, -1)
    return jnp.stack([rows[0], jnp.zeros_like(rows[0]), rows[1]])


def reduce_bucket(own, other):
    received = [swap(value) for value in other]
    sums = [
        (mine.astype(F32) + theirs.astype(F32)).astype(BF16) for mine, theirs in zip(own, received)
    ]
    return [value.astype(F32) for value in lax.psum(tuple(sums), "dp")]


def on_device(
    video_input,
    text_input,
    caption_lengths,
    video_first_gain,
    video_first_shift,
    video_message_weight,
    video_message_bias,
    video_message_gain,
    video_message_shift,
    video_message_attend_weight,
    video_message_attend_bias,
    video_message_out_weight,
    video_message_out_bias,
    video_attend_weight,
    video_attend_bias,
    video_output_weight,
    video_output_bias,
    video_final_gain,
    video_final_shift,
    video_expand_weight,
    video_expand_bias,
    video_reduce_weight,
    video_reduce_bias,
    text_first_gain,
    text_first_shift,
    text_attend_weight,
    text_attend_bias,
    text_output_weight,
    text_output_bias,
    text_final_gain,
    text_final_shift,
    text_expand_weight,
    text_expand_bias,
    text_reduce_weight,
    text_reduce_bias,
    video_out_grad,
    message_out_grad,
    text_out_grad,
):
    core = lax.axis_index("tensor")
    frames, tokens, width = video_input.shape[1:]
    frame_rows = -(-(tokens + 1) // 16) * 16
    spare = ((0, 0), (0, frame_rows - tokens), (0, 0))
    text_count, text_width = text_input.shape
    halo = -(-(MAXLEN - 1) // LANES) * LANES

    class_rows = video_input[0, :, 0, :]
    messages_here = (
        jnp.dot(class_rows, video_message_weight, preferred_element_type=F32)
        + video_message_bias.astype(F32)
    )
    messages_there = swap(messages_here)
    text_qkv = (text_attend_weight.transpose(1, 0, 2),)
    video_qkv = (video_attend_weight.transpose(1, 0, 2),)
    small = (video_attend_bias, video_expand_bias, text_attend_bias, text_expand_bias)
    packed = jnp.concatenate([value.reshape(-1) for value in small])
    packed_there = swap(packed)
    biases = []
    begin = 0
    for value in small:
        biases.append((packed[begin : begin + value.size], packed_there[begin : begin + value.size]))
        begin += value.size
    text_ahead = lax.ppermute(text_input[text_count - halo :], "tensor", [(0, 1)])
    text_qkv += (swap(text_qkv[0]),)
    video_qkv += (swap(video_qkv[0]),)
    text_out = (text_output_weight, swap(text_output_weight))
    video_out = (video_output_weight, swap(video_output_weight))
    video_expand = (video_expand_weight, swap(video_expand_weight))
    video_reduce = (video_reduce_weight, swap(video_reduce_weight))
    text_expand = (text_expand_weight, swap(text_expand_weight))
    text_reduce = (text_reduce_weight, swap(text_reduce_weight))
    video_qkv_bias = [qkv_bias(flat) for flat in biases[0]]
    text_qkv_bias = [qkv_bias(flat) for flat in biases[2]]
    sides = (0, 1)

    text_rows = jnp.concatenate([text_ahead, text_input])
    rows_all = text_count + halo
    caption_ends = jnp.cumsum(caption_lengths[0])
    positions = core * text_count - halo + jnp.arange(rows_all, dtype=jnp.int32)
    segment = jnp.sum((positions[:, None] >= caption_ends[None, :]).astype(jnp.int32), axis=1)
    segment = jnp.where(positions < 0, -1, segment)
    segments = (segment.reshape(-1, 1), segment.reshape(1, -1))
    text_plan = {
        "groups": [
            (halo + start, LANES, start, halo + LANES, start)
            for start in range(0, text_count, LANES)
        ],
        "keys": None,
        "out_rows": text_count,
    }
    text_gain, text_gain_two = row_of(text_first_gain), row_of(text_final_gain)
    text_normed = text_first(text_rows, text_gain, row_of(text_first_shift), LANES)
    text_attention = [
        attention_forward(
            text_normed, text_qkv[side], text_qkv_bias[side], text_plan, segments, "text_attention"
        )
        for side in sides
    ]
    text_resid, text_second = project_norm(
        [text_attention[side][1] for side in sides],
        text_out,
        text_rows,
        row_of(text_output_bias),
        text_gain_two,
        row_of(text_final_shift),
        LANES,
        halo // LANES,
        "text_project",
    )

    messages = in_order(messages_here, messages_there)
    message_weight = video_message_attend_weight.transpose(1, 0, 2)
    message_gain = row_of(video_message_gain)
    message_normed, message_mixed, message_attended, message_tokens = messages_forward(
        messages,
        message_gain,
        row_of(video_message_shift),
        message_weight,
        qkv_bias(video_message_attend_bias),
        video_message_out_weight,
        row_of(video_message_out_bias),
    )
    tokens_here = own_part(message_tokens, frames)

    video_gain, video_gain_two = row_of(video_first_gain), row_of(video_final_gain)
    video_rows, video_normed = video_first(
        jnp.pad(video_input[0], spare),
        tokens_here[:, None],
        video_gain,
        row_of(video_first_shift),
        tokens,
    )
    video_plan = {
        "groups": [
            (start, frame_rows, start, frame_rows, start)
            for start in range(0, frames * frame_rows, frame_rows)
        ],
        "keys": tokens + 1,
        "out_rows": frames * frame_rows,
    }
    video_attention = [
        attention_forward(
            video_normed, video_qkv[side], video_qkv_bias[side], video_plan, (), "video_attention"
        )
        for side in sides
    ]
    video_resid, video_second = project_norm(
        [video_attention[side][1] for side in sides],
        video_out,
        video_rows,
        row_of(video_output_bias),
        video_gain_two,
        row_of(video_final_shift),
        frame_rows,
        0,
        "video_project",
    )
    message_output = video_resid.reshape(frames, frame_rows, width)[:, tokens].astype(BF16)[None]

    video_cot = jnp.pad(video_out_grad[0], spare).reshape(-1, width)
    video_units = {}
    text_units = {}
    for side in (1, 0):
        video_units[side] = feed_forward(
            video_second,
            video_cot,
            video_expand[side],
            row_of(biases[1][side]),
            video_reduce[side],
            video_expand[side].shape[1] // 3,
            "video_units",
        )
    for side in (1, 0):
        text_units[side] = feed_forward(
            text_second,
            text_out_grad,
            text_expand[side],
            row_of(biases[3][side]),
            text_reduce[side],
            text_expand[side].shape[1] // 2,
            "text_units",
        )
    grad_video_expand_weight, grad_video_reduce_weight = reduce_bucket(
        video_units[0][:2], video_units[1][:2]
    )
    grad_text_expand_weight, grad_text_reduce_weight = reduce_bucket(
        text_units[0][:2], text_units[1][:2]
    )
    video_final, video_grad_resid, video_low, video_sums = resid_back(
        video_resid,
        [video_units[side][3] for side in sides],
        [video_units[side][4] for side in sides],
        video_cot,
        message_out_grad[0].astype(F32)[:, None],
        video_gain_two,
        row_of(video_reduce_bias),
        frame_rows,
        tokens,
        "video_resid_back",
    )
    text_final, text_grad_resid, text_low, text_sums = resid_back(
        text_resid,
        [text_units[side][3] for side in sides],
        [text_units[side][4] for side in sides],
        text_out_grad,
        None,
        text_gain_two,
        row_of(text_reduce_bias),
        LANES,
        None,
        "text_resid_back",
    )
    video_output = video_final.reshape(1, frames, frame_rows, width)[:, :, :tokens]

    video_back, text_back = {}, {}
    for side in (1, 0):
        video_back[side] = attention_backward(
            video_low,
            video_out[side],
            video_attention[side][1],
            video_normed,
            video_qkv[side],
            video_attention[side][0],
            video_attention[side][2],
            video_plan,
            (),
            "video_attention_back",
        )
    for side in (1, 0):
        text_back[side] = attention_backward(
            text_low,
            text_out[side],
            text_attention[side][1],
            text_normed,
            text_qkv[side],
            text_attention[side][0],
            text_attention[side][2],
            text_plan,
            segments,
            "text_attention_back",
        )
    grad_video_output_weight, grad_video_attend_weight = reduce_bucket(
        video_back[0][:2], video_back[1][:2]
    )
    grad_text_output_weight, grad_text_attend_weight = reduce_bucket(
        text_back[0][:2], text_back[1][:2]
    )
    video_grads, video_edges, video_sums_one = video_rows_back(
        video_rows,
        [video_back[side][3] for side in sides],
        video_grad_resid,
        video_gain,
        frame_rows,
        tokens,
    )
    text_grads, text_sums_one = text_rows_back(
        text_rows, [text_back[side][3] for side in sides], text_grad_resid, text_gain, LANES
    )
    text_later = lax.ppermute(text_grads[:halo], "tensor", [(1, 0)])
    text_own = text_grads[halo:]
    text_input_grad = jnp.concatenate(
        [text_own[: text_count - halo], text_own[text_count - halo :] + text_later]
    ).astype(BF16)

    token_here = video_edges[:, 1]
    token_grads = in_order(token_here, swap(token_here))
    message_grads, message_low, class_grads, message_sums = messages_backward(
        messages,
        message_mixed,
        token_grads,
        message_gain,
        message_weight,
        video_message_out_weight,
        video_message_weight,
    )
    class_row = (video_edges[:, 0] + own_part(class_grads, frames)).astype(BF16)
    video_input_grad = (
        video_grads.reshape(frames, frame_rows, width)[:, :tokens].at[:, 0].set(class_row)[None]
    )
    factors = jnp.concatenate(
        [
            class_rows,
            own_part(message_normed, frames),
            own_part(message_attended, frames),
            token_here.astype(BF16),
            own_part(message_low, frames),
        ]
        + [own_part(message_grads[part], frames) for part in range(3)],
        axis=1,
    )
    factors = lax.all_gather(factors, ("dp", "tensor"), axis=0, tiled=True)
    factors = [factors[:, at * width : (at + 1) * width] for at in range(8)]
    contract = functools.partial(jnp.einsum, "rd,re->de", preferred_element_type=F32)
    grad_video_message_weight = contract(factors[0], factors[4])
    grad_video_message_out_weight = contract(factors[2], factors[3])
    grad_video_message_attend_weight = jnp.stack(
        [contract(factors[1], factors[5 + part]) for part in range(3)]
    ).transpose(1, 0, 2)

    vectors = [
        video_sums_one[0],
        video_sums_one[1],
        message_sums[4] * 0.5,
        message_sums[2] * 0.5,
        message_sums[3] * 0.5,
        message_sums[0] * 0.5,
        message_sums[1] * 0.5,
        message_sums[5] * 0.5,
        video_sums[3],
        video_sums[1],
        video_sums[2],
        video_sums[0],
        text_sums_one[0],
        text_sums_one[1],
        text_sums[3],
        text_sums[1],
        text_sums[2],
        text_sums[0],
        in_order(video_back[0][2][0], video_back[1][2][0]),
        in_order(video_back[0][2][1], video_back[1][2][1]),
        in_order(video_units[0][2][0], video_units[1][2][0]),
        in_order(text_back[0][2][0], text_back[1][2][0]),
        in_order(text_back[0][2][1], text_back[1][2][1]),
        in_order(text_units[0][2][0], text_units[1][2][0]),
    ]
    summed = lax.psum(jnp.concatenate(vectors), ("dp", "tensor"))
    done = []
    begin = 0
    for value in vectors:
        done.append(summed[begin : begin + value.size])
        begin += value.size
    half = [own_part(value, value.size // 2) for value in done[18:]]
    return (
        video_output,
        message_output,
        text_final,
        video_input_grad,
        text_input_grad,
        done[0],
        done[1],
        grad_video_message_weight,
        done[2],
        done[3],
        done[4],
        grad_video_message_attend_weight,
        jnp.stack([done[5], done[6]]),
        grad_video_message_out_weight,
        done[7],
        grad_video_attend_weight.transpose(1, 0, 2),
        jnp.stack([half[0], half[1]]),
        grad_video_output_weight,
        done[8],
        done[9],
        done[10],
        grad_video_expand_weight,
        half[2],
        grad_video_reduce_weight,
        done[11],
        done[12],
        done[13],
        grad_text_attend_weight.transpose(1, 0, 2),
        jnp.stack([half[3], half[4]]),
        grad_text_output_weight,
        done[14],
        done[15],
        done[16],
        grad_text_expand_weight,
        half[5],
        grad_text_reduce_weight,
        done[17],
    )


def solution(mesh):
    in_specs = (
        P("dp", "tensor", None, None),
        P(("dp", "tensor"), None),
        P("dp", None),
        P(),
        P(),
        P(),
        P(),
        P(),
        P(),
        P(),
        P(),
        P(),
        P(),
        P(None, None, "tensor"),
        P(None, "tensor"),
        P("tensor", None),
        P(),
        P(),
        P(),
        P(None, "tensor"),
        P("tensor"),
        P("tensor", None),
        P(),
        P(),
        P(),
        P(None, None, "tensor"),
        P(None, "tensor"),
        P("tensor", None),
        P(),
        P(),
        P(),
        P(None, "tensor"),
        P("tensor"),
        P("tensor", None),
        P(),
        P("dp", "tensor", None, None),
        P("dp", "tensor", None),
        P(("dp", "tensor"), None),
    )
    out_specs = (
        P("dp", "tensor", None, None),
        P("dp", "tensor", None),
        P(("dp", "tensor"), None),
        P("dp", "tensor", None, None),
        P(("dp", "tensor"), None),
        P(),
        P(),
        P(),
        P(),
        P(),
        P(),
        P(),
        P(),
        P(),
        P(),
        P(None, None, "tensor"),
        P(None, "tensor"),
        P("tensor", None),
        P(),
        P(),
        P(),
        P(None, "tensor"),
        P("tensor"),
        P("tensor", None),
        P(),
        P(),
        P(),
        P(None, None, "tensor"),
        P(None, "tensor"),
        P("tensor", None),
        P(),
        P(),
        P(),
        P(None, "tensor"),
        P("tensor"),
        P("tensor", None),
        P(),
    )
    return jax.shard_map(
        on_device, mesh=mesh, in_specs=in_specs, out_specs=out_specs, check_vma=False
    )
```

time: 1290 us -> 774 us (0.60)
  matrix products: 214 us -> 6.82 us
  Pallas kernels: 0 us -> 195 us
  waiting for transfers between devices: 607 us -> 438 us
  blocking collectives: 125 us -> 0 us
  local copies, waits for them, and re-layouts: 168 us -> 43.6 us
  other arithmetic: 135 us -> 54.9 us
    dot_general x58 -> x6, matrix products: 212 us -> 6.82 us  [the longest x1 1.9 us: on_device(): grad_video_message_out_weight = contract(factors[2], factors[3])]
    pallas_call x0 -> x22, Pallas kernels: none -> 195 us  [call(): pl.pallas_call(body, grid=grid, in_specs=in_specs, out_specs=out_specs, o...]
    psum x2, waiting for transfers between devices: 566 us -> 385 us  [the longest x1 294 us: reduce_bucket(): return [value.astype(F32) for value in lax.psum(tuple(sums), 'dp')]]
    psum x2 -> x0, blocking collectives: 118 us -> none  [the longest x1 77.5 us: on_device(): lax.psum((grad_video_attend_weight, grad_video_attend_bias, grad_video_ou...]
    reduce_sum x27 -> x0, other arithmetic: 56.9 us -> none  [the longest x4 20 us: norm_backward(): gain_grad = jnp.sum((grad_out * unit_rows).reshape(-1, columns), axis=0)]
    another operation x22 -> x6, local copies, waits for them, and re-layouts: 48.4 us -> 0.84 us  [the longest x6 20.3 us: on_device(): jnp.stack([video_grad_queries, video_grad_keys, video_grad_values], axis=3)]
    all_gather x8 -> x1, waiting for transfers between devices: 9.01 us -> 52.2 us  [on_device(): factors = lax.all_gather(factors, ('dp', 'tensor'), axis=0, tiled=True)]
    unnamed x20 -> x3, waiting for transfers between devices: 29.9 us -> 0.05 us
  transfers between devices with their start and end apart: 17 -> 24, of which waited for: 8 -> 4; matrix products, arithmetic and copies ran while one was open for 32% -> 11% of each run, Pallas kernels for 0% -> 26%
where the time goes in v2:
time: 774 us; the launch traced here: 764 us
  waiting for transfers between devices  438 us (57%)
  Pallas kernels  195 us (25%)
  other arithmetic  54.9 us (7%)
  local copies, waits for them, and re-layouts  43.6 us (6%)
  between operations  15.3 us (2%)
  starting transfers between devices  9.16 us (1%)
    psum x1, waiting for transfers between devices, reduce_bucket(): return [value.astype(F32) for value in lax.psum(tuple(sums), 'dp')]  294 us
    pallas_call x22, Pallas kernels, call(): pl.pallas_call(body, grid=grid, in_specs=in_specs, out_specs=out_specs, o...  195 us
    psum x1, waiting for transfers between devices, on_device(): summed = lax.psum(jnp.concatenate(vectors), ('dp', 'tensor'))  90.8 us
    all_gather x1, waiting for transfers between devices, on_device(): factors = lax.all_gather(factors, ('dp', 'tensor'), axis=0, tiled=True)  52.2 us
  transfers between devices with their start and end apart: 24, of which 4 were waited for; matrix products, arithmetic and copies ran while one was open for 11% of the time, Pallas kernels for 26%

profile of v2, /device:TPU:0, one launch (start us, length us, event | category | flops | bytes accessed | tf_op | source)
XLA Modules:
  0.0 763.6 jit_solution(13461971262630953253)
XLA Ops:
  39.6 4.3 messages.1
  45.2 4.0 video_first.1
  49.2 8.6 %video_attention.2 = (bf16[3,832,384]{2,1,0:T(8,128)(2,1)}, bf16[832,384]{1,0:T(8,128)(2,1)}, f32[832,384]{1,0:T(8,128)}) custom-call(bf16[832,768]{1,0:T(8,128)(2,1)} %get-tuple-element.125.x_ref, bf16[3,768,384]{2,1,0:T(8,128)(2,1)} %bitcast.140, f32[3,384]{1,0:T(4,128)} %get-tuple-element.271.b_ref), custom_call_target="tpu_custom_call" | custom-call | flops 2944401408 | bytes 6885888 | tf_op jit(solution)/shard_map/video_attention/pallas_call | solution.py:78
  59.4 4.1 text_first.1.x_ref
  63.5 4.8 text_attention.2
  68.5 4.8 text_attention.3
  73.9 4.4 text_project.1
  78.3 6.8 text_units.2
  85.6 6.8 text_units.3
  92.4 4.9 text_resid_back.1
  97.3 11.0 %text_attention_back.2 = (bf16[256,512]{1,0:T(8,128)(2,1)}, bf16[3,512,256]{2,1,0:T(8,128)(2,1)}, f32[2,256]{1,0:T(2,128)}, f32[640,512]{1,0:T(8,128)}) custom-call(bf16[512,512]{1,0:T(8,128)(2,1)} %get-tuple-element.157.low_ref, bf16[256,512]{1,0:T(8,128)(2,1)} %ow_ref.7, bf16[512,256]{1,0:T(8,128)(2,1)} %get-tuple-element.136.a_ref.att_ref, ...), custom_call_target="tpu_custom_call" | custom-call | flops 2684354560 | bytes 6364160 | tf_op jit(solution)/shard_map/text_attention_back/pallas_call | solution.py:78
  108.4 10.6 %text_attention_back.3 = (bf16[256,512]{1,0:T(8,128)(2,1)}, bf16[3,512,256]{2,1,0:T(8,128)(2,1)}, f32[2,256]{1,0:T(2,128)}, f32[640,512]{1,0:T(8,128)}) custom-call(bf16[512,512]{1,0:T(8,128)(2,1)} %get-tuple-element.157.low_ref, bf16[256,512]{1,0:T(8,128)(2,1)} %copy-done.23, bf16[512,256]{1,0:T(8,128)(2,1)} %get-tuple-element.137.b_ref.att_ref, ...), custom_call_target="tpu_custom_call" | custom-call | flops 2684354560 | bytes 6364160 | tf_op jit(solution)/shard_map/text_attention_back/pallas_call | solution.py:78
  119.0 5.5 text_rows_back.1
  128.1 8.5 %video_attention.3 = (bf16[3,832,384]{2,1,0:T(8,128)(2,1)}, bf16[832,384]{1,0:T(8,128)(2,1)}, f32[832,384]{1,0:T(8,128)}) custom-call(bf16[832,768]{1,0:T(8,128)(2,1)} %get-tuple-element.125.x_ref, bf16[3,768,384]{2,1,0:T(8,128)(2,1)} %collective-permute-done.1.w_ref, f32[3,384]{1,0:T(4,128)} %get-tuple-element.270.b_ref), custom_call_target="tpu_custom_call" | custom-call | flops 2944401408 | bytes 6885888 | tf_op jit(solution)/shard_map/video_attention/pallas_call | solution.py:78
  137.4 6.0 video_project.1
  143.4 18.0 %video_units.2 = (bf16[768,1536]{1,0:T(8,128)(2,1)}, bf16[1536,768]{1,0:T(8,128)(2,1)}, f32[1,1536]{1,0:T(1,128)}, f32[832,768]{1,0:T(8,128)}, f32[832,768]{1,0:T(8,128)}) custom-call(bf16[832,768]{1,0:T(8,128)(2,1)} %get-tuple-element.130.x_ref, bf16[832,768]{1,0:T(8,128)(2,1)} %bitcast.96, bf16[768,1536]{1,0:T(8,128)(2,1)} %e_ref.2, ...), custom_call_target="tpu_custom_call" | custom-call | flops 11777605632 | bytes 17117184 | tf_op jit(solution)/shard_map/video_units/pallas_call | solution.py:78
  162.1 17.9 %video_units.3 = (bf16[768,1536]{1,0:T(8,128)(2,1)}, bf16[1536,768]{1,0:T(8,128)(2,1)}, f32[1,1536]{1,0:T(1,128)}, f32[832,768]{1,0:T(8,128)}, f32[832,768]{1,0:T(8,128)}) custom-call(bf16[832,768]{1,0:T(8,128)(2,1)} %get-tuple-element.130.x_ref, bf16[832,768]{1,0:T(8,128)(2,1)} %bitcast.97, bf16[768,1536]{1,0:T(8,128)(2,1)} %collective-permute-done.4.e_ref, ...), custom_call_target="tpu_custom_call" | custom-call | flops 11777605632 | bytes 17117184 | tf_op jit(solution)/shard_map/video_units/pallas_call | solution.py:78
  180.0 8.2 %video_resid_back.1 = (bf16[832,768]{1,0:T(8,128)(2,1)}, f32[832,768]{1,0:T(8,128)}, bf16[832,768]{1,0:T(8,128)(2,1)}, f32[4,768]{1,0:T(4,128)}) custom-call(f32[832,768]{1,0:T(8,128)} %get-tuple-element.129.res_ref, f32[832,768]{1,0:T(8,128)} %get-tuple-element.131.oa_ref, f32[832,768]{1,0:T(8,128)} %get-tuple-element.132.ob_ref, ...), custom_call_target="tpu_custom_call" | custom-call | bytes 19200000 | tf_op jit(solution)/shard_map/video_resid_back/pallas_call | solution.py:78
  188.2 21.8 %video_attention_back.2 = (bf16[384,768]{1,0:T(8,128)(2,1)}, bf16[3,768,384]{2,1,0:T(8,128)(2,1)}, f32[2,384]{1,0:T(2,128)}, f32[832,768]{1,0:T(8,128)}) custom-call(bf16[832,768]{1,0:T(8,128)(2,1)} %get-tuple-element.145.low_ref, bf16[384,768]{1,0:T(8,128)(2,1)} %ow_ref.5, bf16[832,384]{1,0:T(8,128)(2,1)} %get-tuple-element.126.a_ref.att_ref, ...), custom_call_target="tpu_custom_call" | custom-call | flops 7851737088 | bytes 13667328 | tf_op jit(solution)/shard_map/video_attention_back/pallas_call | solution.py:78
  210.0 21.6 %video_attention_back.3 = (bf16[384,768]{1,0:T(8,128)(2,1)}, bf16[3,768,384]{2,1,0:T(8,128)(2,1)}, f32[2,384]{1,0:T(2,128)}, f32[832,768]{1,0:T(8,128)}) custom-call(bf16[832,768]{1,0:T(8,128)(2,1)} %get-tuple-element.145.low_ref, bf16[384,768]{1,0:T(8,128)(2,1)} %copy-done.20, bf16[832,384]{1,0:T(8,128)(2,1)} %get-tuple-element.127.b_ref.att_ref, ...), custom_call_target="tpu_custom_call" | custom-call | flops 7851737088 | bytes 13667328 | tf_op jit(solution)/shard_map/video_attention_back/pallas_call | solution.py:78
  231.7 6.6 video_rows_back.1
  242.6 6.3 messages_back.1
  260.4 2.5 add_convert_fusion.3
  262.9 2.8 add_convert_fusion.4
  266.7 3.3 fusion
  284.6 90.8 %all-reduce.6.cloned.1.call-done = f32[19968]{0:T(1024)} async-done(((f32[19968]{0:T(1024)}), f32[19968]{0:T(1024)}) %all-reduce.6.cloned.1.call-update) | async-done | bytes 79888 | tf_op jit(solution)/shard_map/psum | solution.py:1019
  383.0 52.2 %all-gather.3.cloned.1.call-done = bf16[32,4,6144]{2,1,0:T(4,128)(2,1)} async-done(((bf16[1,4,6144]{2,1,0:T(4,128)(2,1)}), bf16[32,4,6144]{2,1,0:T(4,128)(2,1)}) %all-gather.3.cloned.1.call-update) | async-done | bytes 1572880 | tf_op jit(solution)/shard_map/all_gather | solution.py:984
  435.2 2.7 reshape.421
  439.4 3.4 maximum_bitcast_fusion
  446.6 294.4 %all-reduce.8.cloned.1.call-done = (bf16[768,3,384]{2,0,1:T(8,128)(2,1)}, bf16[384,768]{1,0:T(8,128)(2,1)}, bf16[768,1536]{1,0:T(8,128)(2,1)}, bf16[1536,768]{1,...) async-done(((bf16[768,3,384]{2,0,1:T(8,128)(2,1)}, ...) | async-done | bytes 10223632 | tf_op jit(solution)/shard_map/psum | solution.py:690
  741.0 4.6 convert_element_type.188
  745.7 2.5 convert_element_type.192
  (335 shorter events, 93.7 us)
Async XLA Ops:
  7.2 14.8 %copy-start.7 = (bf16[1,4,197,768]{3,1,2,0:T(4,128)(2,1)S(1)}, bf16[1,4,197,768]{3,1,2,0:T(4,128)(2,1)}, u32[]{:S(2)}) copy-start(bf16[1,4,197,768]{3,1,2,0:T(4,128)(2,1)} %param.40) | copy-start | bytes 3631108
  7.2 368.2 %all-reduce.6.cloned.1.call-start = ((), (), s32[]{:S(2)}) async-start(), calls=%async_computation | async-start | bytes 163840 | tf_op jit(solution)/shard_map/psum | solution.py:1019
  9.6 14.9 %copy-start.52 = (bf16[768]{0:T(1024)(128)(2,1)S(1)}, bf16[768]{0:T(1024)(128)(2,1)}, u32[]{:S(2)}) copy-start(bf16[768]{0:T(1024)(128)(2,1)} %param.52) | copy-start | bytes 4612
  9.6 15.4 %copy-start.53 = (bf16[768]{0:T(1024)(128)(2,1)S(1)}, bf16[768]{0:T(1024)(128)(2,1)}, u32[]{:S(2)}) copy-start(bf16[768]{0:T(1024)(128)(2,1)} %param.43) | copy-start | bytes 4612
  9.7 16.0 %copy-start.54 = (bf16[768]{0:T(1024)(128)(2,1)S(1)}, bf16[768]{0:T(1024)(128)(2,1)}, u32[]{:S(2)}) copy-start(bf16[768]{0:T(1024)(128)(2,1)} %param.44) | copy-start | bytes 4612
  9.7 16.6 %copy-start.55 = (bf16[768]{0:T(1024)(128)(2,1)S(1)}, bf16[768]{0:T(1024)(128)(2,1)}, u32[]{:S(2)}) copy-start(bf16[768]{0:T(1024)(128)(2,1)} %param.57) | copy-start | bytes 4612
  9.7 17.2 %copy-start.56 = (bf16[768]{0:T(1024)(128)(2,1)S(1)}, bf16[768]{0:T(1024)(128)(2,1)}, u32[]{:S(2)}) copy-start(bf16[768]{0:T(1024)(128)(2,1)} %param.56) | copy-start | bytes 4612
  9.7 17.7 %copy-start.57 = (bf16[768]{0:T(1024)(128)(2,1)S(1)}, bf16[768]{0:T(1024)(128)(2,1)}, u32[]{:S(2)}) copy-start(bf16[768]{0:T(1024)(128)(2,1)} %param.58) | copy-start | bytes 4612
  9.7 29.2 %collective-permute-start = (f32[4,768]{1,0:T(4,128)S(1)}, f32[4,768]{1,0:T(4,128)S(1)}, u32[]{:S(2)}, u32[]{:S(2)}) collective-permute-start(f32[4,768]{1,0:T(4,128)S(1)} %convolution_add_fusion), channel_id=1, source_target_pairs={{0,1},{1,0},{2,3},{3,2},{4,5},{5,4},{6,7},{7,6},{8,9},{9,8},{10,11... | collective-permute-start | bytes 36872 | tf_op jit(solution)/shard_map/ppermute | solution.py:662
  12.4 23.5 %collective-permute-start.2 = (bf16[3840]{0:T(1024)(128)(2,1)S(1)}, bf16[3840]{0:T(1024)(128)(2,1)S(1)}, u32[]{:S(2)}, u32[]{:S(2)}) collective-permute-start(bf16[3840]{0:T(1024)(128)(2,1)S(1)} %pad_maximum_fusion.2), channel_id=1, source_target_pairs={{0,1},{1,0},{2,3},{3,2},{4,5},{5,4},{6,7},{7,6},{8,9},{9,8},{10,11... | collective-permute-start | bytes 23048 | tf_op jit(solution)/shard_map/ppermute | solution.py:662
  12.4 115.2 %collective-permute-start.1 = (bf16[3,768,384]{2,1,0:T(8,128)(2,1)}, bf16[3,768,384]{2,1,0:T(8,128)(2,1)}, u32[]{:S(2)}, u32[]{:S(2)}) collective-permute-start(bf16[3,768,384]{2,1,0:T(8,128)(2,1)} %bitcast.139), channel_id=1, source_target_pairs={{0,1},{1,0},{2,3},{3,2},{4,5},{5,4},{6,7},{7,6},{8,9},{9,8},{10,11... | collective-permute-start | bytes 5308424 | tf_op jit(solution)/shard_map/ppermute | solution.py:662
  13.8 44.1 %collective-permute-start.6 = (bf16[128,512]{1,0:T(8,128)(2,1)S(1)}, bf16[128,512]{1,0:T(8,128)(2,1)S(1)}, u32[]{:S(2)}, u32[]{:S(2)}) collective-permute-start(bf16[128,512]{1,0:T(8,128)(2,1)S(1)} %slice.319), channel_id=1, source_target_pairs={{0,1},{2,3},{4,5},{6,7},{8,9},{10,11},{12,13},{14,15},{16,17},{18,... | collective-permute-start | bytes 393224 | tf_op jit(solution)/shard_map/ppermute | solution.py:756
  15.8 52.5 %collective-permute-start.7 = (bf16[3,512,256]{2,1,0:T(8,128)(2,1)}, bf16[3,512,256]{2,1,0:T(8,128)(2,1)}, u32[]{:S(2)}, u32[]{:S(2)}) collective-permute-start(bf16[3,512,256]{2,1,0:T(8,128)(2,1)} %bitcast.142), channel_id=1, source_target_pairs={{0,1},{1,0},{2,3},{3,2},{4,5},{5,4},{6,7},{7,6},{8,9},{9,8},{10,11... | collective-permute-start | bytes 2359304 | tf_op jit(solution)/shard_map/ppermute | solution.py:662
  35.9 49.2 %collective-permute-start.10 = (bf16[1024,512]{1,0:T(8,128)(2,1)}, bf16[1024,512]{1,0:T(8,128)(2,1)}, u32[]{:S(2)}, u32[]{:S(2)}) collective-permute-start(bf16[1024,512]{1,0:T(8,128)(2,1)} %r_ref.3), channel_id=1, source_target_pairs={{0,1},{1,0},{2,3},{3,2},{4,5},{5,4},{6,7},{7,6},{8,9},{9,8},{10,11... | collective-permute-start | bytes 3145736 | tf_op jit(solution)/shard_map/ppermute | solution.py:662
  38.9 46.7 %collective-permute-start.9 = (bf16[512,1024]{1,0:T(8,128)(2,1)}, bf16[512,1024]{1,0:T(8,128)(2,1)}, u32[]{:S(2)}, u32[]{:S(2)}) collective-permute-start(bf16[512,1024]{1,0:T(8,128)(2,1)} %e_ref.3), channel_id=1, source_target_pairs={{0,1},{1,0},{2,3},{3,2},{4,5},{5,4},{6,7},{7,6},{8,9},{9,8},{10,11... | collective-permute-start | bytes 3145736 | tf_op jit(solution)/shard_map/ppermute | solution.py:662
  57.9 15.3 %collective-permute-start.8 = (bf16[256,512]{1,0:T(8,128)(2,1)S(1)}, bf16[256,512]{1,0:T(8,128)(2,1)S(1)}, u32[]{:S(2)}, u32[]{:S(2)}) collective-permute-start(bf16[256,512]{1,0:T(8,128)(2,1)S(1)} %copy-done.22), channel_id=1, source_target_pairs={{0,1},{1,0},{2,3},{3,2},{4,5},{5,4},{6,7},{7,6},{8,9},{9,8},{10,11... | collective-permute-start | bytes 786440 | tf_op jit(solution)/shard_map/ppermute | solution.py:662
  68.4 68.2 %collective-permute-start.3 = (bf16[384,768]{1,0:T(8,128)(2,1)S(1)}, bf16[384,768]{1,0:T(8,128)(2,1)S(1)}, u32[]{:S(2)}, u32[]{:S(2)}) collective-permute-start(bf16[384,768]{1,0:T(8,128)(2,1)S(1)} %copy-done.19), channel_id=1, source_target_pairs={{0,1},{1,0},{2,3},{3,2},{4,5},{5,4},{6,7},{7,6},{8,9},{9,8},{10,11... | collective-permute-start | bytes 1769480 | tf_op jit(solution)/shard_map/ppermute | solution.py:662
  73.2 88.8 %collective-permute-start.4 = (bf16[768,1536]{1,0:T(8,128)(2,1)}, bf16[768,1536]{1,0:T(8,128)(2,1)}, u32[]{:S(2)}, u32[]{:S(2)}) collective-permute-start(bf16[768,1536]{1,0:T(8,128)(2,1)} %e_ref.2), channel_id=1, source_target_pairs={{0,1},{1,0},{2,3},{3,2},{4,5},{5,4},{6,7},{7,6},{8,9},{9,8},{10,11... | collective-permute-start | bytes 7077896 | tf_op jit(solution)/shard_map/ppermute | solution.py:662
  85.1 77.0 %collective-permute-start.5 = (bf16[1536,768]{1,0:T(8,128)(2,1)}, bf16[1536,768]{1,0:T(8,128)(2,1)}, u32[]{:S(2)}, u32[]{:S(2)}) collective-permute-start(bf16[1536,768]{1,0:T(8,128)(2,1)} %r_ref.2), channel_id=1, source_target_pairs={{0,1},{1,0},{2,3},{3,2},{4,5},{5,4},{6,7},{7,6},{8,9},{9,8},{10,11... | collective-permute-start | bytes 7077896 | tf_op jit(solution)/shard_map/ppermute | solution.py:662
  127.0 126.8 %collective-permute-start.18 = (bf16[256,512]{1,0:T(8,128)(2,1)}, bf16[256,512]{1,0:T(8,128)(2,1)}, u32[]{:S(2)}, u32[]{:S(2)}) collective-permute-start(bf16[256,512]{1,0:T(8,128)(2,1)} %get-tuple-element.194), channel_id=1, source_target_pairs={{0,1},{1,0},{2,3},{3,2},{4,5},{5,4},{6,7},{7,6},{8,9},{9,8},{10,11... | collective-permute-start | bytes 786440 | tf_op jit(solution)/shard_map/ppermute | solution.py:662
  127.6 127.9 %collective-permute-start.17 = (bf16[3,512,256]{2,1,0:T(8,128)(2,1)}, bf16[3,512,256]{2,1,0:T(8,128)(2,1)}, u32[]{:S(2)}, u32[]{:S(2)}) collective-permute-start(bf16[3,512,256]{2,1,0:T(8,128)(2,1)} %get-tuple-element.192), channel_id=1, source_target_pairs={{0,1},{1,0},{2,3},{3,2},{4,5},{5,4},{6,7},{7,6},{8,9},{9,8},{10,11... | collective-permute-start | bytes 2359304 | tf_op jit(solution)/shard_map/ppermute | solution.py:662
  136.6 123.4 %collective-permute-start.20 = (bf16[1024,512]{1,0:T(8,128)(2,1)}, bf16[1024,512]{1,0:T(8,128)(2,1)}, u32[]{:S(2)}, u32[]{:S(2)}) collective-permute-start(bf16[1024,512]{1,0:T(8,128)(2,1)} %get-tuple-element.198), channel_id=1, source_target_pairs={{0,1},{1,0},{2,3},{3,2},{4,5},{5,4},{6,7},{7,6},{8,9},{9,8},{10,11... | collective-permute-start | bytes 3145736 | tf_op jit(solution)/shard_map/ppermute | solution.py:662
  239.8 1.9 collective-permute-start.11
  241.2 25.5 %collective-permute-start.13 = (bf16[3,768,384]{2,1,0:T(8,128)(2,1)}, bf16[3,768,384]{2,1,0:T(8,128)(2,1)}, u32[]{:S(2)}, u32[]{:S(2)}) collective-permute-start(bf16[3,768,384]{2,1,0:T(8,128)(2,1)} %get-tuple-element.184), channel_id=1, source_target_pairs={{0,1},{1,0},{2,3},{3,2},{4,5},{5,4},{6,7},{7,6},{8,9},{9,8},{10,11... | collective-permute-start | bytes 5308424 | tf_op jit(solution)/shard_map/ppermute | solution.py:662
  241.7 28.2 %collective-permute-start.16 = (bf16[1536,768]{1,0:T(8,128)(2,1)}, bf16[1536,768]{1,0:T(8,128)(2,1)S(1)}, u32[]{:S(2)}, u32[]{:S(2)}) collective-permute-start(bf16[1536,768]{1,0:T(8,128)(2,1)} %get-tuple-element.190), channel_id=1, source_target_pairs={{0,1},{1,0},{2,3},{3,2},{4,5},{5,4},{6,7},{7,6},{8,9},{9,8},{10,11... | collective-permute-start | bytes 7077896 | tf_op jit(solution)/shard_map/ppermute | solution.py:662
  251.1 184.2 %all-gather.3.cloned.1.call-start = ((), (), s32[]{:S(2)}) async-start(), calls=%async_computation.1 | async-start | bytes 1622016 | tf_op jit(solution)/shard_map/all_gather | solution.py:984
  253.8 9.1 %collective-permute-start.19 = (bf16[512,1024]{1,0:T(8,128)(2,1)}, bf16[512,1024]{1,0:T(8,128)(2,1)}, u32[]{:S(2)}, u32[]{:S(2)}) collective-permute-start(bf16[512,1024]{1,0:T(8,128)(2,1)} %get-tuple-element.196), channel_id=1, source_target_pairs={{0,1},{1,0},{2,3},{3,2},{4,5},{5,4},{6,7},{7,6},{8,9},{9,8},{10,11... | collective-permute-start | bytes 3145736 | tf_op jit(solution)/shard_map/ppermute | solution.py:662
  255.5 485.6 %all-reduce.8.cloned.1.call-start = ((), (), s32[]{:S(2)}) async-start(), calls=%async_computation.2 | async-start | bytes 20447232 | tf_op jit(solution)/shard_map/psum | solution.py:690
  255.5 16.4 %collective-permute-start.15 = (bf16[768,1536]{1,0:T(8,128)(2,1)}, bf16[768,1536]{1,0:T(8,128)(2,1)S(1)}, u32[]{:S(2)}, u32[]{:S(2)}) collective-permute-start(bf16[768,1536]{1,0:T(8,128)(2,1)} %get-tuple-element.188), channel_id=1, source_target_pairs={{0,1},{1,0},{2,3},{3,2},{4,5},{5,4},{6,7},{7,6},{8,9},{9,8},{10,11... | collective-permute-start | bytes 7077896 | tf_op jit(solution)/shard_map/ppermute | solution.py:662
  259.9 5.7 collective-permute-start.14
  275.1 3.4 collective-permute-start.12
  284.6 153.8 %copy-start.8 = (bf16[1,4,197,768]{3,1,2,0:T(4,128)(2,1)}, bf16[1,4,197,768]{3,1,2,0:T(4,128)(2,1)S(1)}, u32[]{:S(2)}) copy-start(bf16[1,4,197,768]{3,1,2,0:T(4,128)(2,1)S(1)} %fusion.19) | copy-start | bytes 3631108
  (60 other events, 348.3 us)
Sparse Core Ops, SparseCore 0:
  251.2 124.1 all-reduce.5
  378.3 56.9 all-gather.2
  443.9 297.0 all-reduce.7

commit v3 on v2

--- a/solution.py
+++ b/solution.py
@@ -9,6 +9,8 @@
 HD = 64
 MAXLEN = 77
 LANES = 128
+VIDEO_CHUNKS = 2
+TEXT_CHUNKS = 2
 NEGATIVE = -1000000000.0
 F32 = jnp.float32
 BF16 = jnp.bfloat16
@@ -228,8 +230,7 @@
     def body(low_ref, ow_ref, att_ref, x_ref, w_ref, mixed_ref, lse_ref, *rest):
         segment_refs = rest[: len(segments)]
         (
-            out_grad_ref,
-            weight_grad_ref,
+            flat_ref,
             bias_ref,
             first_grad_ref,
             wide_ref,
@@ -249,7 +250,11 @@
             wide_ref[:, part * LANES : (part + 1) * LANES] = w_ref[part]
         low_rows = low_ref[...]
         grad_out = nt(low_rows, ow_ref[...]).astype(BF16)
-        out_grad_ref[...] = tn(att_ref[...], low_rows).astype(BF16)
+        out_grad = tn(att_ref[...], low_rows).astype(BF16)
+        for part in range(width // LANES):
+            flat_ref[3, 0, part * LANES : (part + 1) * LANES, :] = out_grad[
+                :, part * LANES : (part + 1) * LANES
+            ]
         if shared:
             grad_ref[...] = jnp.zeros_like(grad_ref)
             key_ref[...] = jnp.zeros_like(key_ref)
@@ -292,7 +297,7 @@
         weight_grads = mm(turned_ref[...], grads)
         sums = column_sum(grads.astype(F32))
         for part in range(3):
-            weight_grad_ref[part] = weight_grads[:, part * LANES : (part + 1) * LANES].astype(BF16)
+            flat_ref[part, 0] = weight_grads[:, part * LANES : (part + 1) * LANES].astype(BF16)
         bias_ref[0:1, :] = sums[:, :LANES]
         bias_ref[1:2, :] = sums[:, 2 * LANES :]
         first_grad_ref[...] += nt(grads, wide_ref[...])
@@ -313,14 +318,12 @@
         ]
         + [whole(s) for s in segments],
         [
-            shape_of((heads_width, width), BF16),
-            shape_of((3, width, heads_width), BF16),
+            shape_of((4, steps, width, LANES), BF16),
             shape_of((2, heads_width), F32),
             shape_of((rows, width), F32),
         ],
         [
-            pl.BlockSpec((LANES, width), lambda i: (i, 0)),
-            pl.BlockSpec((3, width, LANES), lambda i: (0, 0, i)),
+            pl.BlockSpec((4, 1, width, LANES), lambda i: (0, i, 0, 0)),
             pl.BlockSpec((2, LANES), lambda i: (0, i)),
             pl.BlockSpec((rows, width), lambda i: (0, 0)),
         ],
@@ -376,9 +379,10 @@
 def feed_forward(second, cot, expand, expand_bias, reduce, chunk, name):
     rows, width = second.shape
     units = expand.shape[1]
+    size = width * chunk // LANES
 
     def body(x_ref, cot_ref, e_ref, b_ref, r_ref, *rest):
-        ge_ref, gr_ref, gb_ref, out_ref, back_ref, turned_ref = rest
+        flat_ref, gb_ref, out_ref, back_ref, turned_ref = rest
 
         @pl.when(pl.program_id(0) == 0)
         def _():
@@ -397,8 +401,16 @@
         gb_ref[...] = column_sum(grad_low.astype(F32))
         out_ref[...] += mm(active, r_ref[...])
         back_ref[...] += nt(grad_low, e_ref[...])
-        gr_ref[...] = tn(active, cot_rows).astype(BF16)
-        ge_ref[...] = mm(turned_ref[...], grad_low).astype(BF16)
+        reduce_grad = tn(active, cot_rows).astype(BF16)
+        expand_grad = mm(turned_ref[...], grad_low).astype(BF16)
+        for part in range(chunk // LANES):
+            flat_ref[0, 0, part * width : (part + 1) * width, :] = expand_grad[
+                :, part * LANES : (part + 1) * LANES
+            ]
+        for part in range(width // LANES):
+            flat_ref[1, 0, part * chunk : (part + 1) * chunk, :] = reduce_grad[
+                :, part * LANES : (part + 1) * LANES
+            ]
 
     ins = (second, cot, expand, expand_bias, reduce)
     return call(
@@ -413,15 +425,13 @@
             pl.BlockSpec((chunk, width), lambda i: (i, 0)),
         ],
         [
-            shape_of((width, units), BF16),
-            shape_of((units, width), BF16),
+            shape_of((2, units // chunk, size, LANES), BF16),
             shape_of((1, units), F32),
             shape_of((rows, width), F32),
             shape_of((rows, width), F32),
         ],
         [
-            pl.BlockSpec((width, chunk), lambda i: (0, i)),
-            pl.BlockSpec((chunk, width), lambda i: (i, 0)),
+            pl.BlockSpec((2, 1, size, LANES), lambda i: (0, i, 0, 0)),
             pl.BlockSpec((1, chunk), lambda i: (0, i)),
             pl.BlockSpec((rows, width), lambda i: (0, 0)),
             pl.BlockSpec((rows, width), lambda i: (0, 0)),
@@ -682,12 +692,216 @@
     return jnp.stack([rows[0], jnp.zeros_like(rows[0]), rows[1]])
 
 
-def reduce_bucket(own, other):
-    received = [swap(value) for value in other]
-    sums = [
-        (mine.astype(F32) + theirs.astype(F32)).astype(BF16) for mine, theirs in zip(own, received)
-    ]
-    return [value.astype(F32) for value in lax.psum(tuple(sums), "dp")]
+def exchange(value, away):
+    size = lax.axis_size("dp")
+    return lax.ppermute(value, "dp", [(at, at ^ away) for at in range(size)])
+
+
+def bit_of(bit):
+    return (lax.axis_index("dp") >> bit) & 1
+
+
+def add(*values):
+    return sum(value.astype(F32) for value in values).astype(BF16)
+
+
+def dp_bits():
+    return lax.axis_size("dp").bit_length() - 1
+
+
+def by_bit(own, other, mine):
+    return jnp.where(
+        mine == 0, jnp.concatenate([own, other], 0), jnp.concatenate([other, own], 0)
+    )
+
+
+class Steps:
+    def __init__(self, make, *ins):
+        self.after = ()
+        self.steps = make(self, *ins)
+        self.result = None
+
+    def step(self, *after):
+        self.after = after
+        try:
+            return next(self.steps)
+        except StopIteration as stop:
+            self.result = stop.value
+            return ()
+
+    def hold(self, values):
+        return tie(values, self.after) if self.after else values
+
+
+def tie(value, *waited):
+    return lax.optimization_barrier((value, waited))[0]
+
+
+def take(rows, part, size):
+    return lax.dynamic_slice_in_dim(rows, part * size, size)
+
+
+def bucket_steps(steps, own, received):
+    orders = (0, 1), (1, 0)
+    bits = [bit_of(bit) for bit in orders[0]]
+    half = own.shape[0] // 2
+    spans = slice(0, half), slice(half, None)
+    parts = [[own[span], received[span]] for span in spans]
+    for at in range(2):
+        kept, arrived = [], []
+        for values, order in zip(parts, orders):
+            size = values[0].shape[0] // 2
+            mine = bits[order[at]]
+            send = [take(value, 1 - mine, size) for value in values]
+            kept.append([take(value, mine, size) for value in values])
+            arrived.append(exchange(add(*send) if at == 0 else send[0], 1 << order[at]))
+        yield arrived
+        arrived = steps.hold(arrived)
+        parts = [[add(*keep, there)] for keep, there in zip(kept, arrived)]
+    rows = jnp.concatenate([values[0] for values in parts])
+    count = lax.axis_size("dp") // 4
+    here = lax.axis_index("dp") >> 2
+    size = rows.shape[0] // count
+    arrived = [exchange(take(rows, here ^ away, size), away << 2) for away in range(1, count)]
+    yield arrived
+    arrived = steps.hold(arrived)
+    rows = add(take(rows, here, size), *arrived)
+    arrived = [exchange(rows, away << 2) for away in range(1, count)]
+    yield arrived
+    arrived = steps.hold(arrived)
+    pieces = jnp.concatenate([rows] + arrived)
+    rows = jnp.concatenate([take(pieces, at ^ here, size) for at in range(count)])
+    half = rows.shape[0] // 2
+    parts = [rows[:half], rows[half:]]
+    for at in (1, 0):
+        arrived = [exchange(value, 1 << order[at]) for value, order in zip(parts, orders)]
+        yield arrived
+        arrived = steps.hold(arrived)
+        parts = [jnp.concatenate(pair) for pair in zip(parts, arrived)]
+    return jnp.concatenate(parts), jnp.stack([bits[0] * 2 + bits[1], bits[1] * 2 + bits[0]])
+
+
+def place(at, blocks, here_ref):
+    part = blocks // 8
+    piece = at // part
+    return ((piece ^ here_ref[piece // 4]) * part + at % part, 0)
+
+
+def vector_steps(steps, vectors):
+    total = jnp.concatenate(vectors).reshape(-1, LANES)
+    there = swap(total)
+    yield there
+    total = total + steps.hold(there)
+    for bit in range(dp_bits()):
+        there = exchange(total, 1 << bit)
+        yield there
+        total = total + steps.hold(there)
+    total = total.reshape(-1)
+    done = []
+    begin = 0
+    for value in vectors:
+        done.append(total[begin : begin + value.size])
+        begin += value.size
+    return done
+
+
+def gather_steps(steps, values):
+    for bit in reversed(range(dp_bits())):
+        there = exchange(values, 1 << bit)
+        yield there
+        values = by_bit(values, steps.hold(there), bit_of(bit))
+    there = swap(values)
+    yield there
+    return in_order(values, steps.hold(there))
+
+
+def unpack(summed, first, count, block, out_shape, out_block, out_index, name):
+    rows, here = summed
+    blocks = rows.shape[0] // block
+
+    def in_index(i, here_ref):
+        return place(first + i, blocks, here_ref)
+
+    def body(here_ref, rows_ref, out_ref):
+        out_ref[...] = rows_ref[...].astype(F32).reshape(out_ref.shape)
+
+    out = shape_of(out_shape, F32)
+    return pl.pallas_call(
+        body,
+        grid_spec=pltpu.PrefetchScalarGridSpec(
+            num_scalar_prefetch=1,
+            grid=(count,),
+            in_specs=[pl.BlockSpec((block, LANES), in_index)],
+            out_specs=pl.BlockSpec(out_block, lambda i, here_ref: out_index(i)),
+        ),
+        out_shape=out,
+        compiler_params=PARAMS,
+        cost_estimate=cost(0, (rows,), (out,)),
+        name=name,
+    )(here, rows)
+
+
+def unpack_units(summed, width, units, chunk, name):
+    across = width // LANES
+    count = units // LANES
+    expand = unpack(
+        summed, 0, count, width, (width, units), (width, LANES), lambda i: (0, i), name
+    )
+    reduce = unpack(
+        summed,
+        count,
+        count,
+        chunk,
+        (units, width),
+        (chunk, LANES),
+        lambda i: (i // across, i % across),
+        name,
+    )
+    return expand, reduce
+
+
+def unpack_attention(summed, first, width, steps, name):
+    rows, here = summed
+    block = width // 2
+    blocks = rows.shape[0] // block
+
+    def body(here_ref, *refs):
+        attend_ref, out_ref = refs[8:]
+        for at in range(8):
+            values = refs[at][...].astype(F32)
+            start = at % 2 * block
+            if at < 6:
+                attend_ref[at // 2, start : start + block, :] = values
+                continue
+            for part in range(block // LANES):
+                begin = start + part * LANES
+                out_ref[:, begin : begin + LANES] = values[part * LANES : (part + 1) * LANES, :]
+
+    def in_spec(at):
+        return pl.BlockSpec(
+            (block, LANES),
+            lambda i, here_ref: place(
+                (first + at // 2 * steps + i) * 2 + at % 2, blocks, here_ref
+            ),
+        )
+
+    outs = [shape_of((3, width, steps * LANES), F32), shape_of((steps * LANES, width), F32)]
+    return pl.pallas_call(
+        body,
+        grid_spec=pltpu.PrefetchScalarGridSpec(
+            num_scalar_prefetch=1,
+            grid=(steps,),
+            in_specs=[in_spec(at) for at in range(8)],
+            out_specs=[
+                pl.BlockSpec((3, width, LANES), lambda i, here_ref: (0, 0, i)),
+                pl.BlockSpec((LANES, width), lambda i, here_ref: (i, 0)),
+            ],
+        ),
+        out_shape=outs,
+        compiler_params=PARAMS,
+        cost_estimate=cost(0, (rows,), outs),
+        name=name,
+    )(here, *([rows] * 8))
 
 
 def on_device(
@@ -766,41 +980,6 @@
     text_qkv_bias = [qkv_bias(flat) for flat in biases[2]]
     sides = (0, 1)
 
-    text_rows = jnp.concatenate([text_ahead, text_input])
-    rows_all = text_count + halo
-    caption_ends = jnp.cumsum(caption_lengths[0])
-    positions = core * text_count - halo + jnp.arange(rows_all, dtype=jnp.int32)
-    segment = jnp.sum((positions[:, None] >= caption_ends[None, :]).astype(jnp.int32), axis=1)
-    segment = jnp.where(positions < 0, -1, segment)
-    segments = (segment.reshape(-1, 1), segment.reshape(1, -1))
-    text_plan = {
-        "groups": [
-            (halo + start, LANES, start, halo + LANES, start)
-            for start in range(0, text_count, LANES)
-        ],
-        "keys": None,
-        "out_rows": text_count,
-    }
-    text_gain, text_gain_two = row_of(text_first_gain), row_of(text_final_gain)
-    text_normed = text_first(text_rows, text_gain, row_of(text_first_shift), LANES)
-    text_attention = [
-        attention_forward(
-            text_normed, text_qkv[side], text_qkv_bias[side], text_plan, segments, "text_attention"
-        )
-        for side in sides
-    ]
-    text_resid, text_second = project_norm(
-        [text_attention[side][1] for side in sides],
-        text_out,
-        text_rows,
-        row_of(text_output_bias),
-        text_gain_two,
-        row_of(text_final_shift),
-        LANES,
-        halo // LANES,
-        "text_project",
-    )
-
     messages = in_order(messages_here, messages_there)
     message_weight = video_message_attend_weight.transpose(1, 0, 2)
     message_gain = row_of(video_message_gain)
@@ -852,7 +1031,6 @@
 
     video_cot = jnp.pad(video_out_grad[0], spare).reshape(-1, width)
     video_units = {}
-    text_units = {}
     for side in (1, 0):
         video_units[side] = feed_forward(
             video_second,
@@ -860,29 +1038,118 @@
             video_expand[side],
             row_of(biases[1][side]),
             video_reduce[side],
-            video_expand[side].shape[1] // 3,
+            video_expand[side].shape[1] // VIDEO_CHUNKS,
             "video_units",
         )
+    units_bucket = Steps(
+        bucket_steps,
+        video_units[0][0].reshape(-1, LANES),
+        swap(video_units[1][0].reshape(-1, LANES)),
+    )
+    units_there = units_bucket.step()
+    text_rows = jnp.concatenate([text_ahead, text_input])
+    rows_all = text_count + halo
+    caption_ends = jnp.cumsum(caption_lengths[0])
+    positions = core * text_count - halo + jnp.arange(rows_all, dtype=jnp.int32)
+    segment = jnp.sum((positions[:, None] >= caption_ends[None, :]).astype(jnp.int32), axis=1)
+    segment = jnp.where(positions < 0, -1, segment)
+    segments = (segment.reshape(-1, 1), segment.reshape(1, -1))
+    text_plan = {
+        "groups": [
+            (halo + start, LANES, start, halo + LANES, start)
+            for start in range(0, text_count, LANES)
+        ],
+        "keys": None,
+        "out_rows": text_count,
+    }
+    text_gain, text_gain_two = row_of(text_first_gain), row_of(text_final_gain)
+    text_normed = text_first(
+        tie(text_rows, video_units[0][1]), text_gain, row_of(text_first_shift), LANES
+    )
+    text_attention = {}
+    for side in (0, 1):
+        text_attention[side] = attention_forward(
+            text_normed,
+            text_qkv[side],
+            text_qkv_bias[side],
+            text_plan,
+            segments,
+            "text_attention",
+        )
+    text_resid, text_second = project_norm(
+        [text_attention[side][1] for side in sides],
+        text_out,
+        text_rows,
+        row_of(text_output_bias),
+        text_gain_two,
+        row_of(text_final_shift),
+        LANES,
+        halo // LANES,
+        "text_project",
+    )
+    text_units = {}
     for side in (1, 0):
         text_units[side] = feed_forward(
-            text_second,
+            tie(text_second, units_there) if side == 0 else text_second,
             text_out_grad,
             text_expand[side],
             row_of(biases[3][side]),
             text_reduce[side],
-            text_expand[side].shape[1] // 2,
+            text_expand[side].shape[1] // TEXT_CHUNKS,
             "text_units",
         )
-    grad_video_expand_weight, grad_video_reduce_weight = reduce_bucket(
-        video_units[0][:2], video_units[1][:2]
-    )
-    grad_text_expand_weight, grad_text_reduce_weight = reduce_bucket(
-        text_units[0][:2], text_units[1][:2]
-    )
+    units_there = units_bucket.step(text_units[1][1])
+    text_final, text_grad_resid, text_low, text_sums = resid_back(
+        text_resid,
+        [text_units[side][2] for side in sides],
+        [text_units[side][3] for side in sides],
+        text_out_grad,
+        None,
+        text_gain_two,
+        row_of(text_reduce_bias),
+        LANES,
+        None,
+        "text_resid_back",
+    )
+    text_back = {}
+    for side in (1, 0):
+        text_back[side] = attention_backward(
+            tie(text_low, units_there) if side == 1 else text_low,
+            text_out[side],
+            text_attention[side][1],
+            text_normed,
+            text_qkv[side],
+            text_attention[side][0],
+            text_attention[side][2],
+            text_plan,
+            segments,
+            "text_attention_back",
+        )
+    text_flat, text_flat_there = (
+        jnp.concatenate(
+            [grads.reshape(-1, LANES) for grads in (text_units[side][0], text_back[side][0])]
+        )
+        for side in sides
+    )
+    text_flat_there = swap(text_flat_there)
+    text_bucket = Steps(bucket_steps, text_flat, text_flat_there)
+    units_there = units_bucket.step(text_low)
+    text_grads, text_sums_one = text_rows_back(
+        text_rows,
+        [text_back[side][2] for side in sides],
+        text_grad_resid,
+        text_gain,
+        LANES,
+    )
+    text_later = lax.ppermute(text_grads[:halo], "tensor", [(1, 0)])
+    text_own = text_grads[halo:]
+    text_input_grad = jnp.concatenate(
+        [text_own[: text_count - halo], text_own[text_count - halo :] + text_later]
+    ).astype(BF16)
     video_final, video_grad_resid, video_low, video_sums = resid_back(
-        video_resid,
+        tie(video_resid, units_there, text_flat_there, text_grads),
+        [video_units[side][2] for side in sides],
         [video_units[side][3] for side in sides],
-        [video_units[side][4] for side in sides],
         video_cot,
         message_out_grad[0].astype(F32)[:, None],
         video_gain_two,
@@ -891,24 +1158,14 @@
         tokens,
         "video_resid_back",
     )
-    text_final, text_grad_resid, text_low, text_sums = resid_back(
-        text_resid,
-        [text_units[side][3] for side in sides],
-        [text_units[side][4] for side in sides],
-        text_out_grad,
-        None,
-        text_gain_two,
-        row_of(text_reduce_bias),
-        LANES,
-        None,
-        "text_resid_back",
-    )
     video_output = video_final.reshape(1, frames, frame_rows, width)[:, :, :tokens]
 
-    video_back, text_back = {}, {}
+    text_there = text_bucket.step()
+    units_there = units_bucket.step(video_low)
+    video_back = {}
     for side in (1, 0):
         video_back[side] = attention_backward(
-            video_low,
+            tie(video_low, units_there, text_there) if side == 0 else video_low,
             video_out[side],
             video_attention[side][1],
             video_normed,
@@ -919,44 +1176,25 @@
             (),
             "video_attention_back",
         )
-    for side in (1, 0):
-        text_back[side] = attention_backward(
-            text_low,
-            text_out[side],
-            text_attention[side][1],
-            text_normed,
-            text_qkv[side],
-            text_attention[side][0],
-            text_attention[side][2],
-            text_plan,
-            segments,
-            "text_attention_back",
-        )
-    grad_video_output_weight, grad_video_attend_weight = reduce_bucket(
-        video_back[0][:2], video_back[1][:2]
-    )
-    grad_text_output_weight, grad_text_attend_weight = reduce_bucket(
-        text_back[0][:2], text_back[1][:2]
-    )
+    video_flat = video_back[0][0].reshape(-1, LANES)
+    video_flat_there = swap(video_back[1][0].reshape(-1, LANES))
+    video_bucket = Steps(bucket_steps, video_flat, video_flat_there)
+    text_there = text_bucket.step(video_back[1][1])
+    units_there = units_bucket.step(video_back[1][1])
     video_grads, video_edges, video_sums_one = video_rows_back(
-        video_rows,
-        [video_back[side][3] for side in sides],
+        tie(video_rows, video_flat_there, units_there, text_there),
+        [video_back[side][2] for side in sides],
         video_grad_resid,
         video_gain,
         frame_rows,
         tokens,
     )
-    text_grads, text_sums_one = text_rows_back(
-        text_rows, [text_back[side][3] for side in sides], text_grad_resid, text_gain, LANES
-    )
-    text_later = lax.ppermute(text_grads[:halo], "tensor", [(1, 0)])
-    text_own = text_grads[halo:]
-    text_input_grad = jnp.concatenate(
-        [text_own[: text_count - halo], text_own[text_count - halo :] + text_later]
-    ).astype(BF16)
+
+    arrivals = (text_bucket.step(video_back[0][1]), units_bucket.step(video_back[0][1]))
 
     token_here = video_edges[:, 1]
-    token_grads = in_order(token_here, swap(token_here))
+    token_there = swap(token_here)
+    token_grads = in_order(token_here, token_there)
     message_grads, message_low, class_grads, message_sums = messages_backward(
         messages,
         message_mixed,
@@ -981,15 +1219,7 @@
         + [own_part(message_grads[part], frames) for part in range(3)],
         axis=1,
     )
-    factors = lax.all_gather(factors, ("dp", "tensor"), axis=0, tiled=True)
-    factors = [factors[:, at * width : (at + 1) * width] for at in range(8)]
-    contract = functools.partial(jnp.einsum, "rd,re->de", preferred_element_type=F32)
-    grad_video_message_weight = contract(factors[0], factors[4])
-    grad_video_message_out_weight = contract(factors[2], factors[3])
-    grad_video_message_attend_weight = jnp.stack(
-        [contract(factors[1], factors[5 + part]) for part in range(3)]
-    ).transpose(1, 0, 2)
-
+    factor_rows = Steps(gather_steps, factors)
     vectors = [
         video_sums_one[0],
         video_sums_one[1],
@@ -1009,19 +1239,47 @@
         text_sums[1],
         text_sums[2],
         text_sums[0],
-        in_order(video_back[0][2][0], video_back[1][2][0]),
-        in_order(video_back[0][2][1], video_back[1][2][1]),
-        in_order(video_units[0][2][0], video_units[1][2][0]),
-        in_order(text_back[0][2][0], text_back[1][2][0]),
-        in_order(text_back[0][2][1], text_back[1][2][1]),
-        in_order(text_units[0][2][0], text_units[1][2][0]),
+        in_order(video_back[0][1][0], video_back[1][1][0]),
+        in_order(video_back[0][1][1], video_back[1][1][1]),
+        in_order(video_units[0][1][0], video_units[1][1][0]),
+        in_order(text_back[0][1][0], text_back[1][1][0]),
+        in_order(text_back[0][1][1], text_back[1][1][1]),
+        in_order(text_units[0][1][0], text_units[1][1][0]),
     ]
-    summed = lax.psum(jnp.concatenate(vectors), ("dp", "tensor"))
-    done = []
-    begin = 0
-    for value in vectors:
-        done.append(summed[begin : begin + value.size])
-        begin += value.size
+    vector_sums = Steps(vector_steps, vectors)
+    chains = (units_bucket, text_bucket, video_bucket, factor_rows, vector_sums)
+    while any(chain.result is None for chain in chains):
+        waited = (message_low, arrivals)
+        arrivals = tuple(chain.step(*waited) for chain in chains if chain.result is None)
+    done = vector_sums.result
+
+    factors = factor_rows.result
+    factors = [factors[:, at * width : (at + 1) * width] for at in range(8)]
+    contract = functools.partial(jnp.einsum, "rd,re->de", preferred_element_type=F32)
+    grad_video_message_weight = contract(factors[0], factors[4])
+    grad_video_message_out_weight = contract(factors[2], factors[3])
+    grad_video_message_attend_weight = jnp.stack(
+        [contract(factors[1], factors[5 + part]) for part in range(3)]
+    ).transpose(1, 0, 2)
+    grad_video_attend_weight, grad_video_output_weight = unpack_attention(
+        video_bucket.result, 0, width, video_attend_weight.shape[2] // LANES, "video_attention_grads"
+    )
+    text_summed = text_bucket.result
+    units = text_expand_weight.shape[1]
+    grad_text_expand_weight, grad_text_reduce_weight = unpack_units(
+        text_summed, text_width, units, units // TEXT_CHUNKS, "text_units_grads"
+    )
+    grad_text_attend_weight, grad_text_output_weight = unpack_attention(
+        text_summed,
+        2 * units // LANES,
+        text_width,
+        text_attend_weight.shape[2] // LANES,
+        "text_attention_grads",
+    )
+    units = video_expand_weight.shape[1]
+    grad_video_expand_weight, grad_video_reduce_weight = unpack_units(
+        units_bucket.result, width, units, units // VIDEO_CHUNKS, "video_units_grads"
+    )
     half = [own_part(value, value.size // 2) for value in done[18:]]
     return (
         video_output,

time: 774 us -> 543 us (0.70)
  waiting for transfers between devices: 438 us -> 52.9 us
  starting transfers between devices: 9.16 us -> 75.8 us
  Pallas kernels: 195 us -> 242 us
  local copies, waits for them, and re-layouts: 43.6 us -> 76.9 us
  other arithmetic: 54.9 us -> 80.7 us
  between operations: 15.3 us -> 2.7 us
    psum x2 -> x0, waiting for transfers between devices: 385 us -> none  [the longest x1 294 us: reduce_bucket(): return [value.astype(F32) for value in lax.psum(tuple(sums), 'dp')]]
    ppermute x0 -> x50, starting transfers between devices: none -> 69.3 us  [exchange(): return lax.ppermute(value, 'dp', [(at, at ^ away) for at in range(size)])]
    ppermute x0 -> x50, waiting for transfers between devices: none -> 52.9 us  [exchange(): return lax.ppermute(value, 'dp', [(at, at ^ away) for at in range(size)])]
    all_gather x1 -> x0, waiting for transfers between devices: 52.2 us -> none  [on_device(): factors = lax.all_gather(factors, ('dp', 'tensor'), axis=0, tiled=True)]
    pallas_call x0 -> x6, Pallas kernels: none -> 38.8 us  [the longest x4 30.1 us: unpack(): pl.pallas_call(body, grid_spec=pltpu.PrefetchScalarGridSpec(num_scalar_pr...]
    concatenate x1 -> x20, other arithmetic: 0.01 us -> 28.1 us  [the longest x6 9.15 us: bucket_steps(): parts = [jnp.concatenate(pair) for pair in zip(parts, arrived)]]
    unnamed x169 -> x244, local copies, waits for them, and re-layouts: 14.8 us -> 32.4 us
    slice x8 -> x14, local copies, waits for them, and re-layouts: 6.57 us -> 17 us  [the longest x6 13 us: bucket_steps(): parts = [[own[span], received[span]] for span in spans]]
  transfers between devices with their start and end apart: 24 -> 68, of which waited for: 4 -> 13; matrix products, arithmetic and copies ran while one was open for 11% -> 24% of each run, Pallas kernels for 26% -> 37%
where the time goes in v3:
time: 543 us; the launch traced here: 538 us
  Pallas kernels  242 us (45%)
  other arithmetic  80.7 us (15%)
  local copies, waits for them, and re-layouts  76.9 us (14%)
  starting transfers between devices  75.8 us (14%)
  waiting for transfers between devices  52.9 us (10%)
  matrix products  6.88 us (1%)
    pallas_call x22, Pallas kernels, call(): pl.pallas_call(body, grid=grid, in_specs=in_specs, out_specs=out_specs, o...  203 us
    ppermute x50, starting transfers between devices, exchange(): return lax.ppermute(value, 'dp', [(at, at ^ away) for at in range(size)])  69.3 us
    ppermute x50, waiting for transfers between devices, exchange(): return lax.ppermute(value, 'dp', [(at, at ^ away) for at in range(size)])  52.9 us
    unnamed x244, local copies, waits for them, and re-layouts  32.4 us
    pallas_call x4, Pallas kernels, unpack(): pl.pallas_call(body, grid_spec=pltpu.PrefetchScalarGridSpec(num_scalar_pr...  30.1 us
    convert_element_type x20, other arithmetic, add(): return sum((value.astype(F32) for value in values)).astype(BF16)  23 us
    slice x6, local copies, waits for them, and re-layouts, bucket_steps(): parts = [[own[span], received[span]] for span in spans]  13 us
  transfers between devices with their start and end apart: 68, of which 13 were waited for; matrix products, arithmetic and copies ran while one was open for 24% of the time, Pallas kernels for 37%

profile of v3, /device:TPU:0, one launch (start us, length us, event | category | flops | bytes accessed | tf_op | source)
XLA Modules:
  0.0 537.6 jit_solution(3625196421196281505)
XLA Ops:
  24.6 4.5 video_first.1
  29.1 8.6 %video_attention.2 = (bf16[3,832,384]{2,1,0:T(8,128)(2,1)}, bf16[832,384]{1,0:T(8,128)(2,1)}, f32[832,384]{1,0:T(8,128)}) custom-call(bf16[832,768]{1,0:T(8,128)(2,1)} %get-tuple-element.179.x_ref, bf16[3,768,384]{2,1,0:T(8,128)(2,1)} %bitcast.232, f32[3,384]{1,0:T(4,128)} %get-tuple-element.414.b_ref), custom_call_target="tpu_custom_call" | custom-call | flops 2944401408 | bytes 6885888 | tf_op jit(solution)/shard_map/video_attention/pallas_call | solution.py:80
  37.7 8.6 %video_attention.3 = (bf16[3,832,384]{2,1,0:T(8,128)(2,1)}, bf16[832,384]{1,0:T(8,128)(2,1)}, f32[832,384]{1,0:T(8,128)}) custom-call(bf16[832,768]{1,0:T(8,128)(2,1)} %get-tuple-element.179.x_ref, bf16[3,768,384]{2,1,0:T(8,128)(2,1)} %collective-permute-done.1.w_ref, f32[3,384]{1,0:T(4,128)} %get-tuple-element.413.b_ref), custom_call_target="tpu_custom_call" | custom-call | flops 2944401408 | bytes 6885888 | tf_op jit(solution)/shard_map/video_attention/pallas_call | solution.py:80
  47.1 6.0 %video_project.1 = (f32[832,768]{1,0:T(8,128)}, bf16[832,768]{1,0:T(8,128)(2,1)}) custom-call(bf16[832,384]{1,0:T(8,128)(2,1)} %get-tuple-element.180.a_ref.att_ref, bf16[832,384]{1,0:T(8,128)(2,1)} %get-tuple-element.181.b_ref.att_ref, bf16[384,768]{1,0:T(8,128)(2,1)} %ow_ref.6, bf16[384,768]{1,0:T(8,128)(2,1)} %copy-done.39, ...), custom_call_target="tpu_custom_call" | custom-call | flops 981467136 | bytes 8856576 | tf_op jit(solution)/shard_map/video_project/pallas_call | solution.py:80
  53.2 20.2 %video_units.3 = (bf16[2,2,4608,128]{3,2,1,0:T(8,128)(2,1)}, f32[1,1536]{1,0:T(1,128)}, f32[832,768]{1,0:T(8,128)}, f32[832,768]{1,0:T(8,128)}) custom-call(bf16[832,768]{1,0:T(8,128)(2,1)} %get-tuple-element.184.x_ref, bf16[832,768]{1,0:T(8,128)(2,1)} %bitcast.176, bf16[768,1536]{1,0:T(8,128)(2,1)} %collective-permute-done.4.e_ref, ...), custom_call_target="tpu_custom_call" | custom-call | flops 11777605632 | bytes 17117184 | tf_op jit(solution)/shard_map/video_units/pallas_call | solution.py:80
  82.6 20.3 %video_units.2 = (bf16[2,2,4608,128]{3,2,1,0:T(8,128)(2,1)}, f32[1,1536]{1,0:T(1,128)}, f32[832,768]{1,0:T(8,128)}, f32[832,768]{1,0:T(8,128)}) custom-call(bf16[832,768]{1,0:T(8,128)(2,1)} %get-tuple-element.184.x_ref, bf16[832,768]{1,0:T(8,128)(2,1)} %bitcast.177, bf16[768,1536]{1,0:T(8,128)(2,1)} %e_ref.2, f32[1,1536]{1,0:T(1,128)} %reshape.459.b_ref, ...), custom_call_target="tpu_custom_call" | custom-call | flops 11777605632 | bytes 17117184 | tf_op jit(solution)/shard_map/video_units/pallas_call | solution.py:80
  122.1 4.8 text_attention.2
  126.9 4.8 text_attention.3
  132.4 4.4 text_project.1
  136.8 7.9 %text_units.2 = (bf16[2,2,2048,128]{3,2,1,0:T(8,128)(2,1)}, f32[1,1024]{1,0:T(1,128)}, f32[512,512]{1,0:T(8,128)}, f32[512,512]{1,0:T(8,128)}) custom-call(bf16[512,512]{1,0:T(8,128)(2,1)} %get-tuple-element.196.x_ref, bf16[512,512]{1,0:T(8,128)(2,1)} %cot_ref.5, bf16[512,1024]{1,0:T(8,128)(2,1)} %collective-permute-done.12.e_ref, f32[1,1024]{1,0:T(1,128)} %bitcast.212, ...), custom_call_target="tpu_custom_call" | custom-call | flops 3221225472 | bytes 7348224 | tf_op jit(solution)/shard_map/text_units/pallas_call | solution.py:80
  152.2 7.5 %text_units.3 = (bf16[2,2,2048,128]{3,2,1,0:T(8,128)(2,1)}, f32[1,1024]{1,0:T(1,128)}, f32[512,512]{1,0:T(8,128)}, f32[512,512]{1,0:T(8,128)}) custom-call(bf16[512,512]{1,0:T(8,128)(2,1)} %get-tuple-element.196.x_ref, bf16[512,512]{1,0:T(8,128)(2,1)} %cot_ref.5, bf16[512,1024]{1,0:T(8,128)(2,1)} %e_ref.3, f32[1,1024]{1,0:T(1,128)} %bitcast.213, ...), custom_call_target="tpu_custom_call" | custom-call | flops 3221225472 | bytes 7348224 | tf_op jit(solution)/shard_map/text_units/pallas_call | solution.py:80
  159.7 4.9 text_resid_back.1
  167.1 10.9 %text_attention_back.2 = (bf16[4,2,512,128]{3,2,1,0:T(8,128)(2,1)}, f32[2,256]{1,0:T(2,128)}, f32[640,512]{1,0:T(8,128)}) custom-call(bf16[512,512]{1,0:T(8,128)(2,1)} %get-tuple-element.205.low_ref, bf16[256,512]{1,0:T(8,128)(2,1)} %copy-done.47, bf16[512,256]{1,0:T(8,128)(2,1)} %get-tuple-element.190.b_ref.att_ref, bf16[640,512]{1,0:T(8,128)(2,1)} %text_first.1.x_ref, ...), custom_call_target="tpu_custom_call" | custom-call | flops 2684354560 | bytes 6364160 | tf_op jit(solution)/shard_map/text_attention_back/pallas_call | solution.py:80
  178.0 5.8 %pad_maximum_fusion = bf16[12288,128]{1,0:T(8,128)(2,1)} fusion(bf16[4096,128]{1,0:T(8,128)(2,1)} %bitcast.191, bf16[8192,128]{1,0:T(8,128)(2,1)S(1)} %bitcast.186), kind=kLoop, calls=%fused_computation.1 | loop fusion | flops 6291456 | bytes 6291456 | tf_op jit(solution)/shard_map/concatenate | solution.py:1129
  190.4 10.9 %text_attention_back.3 = (bf16[4,2,512,128]{3,2,1,0:T(8,128)(2,1)}, f32[2,256]{1,0:T(2,128)}, f32[640,512]{1,0:T(8,128)}) custom-call(bf16[512,512]{1,0:T(8,128)(2,1)} %get-tuple-element.205.low_ref, bf16[256,512]{1,0:T(8,128)(2,1)} %ow_ref.5, bf16[512,256]{1,0:T(8,128)(2,1)} %get-tuple-element.189.a_ref.att_ref, bf16[640,512]{1,0:T(8,128)(2,1)} %text_first.1.x_ref, ...), custom_call_target="tpu_custom_call" | custom-call | flops 2684354560 | bytes 6364160 | tf_op jit(solution)/shard_map/text_attention_back/pallas_call | solution.py:80
  213.4 5.5 %text_rows_back.1 = (f32[640,512]{1,0:T(8,128)}, f32[2,512]{1,0:T(2,128)}) custom-call(bf16[640,512]{1,0:T(8,128)(2,1)} %copy-done.6, f32[640,512]{1,0:T(8,128)} %get-tuple-element.211.fa_ref, f32[640,512]{1,0:T(8,128)} %get-tuple-element.212.fb_ref, f32[512,512]{1,0:T(8,128)} %get-tuple-element.213.grad_ref, f32[1,512]{1,0:T(1,128)} %bitcast.196), custom_call_target="tpu_custom_call" | custom-call | bytes 5642240 | tf_op jit(solution)/shard_map/text_rows_back/pallas_call | solution.py:80
  226.1 8.3 %collective-permute-done.17 = bf16[1152,128]{1,0:T(8,128)(2,1)} collective-permute-done((bf16[1152,128]{1,0:T(8,128)(2,1)}, bf16[1152,128]{1,0:T(8,128)(2,1)}, u32[]{:S(2)}, u32[]{:S(2)}) %collective-permute-start.17) | collective-permute-done | bytes 294944 | tf_op jit(solution)/shard_map/ppermute | solution.py:697
  234.4 8.2 %video_resid_back.1 = (bf16[832,768]{1,0:T(8,128)(2,1)}, f32[832,768]{1,0:T(8,128)}, bf16[832,768]{1,0:T(8,128)(2,1)}, f32[4,768]{1,0:T(4,128)}) custom-call(f32[832,768]{1,0:T(8,128)} %get-tuple-element.215.res_ref, f32[832,768]{1,0:T(8,128)} %get-tuple-element.216.oa_ref, f32[832,768]{1,0:T(8,128)} %get-tuple-element.217.ob_ref, ...), custom_call_target="tpu_custom_call" | custom-call | bytes 19200000 | tf_op jit(solution)/shard_map/video_resid_back/pallas_call | solution.py:80
  244.9 6.2 %collective-permute-start.21 = (bf16[1152,128]{1,0:T(8,128)(2,1)S(1)}, bf16[1152,128]{1,0:T(8,128)(2,1)S(1)}, u32[]{:S(2)}, u32[]{:S(2)}) collective-permute-start(bf16[1152,128]{1,0:T(8,128)(2,1)S(1)} %add_convert_fusion.18), channel_id=1, source_target_pairs={{0,8},{2,10},{4,12},{6,14},{8,0},{10,2},{12,4},{14,6},{16,24},{18,... | collective-permute-start | bytes 884744 | tf_op jit(solution)/shard_map/ppermute | solution.py:697
  255.1 22.2 %video_attention_back.2 = (bf16[4,3,768,128]{3,2,1,0:T(8,128)(2,1)}, f32[2,384]{1,0:T(2,128)}, f32[832,768]{1,0:T(8,128)}) custom-call(bf16[832,768]{1,0:T(8,128)(2,1)} %get-tuple-element.238.low_ref, bf16[384,768]{1,0:T(8,128)(2,1)} %copy-done.39, bf16[832,384]{1,0:T(8,128)(2,1)} %get-tuple-element.181.b_ref.att_ref, ...), custom_call_target="tpu_custom_call" | custom-call | flops 7851737088 | bytes 13667328 | tf_op jit(solution)/shard_map/video_attention_back/pallas_call | solution.py:80
  289.6 10.8 %collective-permute-done.26 = bf16[3072,128]{1,0:T(8,128)(2,1)S(1)} collective-permute-done((bf16[3072,128]{1,0:T(8,128)(2,1)S(1)}, bf16[3072,128]{1,0:T(8,128)(2,1)S(1)}, u32[]{:S(2)}, u32[]{:S(2)}) %collective-permute-start.26) | collective-permute-done | bytes 786464 | tf_op jit(solution)/shard_map/ppermute | solution.py:697
  310.3 22.0 %video_attention_back.3 = (bf16[4,3,768,128]{3,2,1,0:T(8,128)(2,1)}, f32[2,384]{1,0:T(2,128)}, f32[832,768]{1,0:T(8,128)}) custom-call(bf16[832,768]{1,0:T(8,128)(2,1)} %get-tuple-element.238.low_ref, bf16[384,768]{1,0:T(8,128)(2,1)} %ow_ref.6, bf16[832,384]{1,0:T(8,128)(2,1)} %get-tuple-element.180.a_ref.att_ref, ...), custom_call_target="tpu_custom_call" | custom-call | flops 7851737088 | bytes 13667328 | tf_op jit(solution)/shard_map/video_attention_back/pallas_call | solution.py:80
  350.2 6.2 %video_rows_back.1 = (bf16[832,768]{1,0:T(8,128)(2,1)}, f32[4,2,768]{2,1,0:T(2,128)}, f32[2,768]{1,0:T(2,128)}) custom-call(f32[832,768]{1,0:T(8,128)} %get-tuple-element.237.rows_ref, f32[832,768]{1,0:T(8,128)} %get-tuple-element.241.fa_ref, f32[832,768]{1,0:T(8,128)} %get-tuple-element.242.fb_ref, f32[832,768]{1,0:T(8,128)} %get-tuple-element.243.grad_ref, ...), custom_call_target="tpu_custom_call" | custom-call | bytes 11535360 | tf_op jit(solution)/shard_map/video_rows_back/pallas_call | solution.py:80
  365.9 6.3 %messages_back.1 = (bf16[3,8,768]{2,1,0:T(8,128)(2,1)}, bf16[8,768]{1,0:T(8,128)(2,1)}, f32[8,768]{1,0:T(8,128)}, f32[6,768]{1,0:T(8,128)}) custom-call(f32[8,768]{1,0:T(8,128)} %maximum_select_fusion.5.m_ref, bf16[3,8,768]{2,1,0:T(8,128)(2,1)} %get-tuple-element.246.mixed_ref, f32[8,768]{1,0:T(8,128)} %maximum_select_fusion.6.t_ref, ...), custom_call_target="tpu_custom_call" | custom-call | bytes 6079488 | tf_op jit(solution)/shard_map/messages_back/pallas_call | solution.py:80
  392.6 10.7 %collective-permute-done.39 = bf16[768,128]{1,0:T(8,128)(2,1)S(1)} collective-permute-done((bf16[768,128]{1,0:T(8,128)(2,1)S(1)}, bf16[768,128]{1,0:T(8,128)(2,1)S(1)}, u32[]{:S(2)}, u32[]{:S(2)}) %collective-permute-start.39) | collective-permute-done | bytes 196640 | tf_op jit(solution)/shard_map/ppermute | solution.py:697
  413.7 4.7 collective-permute-start.49
  419.0 8.8 %video_units_grads.2 = f32[768,1536]{1,0:T(8,128)} custom-call(s32[2]{0:T(128)} %pad_add_fusion.here_ref, bf16[18432,128]{1,0:T(8,128)(2,1)} %constant_dynamic-update-slice_fusion.19.rows_ref), custom_call_target="tpu_custom_call" | custom-call | bytes 9437184 | tf_op jit(solution)/shard_map/video_units_grads/pallas_call | solution.py:829
  427.8 9.0 %video_units_grads.3 = f32[1536,768]{1,0:T(8,128)} custom-call(s32[2]{0:T(128)} %pad_add_fusion.here_ref, bf16[18432,128]{1,0:T(8,128)(2,1)} %constant_dynamic-update-slice_fusion.19.rows_ref), custom_call_target="tpu_custom_call" | custom-call | bytes 9437184 | tf_op jit(solution)/shard_map/video_units_grads/pallas_call | solution.py:829
  471.0 4.6 collective-permute-done.57
  489.4 6.1 %text_units_grads.2 = f32[512,1024]{1,0:T(8,128)} custom-call(s32[2]{0:T(128)} %pad_add_fusion.here_ref, bf16[12288,128]{1,0:T(8,128)(2,1)} %copy-done), custom_call_target="tpu_custom_call" | custom-call | bytes 5242880 | tf_op jit(solution)/shard_map/text_units_grads/pallas_call | solution.py:829
  495.5 6.2 %text_units_grads.3 = f32[1024,512]{1,0:T(8,128)} custom-call(s32[2]{0:T(128)} %pad_add_fusion.here_ref, bf16[12288,128]{1,0:T(8,128)(2,1)} %copy-done), custom_call_target="tpu_custom_call" | custom-call | bytes 5242880 | tf_op jit(solution)/shard_map/text_units_grads/pallas_call | solution.py:829
  531.9 5.4 %video_attention_grads.1 = (f32[3,768,384]{2,1,0:T(8,128)}, f32[384,768]{1,0:T(8,128)}) custom-call(s32[2]{0:T(128)} %pad_add_fusion.here_ref, bf16[9216,128]{1,0:T(8,128)(2,1)} %constant_dynamic-update-slice_fusion.11.refs_0_.refs_1_.refs_2_.refs_3_.refs_4_.refs_5_.refs_6_.refs_7_, ...), custom_call_target="tpu_custom_call" | custom-call | bytes 7077888 | tf_op jit(solution)/shard_map/video_attention_grads/pallas_call | solution.py:889
  (551 shorter events, 253.8 us)
Async XLA Ops:
  5.8 31.8 %collective-permute-start.1 = (bf16[3,768,384]{2,1,0:T(8,128)(2,1)}, bf16[3,768,384]{2,1,0:T(8,128)(2,1)}, u32[]{:S(2)}, u32[]{:S(2)}) collective-permute-start(bf16[3,768,384]{2,1,0:T(8,128)(2,1)} %bitcast.231), channel_id=1, source_target_pairs={{0,1},{1,0},{2,3},{3,2},{4,5},{5,4},{6,7},{7,6},{8,9},{9,8},{10,11... | collective-permute-start | bytes 5308424 | tf_op jit(solution)/shard_map/ppermute | solution.py:672
  6.3 46.7 %collective-permute-start.4 = (bf16[768,1536]{1,0:T(8,128)(2,1)}, bf16[768,1536]{1,0:T(8,128)(2,1)}, u32[]{:S(2)}, u32[]{:S(2)}) collective-permute-start(bf16[768,1536]{1,0:T(8,128)(2,1)} %e_ref.2), channel_id=1, source_target_pairs={{0,1},{1,0},{2,3},{3,2},{4,5},{5,4},{6,7},{7,6},{8,9},{9,8},{10,11... | collective-permute-start | bytes 7077896 | tf_op jit(solution)/shard_map/ppermute | solution.py:672
  6.4 46.6 %collective-permute-start.5 = (bf16[1536,768]{1,0:T(8,128)(2,1)}, bf16[1536,768]{1,0:T(8,128)(2,1)}, u32[]{:S(2)}, u32[]{:S(2)}) collective-permute-start(bf16[1536,768]{1,0:T(8,128)(2,1)} %r_ref.2), channel_id=1, source_target_pairs={{0,1},{1,0},{2,3},{3,2},{4,5},{5,4},{6,7},{7,6},{8,9},{9,8},{10,11... | collective-permute-start | bytes 7077896 | tf_op jit(solution)/shard_map/ppermute | solution.py:672
  17.0 29.3 %collective-permute-start.3 = (bf16[384,768]{1,0:T(8,128)(2,1)S(1)}, bf16[384,768]{1,0:T(8,128)(2,1)S(1)}, u32[]{:S(2)}, u32[]{:S(2)}) collective-permute-start(bf16[384,768]{1,0:T(8,128)(2,1)S(1)} %copy-done.38), channel_id=1, source_target_pairs={{0,1},{1,0},{2,3},{3,2},{4,5},{5,4},{6,7},{7,6},{8,9},{9,8},{10,11... | collective-permute-start | bytes 1769480 | tf_op jit(solution)/shard_map/ppermute | solution.py:672
  73.4 32.2 %collective-permute-start.6 = (bf16[18432,128]{1,0:T(8,128)(2,1)}, bf16[18432,128]{1,0:T(8,128)(2,1)}, u32[]{:S(2)}, u32[]{:S(2)}) collective-permute-start(bf16[18432,128]{1,0:T(8,128)(2,1)} %bitcast.228), channel_id=1, source_target_pairs={{0,1},{1,0},{2,3},{3,2},{4,5},{5,4},{6,7},{7,6},{8,9},{9,8},{10,11... | collective-permute-start | bytes 14155784 | tf_op jit(solution)/shard_map/ppermute | solution.py:672
  73.9 40.9 %collective-permute-start.9 = (bf16[128,512]{1,0:T(8,128)(2,1)S(1)}, bf16[128,512]{1,0:T(8,128)(2,1)S(1)}, u32[]{:S(2)}, u32[]{:S(2)}) collective-permute-start(bf16[128,512]{1,0:T(8,128)(2,1)S(1)} %slice.451), channel_id=1, source_target_pairs={{0,1},{2,3},{4,5},{6,7},{8,9},{10,11},{12,13},{14,15},{16,17},{18,... | collective-permute-start | bytes 393224 | tf_op jit(solution)/shard_map/ppermute | solution.py:970
  75.9 41.1 %collective-permute-start.10 = (bf16[3,512,256]{2,1,0:T(8,128)(2,1)}, bf16[3,512,256]{2,1,0:T(8,128)(2,1)}, u32[]{:S(2)}, u32[]{:S(2)}) collective-permute-start(bf16[3,512,256]{2,1,0:T(8,128)(2,1)} %bitcast.11.w_ref), channel_id=1, source_target_pairs={{0,1},{1,0},{2,3},{3,2},{4,5},{5,4},{6,7},{7,6},{8,9},{9,8},{10,11... | collective-permute-start | bytes 2359304 | tf_op jit(solution)/shard_map/ppermute | solution.py:672
  76.0 60.8 %collective-permute-start.12 = (bf16[512,1024]{1,0:T(8,128)(2,1)}, bf16[512,1024]{1,0:T(8,128)(2,1)}, u32[]{:S(2)}, u32[]{:S(2)}) collective-permute-start(bf16[512,1024]{1,0:T(8,128)(2,1)} %e_ref.3), channel_id=1, source_target_pairs={{0,1},{1,0},{2,3},{3,2},{4,5},{5,4},{6,7},{7,6},{8,9},{9,8},{10,11... | collective-permute-start | bytes 3145736 | tf_op jit(solution)/shard_map/ppermute | solution.py:672
  76.5 60.3 %collective-permute-start.13 = (bf16[1024,512]{1,0:T(8,128)(2,1)}, bf16[1024,512]{1,0:T(8,128)(2,1)}, u32[]{:S(2)}, u32[]{:S(2)}) collective-permute-start(bf16[1024,512]{1,0:T(8,128)(2,1)} %r_ref.3), channel_id=1, source_target_pairs={{0,1},{1,0},{2,3},{3,2},{4,5},{5,4},{6,7},{7,6},{8,9},{9,8},{10,11... | collective-permute-start | bytes 3145736 | tf_op jit(solution)/shard_map/ppermute | solution.py:672
  110.5 34.1 %collective-permute-start.7 = (bf16[4608,128]{1,0:T(8,128)(2,1)}, bf16[4608,128]{1,0:T(8,128)(2,1)}, u32[]{:S(2)}, u32[]{:S(2)}) collective-permute-start(bf16[4608,128]{1,0:T(8,128)(2,1)} %add_convert_fusion.3), channel_id=1, source_target_pairs={{0,2},{2,0},{4,6},{6,4},{8,10},{10,8},{12,14},{14,12},{16,18},{18,... | collective-permute-start | bytes 3538952 | tf_op jit(solution)/shard_map/ppermute | solution.py:697
  114.8 29.9 %collective-permute-start.8 = (bf16[4608,128]{1,0:T(8,128)(2,1)}, bf16[4608,128]{1,0:T(8,128)(2,1)}, u32[]{:S(2)}, u32[]{:S(2)}) collective-permute-start(bf16[4608,128]{1,0:T(8,128)(2,1)} %add_convert_fusion.2), channel_id=1, source_target_pairs={{0,4},{2,6},{4,0},{6,2},{8,12},{10,14},{12,8},{14,10},{16,20},{18,... | collective-permute-start | bytes 3538952 | tf_op jit(solution)/shard_map/ppermute | solution.py:697
  183.8 50.6 %collective-permute-start.19 = (bf16[12288,128]{1,0:T(8,128)(2,1)}, bf16[12288,128]{1,0:T(8,128)(2,1)}, u32[]{:S(2)}, u32[]{:S(2)}) collective-permute-start(bf16[12288,128]{1,0:T(8,128)(2,1)} %pad_maximum_fusion), channel_id=1, source_target_pairs={{0,1},{1,0},{2,3},{3,2},{4,5},{5,4},{6,7},{7,6},{8,9},{9,8},{10,11... | collective-permute-start | bytes 9437192 | tf_op jit(solution)/shard_map/ppermute | solution.py:672
  244.9 38.0 %collective-permute-start.21 = (bf16[1152,128]{1,0:T(8,128)(2,1)S(1)}, bf16[1152,128]{1,0:T(8,128)(2,1)S(1)}, u32[]{:S(2)}, u32[]{:S(2)}) collective-permute-start(bf16[1152,128]{1,0:T(8,128)(2,1)S(1)} %add_convert_fusion.18), channel_id=1, source_target_pairs={{0,8},{2,10},{4,12},{6,14},{8,0},{10,2},{12,4},{14,6},{16,24},{18,... | collective-permute-start | bytes 884744 | tf_op jit(solution)/shard_map/ppermute | solution.py:697
  251.1 33.4 %collective-permute-start.22 = (bf16[1152,128]{1,0:T(8,128)(2,1)S(1)}, bf16[1152,128]{1,0:T(8,128)(2,1)S(1)}, u32[]{:S(2)}, u32[]{:S(2)}) collective-permute-start(bf16[1152,128]{1,0:T(8,128)(2,1)S(1)} %add_convert_fusion.18), channel_id=1, source_target_pairs={{0,16},{2,18},{4,20},{6,22},{8,24},{10,26},{12,28},{14,30},{16,0},... | collective-permute-start | bytes 884744 | tf_op jit(solution)/shard_map/ppermute | solution.py:697
  252.2 32.3 %collective-permute-start.23 = (bf16[1152,128]{1,0:T(8,128)(2,1)S(1)}, bf16[1152,128]{1,0:T(8,128)(2,1)S(1)}, u32[]{:S(2)}, u32[]{:S(2)}) collective-permute-start(bf16[1152,128]{1,0:T(8,128)(2,1)S(1)} %add_convert_fusion.18), channel_id=1, source_target_pairs={{0,24},{2,26},{4,28},{6,30},{8,16},{10,18},{12,20},{14,22},{16,8},... | collective-permute-start | bytes 884744 | tf_op jit(solution)/shard_map/ppermute | solution.py:697
  277.4 72.8 %collective-permute-start.20 = (bf16[9216,128]{1,0:T(8,128)(2,1)}, bf16[9216,128]{1,0:T(8,128)(2,1)}, u32[]{:S(2)}, u32[]{:S(2)}) collective-permute-start(bf16[9216,128]{1,0:T(8,128)(2,1)} %bitcast.230), channel_id=1, source_target_pairs={{0,1},{1,0},{2,3},{3,2},{4,5},{5,4},{6,7},{7,6},{8,9},{9,8},{10,11... | collective-permute-start | bytes 7077896 | tf_op jit(solution)/shard_map/ppermute | solution.py:672
  287.0 47.9 %collective-permute-start.24 = (bf16[2304,128]{1,0:T(8,128)(2,1)}, bf16[2304,128]{1,0:T(8,128)(2,1)}, u32[]{:S(2)}, u32[]{:S(2)}) collective-permute-start(bf16[2304,128]{1,0:T(8,128)(2,1)} %pad_maximum_fusion.7), channel_id=1, source_target_pairs={{0,4},{2,6},{4,0},{6,2},{8,12},{10,14},{12,8},{14,10},{16,20},{18,... | collective-permute-start | bytes 1769480 | tf_op jit(solution)/shard_map/ppermute | solution.py:697
  288.4 46.5 %collective-permute-start.25 = (bf16[2304,128]{1,0:T(8,128)(2,1)}, bf16[2304,128]{1,0:T(8,128)(2,1)}, u32[]{:S(2)}, u32[]{:S(2)}) collective-permute-start(bf16[2304,128]{1,0:T(8,128)(2,1)} %pad_maximum_fusion.8), channel_id=1, source_target_pairs={{0,2},{2,0},{4,6},{6,4},{8,10},{10,8},{12,14},{14,12},{16,18},{18,... | collective-permute-start | bytes 1769480 | tf_op jit(solution)/shard_map/ppermute | solution.py:697
  304.6 38.5 %collective-permute-start.28 = (bf16[1536,128]{1,0:T(8,128)(2,1)}, bf16[1536,128]{1,0:T(8,128)(2,1)S(1)}, u32[]{:S(2)}, u32[]{:S(2)}) collective-permute-start(bf16[1536,128]{1,0:T(8,128)(2,1)} %constant_dynamic-slice_fusion.18), channel_id=1, source_target_pairs={{0,4},{2,6},{4,0},{6,2},{8,12},{10,14},{12,8},{14,10},{16,20},{18,... | collective-permute-start | bytes 1179656 | tf_op jit(solution)/shard_map/ppermute | solution.py:697
  309.1 34.1 %collective-permute-start.29 = (bf16[1536,128]{1,0:T(8,128)(2,1)}, bf16[1536,128]{1,0:T(8,128)(2,1)}, u32[]{:S(2)}, u32[]{:S(2)}) collective-permute-start(bf16[1536,128]{1,0:T(8,128)(2,1)} %constant_dynamic-slice_fusion.17), channel_id=1, source_target_pairs={{0,2},{2,0},{4,6},{6,4},{8,10},{10,8},{12,14},{14,12},{16,18},{18,... | collective-permute-start | bytes 1179656 | tf_op jit(solution)/shard_map/ppermute | solution.py:697
  337.6 38.9 %collective-permute-start.36 = (bf16[4608,128]{1,0:T(8,128)(2,1)}, bf16[4608,128]{1,0:T(8,128)(2,1)}, u32[]{:S(2)}, u32[]{:S(2)}) collective-permute-start(bf16[4608,128]{1,0:T(8,128)(2,1)} %pad_maximum_fusion.2), channel_id=1, source_target_pairs={{0,2},{2,0},{4,6},{6,4},{8,10},{10,8},{12,14},{14,12},{16,18},{18,... | collective-permute-start | bytes 3538952 | tf_op jit(solution)/shard_map/ppermute | solution.py:697
  340.6 35.9 %collective-permute-start.37 = (bf16[4608,128]{1,0:T(8,128)(2,1)}, bf16[4608,128]{1,0:T(8,128)(2,1)}, u32[]{:S(2)}, u32[]{:S(2)}) collective-permute-start(bf16[4608,128]{1,0:T(8,128)(2,1)} %pad_maximum_fusion.3), channel_id=1, source_target_pairs={{0,4},{2,6},{4,0},{6,2},{8,12},{10,14},{12,8},{14,10},{16,20},{18,... | collective-permute-start | bytes 3538952 | tf_op jit(solution)/shard_map/ppermute | solution.py:697
  347.2 26.5 %collective-permute-start.33 = (bf16[768,128]{1,0:T(8,128)(2,1)}, bf16[768,128]{1,0:T(8,128)(2,1)S(1)}, u32[]{:S(2)}, u32[]{:S(2)}) collective-permute-start(bf16[768,128]{1,0:T(8,128)(2,1)} %get-tuple-element.357), channel_id=1, source_target_pairs={{0,8},{2,10},{4,12},{6,14},{8,0},{10,2},{12,4},{14,6},{16,24},{18,... | collective-permute-start | bytes 589832 | tf_op jit(solution)/shard_map/ppermute | solution.py:697
  348.2 26.8 %collective-permute-start.34 = (bf16[768,128]{1,0:T(8,128)(2,1)}, bf16[768,128]{1,0:T(8,128)(2,1)}, u32[]{:S(2)}, u32[]{:S(2)}) collective-permute-start(bf16[768,128]{1,0:T(8,128)(2,1)} %get-tuple-element.358), channel_id=1, source_target_pairs={{0,16},{2,18},{4,20},{6,22},{8,24},{10,26},{12,28},{14,30},{16,0},... | collective-permute-start | bytes 589832 | tf_op jit(solution)/shard_map/ppermute | solution.py:697
  373.8 29.6 %collective-permute-start.41 = (bf16[2304,128]{1,0:T(8,128)(2,1)S(1)}, bf16[2304,128]{1,0:T(8,128)(2,1)S(1)}, u32[]{:S(2)}, u32[]{:S(2)}) collective-permute-start(bf16[2304,128]{1,0:T(8,128)(2,1)S(1)} %copy-done.42), channel_id=1, source_target_pairs={{0,2},{2,0},{4,6},{6,4},{8,10},{10,8},{12,14},{14,12},{16,18},{18,... | collective-permute-start | bytes 1769480 | tf_op jit(solution)/shard_map/ppermute | solution.py:697
  375.0 28.3 %collective-permute-start.42 = (bf16[2304,128]{1,0:T(8,128)(2,1)S(1)}, bf16[2304,128]{1,0:T(8,128)(2,1)S(1)}, u32[]{:S(2)}, u32[]{:S(2)}) collective-permute-start(bf16[2304,128]{1,0:T(8,128)(2,1)S(1)} %add_convert_fusion.10), channel_id=1, source_target_pairs={{0,4},{2,6},{4,0},{6,2},{8,12},{10,14},{12,8},{14,10},{16,20},{18,... | collective-permute-start | bytes 1769480 | tf_op jit(solution)/shard_map/ppermute | solution.py:697
  405.3 31.5 %collective-permute-start.45 = (bf16[1536,128]{1,0:T(8,128)(2,1)}, bf16[1536,128]{1,0:T(8,128)(2,1)}, u32[]{:S(2)}, u32[]{:S(2)}) collective-permute-start(bf16[1536,128]{1,0:T(8,128)(2,1)} %pad_maximum_fusion.13), channel_id=1, source_target_pairs={{0,4},{2,6},{4,0},{6,2},{8,12},{10,14},{12,8},{14,10},{16,20},{18,... | collective-permute-start | bytes 1179656 | tf_op jit(solution)/shard_map/ppermute | solution.py:697
  406.7 30.1 %collective-permute-start.46 = (bf16[1536,128]{1,0:T(8,128)(2,1)}, bf16[1536,128]{1,0:T(8,128)(2,1)}, u32[]{:S(2)}, u32[]{:S(2)}) collective-permute-start(bf16[1536,128]{1,0:T(8,128)(2,1)} %pad_maximum_fusion.14), channel_id=1, source_target_pairs={{0,2},{2,0},{4,6},{6,4},{8,10},{10,8},{12,14},{14,12},{16,18},{18,... | collective-permute-start | bytes 1179656 | tf_op jit(solution)/shard_map/ppermute | solution.py:697
  408.9 27.9 %collective-permute-start.47 = (bf16[1152,128]{1,0:T(8,128)(2,1)}, bf16[1152,128]{1,0:T(8,128)(2,1)}, u32[]{:S(2)}, u32[]{:S(2)}) collective-permute-start(bf16[1152,128]{1,0:T(8,128)(2,1)} %constant_dynamic-slice_fusion.5), channel_id=1, source_target_pairs={{0,4},{2,6},{4,0},{6,2},{8,12},{10,14},{12,8},{14,10},{16,20},{18,... | collective-permute-start | bytes 884744 | tf_op jit(solution)/shard_map/ppermute | solution.py:697
  412.1 24.7 %collective-permute-start.48 = (bf16[1152,128]{1,0:T(8,128)(2,1)}, bf16[1152,128]{1,0:T(8,128)(2,1)}, u32[]{:S(2)}, u32[]{:S(2)}) collective-permute-start(bf16[1152,128]{1,0:T(8,128)(2,1)} %constant_dynamic-slice_fusion.4), channel_id=1, source_target_pairs={{0,2},{2,0},{4,6},{6,4},{8,10},{10,8},{12,14},{14,12},{16,18},{18,... | collective-permute-start | bytes 884744 | tf_op jit(solution)/shard_map/ppermute | solution.py:697
  439.6 23.8 %collective-permute-start.51 = (bf16[3072,128]{1,0:T(8,128)(2,1)S(1)}, bf16[3072,128]{1,0:T(8,128)(2,1)S(1)}, u32[]{:S(2)}, u32[]{:S(2)}) collective-permute-start(bf16[3072,128]{1,0:T(8,128)(2,1)S(1)} %pad_maximum_fusion.5), channel_id=1, source_target_pairs={{0,2},{2,0},{4,6},{6,4},{8,10},{10,8},{12,14},{14,12},{16,18},{18,... | collective-permute-start | bytes 2359304 | tf_op jit(solution)/shard_map/ppermute | solution.py:697
  477.1 24.6 %collective-permute-start.62 = (f32[156,128]{1,0:T(8,128)}, f32[156,128]{1,0:T(8,128)}, u32[]{:S(2)}, u32[]{:S(2)}) collective-permute-start(f32[156,128]{1,0:T(8,128)} %add.403), channel_id=1, source_target_pairs={{0,16},{2,18},{4,20},{6,22},{8,24},{10,26},{12,28},{14,30},{16,0},... | collective-permute-start | bytes 239624 | tf_op jit(solution)/shard_map/ppermute | solution.py:697
  (132 other events, 1241.6 us)
